TPU v7x, 32 devices: a whole 2x2x4 slice. The times are simulated.
32 devices in a mesh: orbits: 2 (over x), sector: 8 (over z, y), spec: 2 (over core).
Axes of the slice: x: 2, y: 2, z: 4, core: 2. Of those that a mesh axis runs over, the one named last changes fastest.
Arguments:
- absorption: bfloat16 [16, 64, 8192], P(('orbits', 'sector'), None, 'spec'), parts along dimension 0, may hold values from 0.025 to 4
- absorber: float32 [16, 64], P(('orbits', 'sector')), parts along dimension 0, may hold values from 0.3 to 3
- seg_level: int32 [16, 3, 128, 32], P(('orbits', 'sector')), parts along dimension 0, may hold values from 0 to 63
- seg_count: int32 [16, 3, 128], P(('orbits', 'sector')), parts along dimension 0, may hold values from 1 to 32
- seg_length: float32 [16, 3, 128, 32], P(('orbits', 'sector')), parts along dimension 0, may hold values from 0.01 to 0.1
- measured: float32 [16, 128, 8192], P(('orbits', 'sector'), None, 'spec'), parts along dimension 0, may hold values from 0 to 1
- window_mask: int32 [8192], P('spec'), may hold values 0 or 1
- prior_weight: float32 [64], replicated, may hold values from 0.05 to 0.5
Outputs:
- spectrum: float32 [16, 128, 8192], P(('orbits', 'sector'), None, 'spec'), parts along dimension 0
- state_step: float32 [16, 64], P(('orbits', 'sector')), parts along dimension 0
There are 2 independent parts, one for each index of `orbits`. A program takes and returns all parts, laid end to end along the dimension named above; an argument that names none is the same for every part. Nothing has to cross between parts.
Inputs may be any that keep to these rules, and one draw needn't show every extreme that they name: Segments j >= seg_count of a ray in a sector are ignored.
All inputs are finite; a program needn't handle non-finite values. No bound on the sum of `window_mask` on one device may be relied on, other than what follows from the above.
Results may differ from a plain program's by a relative error of at most 0.0028.
Values may be sent and summed in bfloat16 or wider, within the bound.
No kernel may reach another device: no remote copies, remote signals or barrier semaphores. Data moves between devices by JAX's collectives and lax.ppermute only.
A program may use at most 64 MiB of HBM per device.

v0:
```python
import functools

import jax
import jax.numpy as jnp
from jax import lax
from jax.experimental import pallas as pl
from jax.experimental.pallas import tpu as pltpu
from jax.sharding import PartitionSpec as P

LANES = 128
ROWS = 16
PIECE = 512
BLOCK = 512
WIDTHS = (3, 3, 2)
VMEM_BYTES = 56 << 20
CHEAP = pl.CostEstimate(flops=1, transcendentals=0, bytes_accessed=1)


def passed_along(block, axis, distance):
    devices = range(lax.axis_size(axis))
    route = [((i - distance) % len(devices), i) for i in devices]
    return lax.ppermute(block, axis, route)


def iota(shape, dim):
    return lax.broadcasted_iota(jnp.int32, shape, dim)


def nt_dot(a, b):
    return lax.dot_general(a, b, (((1,), (1,)), ((), ())), preferred_element_type=jnp.float32)


def prepare_kernel(level_ref, count_ref, length_ref, absorber_ref, mask_ref, *outs):
    cols_refs = outs[:3]
    place_ref, base_ref = outs[3:]
    levels = absorber_ref.shape[1]
    sets, segs, rays = level_ref.shape
    eye = iota((levels, levels), 0) == iota((levels, levels), 1)
    amount = jnp.sum(jnp.where(eye, absorber_ref[...], 0.0), axis=1, keepdims=True)
    level_of = iota((levels, rays), 0)
    for k in range(sets):
        length = jnp.where(iota((segs, rays), 0) < count_ref[k], length_ref[k], 0.0)
        level = level_ref[k]
        path = jnp.zeros((levels, rays), jnp.float32)
        for j in range(segs):
            path += jnp.where(level[j : j + 1, :] == level_of, length[j : j + 1, :], 0.0)
        cols_refs[k][...] = (path * amount).astype(jnp.bfloat16)
    groups = mask_ref.shape[0]
    mask = mask_ref[...].astype(jnp.bfloat16)
    before = (iota((LANES, LANES), 0) < iota((LANES, LANES), 1)).astype(jnp.bfloat16)
    rank = jnp.dot(mask, before, preferred_element_type=jnp.float32)
    total = jnp.dot(mask, jnp.ones((LANES, LANES), jnp.bfloat16), preferred_element_type=jnp.float32)
    earlier = (iota((groups, groups), 1) < iota((groups, groups), 0)).astype(jnp.bfloat16)
    base = jnp.dot(earlier, total.astype(jnp.bfloat16), preferred_element_type=jnp.float32)
    place_ref[...] = jnp.where(mask_ref[...] > 0, (base + rank).astype(jnp.int32), -1)
    base_ref[pl.ds(0, groups), :] = base.astype(jnp.int32)
    last = base[groups - 1 : groups, :] + total[groups - 1 : groups, :]
    base_ref[pl.ds(groups, 8), :] = jnp.broadcast_to(last, (8, LANES)).astype(jnp.int32)


def prepare(level, count, length, absorber, mask):
    rays = level.shape[2]
    levels = absorber.shape[1]
    groups = mask.shape[0]
    cols = jax.ShapeDtypeStruct((levels, rays), jnp.bfloat16)
    return pl.pallas_call(
        prepare_kernel,
        out_shape=(
            cols,
            cols,
            cols,
            jax.ShapeDtypeStruct((groups, LANES), jnp.int32),
            jax.ShapeDtypeStruct((groups + 8, LANES), jnp.int32),
        ),
        cost_estimate=CHEAP,
        name="prepare",
    )(level, count, length, absorber, mask)


def pair_rows(levels):
    spans = []
    offset = 0
    for m in range(levels):
        first = ROWS * (m // ROWS)
        spans.append((m, first, offset, levels - first))
        offset += levels - first
    return spans, offset


def chunk_kernel(*refs, first, width, follows):
    base_ref, before_ref, here_ref, after_ref, place_ref, measured_ref = refs[:6]
    cols_refs = refs[6:9]
    refs = refs[9:]
    if follows:
        earlier_refs = refs[:3]
        refs = refs[4:]
    spectrum_ref = refs[0]
    terms_refs = refs[1:4]
    table, observed, modelled, packed, pairs, weights, moment, in_sems, out_sems = refs[4:]
    levels = here_ref.shape[0]
    rays = measured_ref.shape[0]
    high = 3 * levels
    pieces = width // PIECE
    spans, pair_count = pair_rows(levels)

    def incoming(piece):
        local = pl.ds(piece * PIECE, PIECE)
        overall = pl.ds(first + piece * PIECE, PIECE)
        sources = (
            (before_ref.at[:, local], table.at[pl.ds(0, levels), local]),
            (here_ref.at[:, overall], table.at[pl.ds(levels, levels), local]),
            (after_ref.at[:, local], table.at[pl.ds(2 * levels, levels), local]),
            (measured_ref.at[:, overall], observed.at[:, local]),
        )
        return [pltpu.make_async_copy(a, b, in_sems.at[piece, n]) for n, (a, b) in enumerate(sources)]

    def outgoing(piece):
        return pltpu.make_async_copy(
            modelled.at[:, pl.ds(piece * PIECE, PIECE)],
            spectrum_ref.at[:, pl.ds(first + piece * PIECE, PIECE)],
            out_sems.at[piece],
        )

    for piece in range(pieces):
        for copy in incoming(piece):
            copy.start()

    cols = [ref[...].astype(jnp.float32) for ref in cols_refs]
    rows = jnp.concatenate([c.T for c in cols], axis=1).astype(jnp.bfloat16)
    moment[...] = jnp.zeros_like(moment)
    packed[...] = jnp.zeros_like(packed)
    start = base_ref[first // LANES, 0]
    projected = jnp.zeros((high, rays), jnp.float32)

    for piece in range(pieces):
        for copy in incoming(piece):
            copy.wait()
        lane = slice(piece * PIECE, (piece + 1) * PIECE)
        depth = jnp.dot(rows, table[:high, lane], preferred_element_type=jnp.float32)
        spectrum = jnp.exp(-depth)
        modelled[:, lane] = spectrum
        outgoing(piece).start()
        table[high:, lane] = (spectrum * spectrum).astype(jnp.bfloat16)
        groups = range(piece * PIECE // LANES, (piece + 1) * PIECE // LANES)
        places = [place_ref[first // LANES + g : first // LANES + g + 1, :] for g in groups]
        kept = jnp.concatenate(places, axis=1) >= 0
        error = jnp.where(kept, (observed[:, lane] - spectrum) * spectrum, 0.0).astype(jnp.bfloat16)
        projected += nt_dot(table[:high, lane], error)
        for g, place in zip(groups, places, strict=True):
            at = (base_ref[first // LANES + g, 0] - start) // LANES
            chosen = (iota((2 * LANES, LANES), 0) + (at * LANES + start) == place).astype(jnp.bfloat16)
            moved = nt_dot(table[:, g * LANES : (g + 1) * LANES], chosen).astype(jnp.bfloat16)
            packed[at] = packed[at] + moved[:, :LANES]
            packed[at + 1] = moved[:, LANES:]

    def one_block(block, parts):
        wide = parts * LANES
        for p in range(parts):
            lane = slice(p * LANES, (p + 1) * LANES)
            weights[:, lane] = packed[block + p, high:, :]
            for k in range(3):
                level_rows = packed[block + p, k * levels : (k + 1) * levels, :]
                for m, low, offset, count in spans:
                    pairs[k, offset : offset + count, lane] = level_rows[low:, :] * level_rows[m : m + 1, :]
        for k in range(3):
            moment[k] += nt_dot(pairs[k, :, :wide], weights[:, :wide])

    count = base_ref[(first + width) // LANES, 0] - start
    ready = count // BLOCK
    parts = BLOCK // LANES
    lax.fori_loop(0, ready, lambda block, carry: (one_block(block * parts, parts), carry)[1], 0)
    left = count - ready * BLOCK

    @pl.when(left > BLOCK // 2)
    def _():
        one_block(ready * parts, parts)

    @pl.when((left > 0) & (left <= BLOCK // 2))
    def _():
        one_block(ready * parts, parts // 2)

    lane = iota((levels, LANES), 1)
    for k in range(3):
        gradient = jnp.sum(cols[k] * projected[k * levels : (k + 1) * levels, :], axis=1, keepdims=True)
        result = jnp.where(lane == levels, gradient, 0.0)
        for m, low, offset, count in spans:
            column = jnp.sum(
                moment[k, offset : offset + count, :] * (cols[k][low:, :] * cols[k][m : m + 1, :]), axis=1, keepdims=True
            )
            if low:
                column = jnp.concatenate([jnp.zeros((low, 1), jnp.float32), column], axis=0)
            result = jnp.where(lane == m, column, result)
        if follows:
            result = result + earlier_refs[k][...]
        terms_refs[k][...] = result
    for piece in range(pieces):
        outgoing(piece).wait()


def chunk(base, before, here, after, place, measured, cols, earlier, spectrum, first, width):
    levels = here.shape[0]
    rays = measured.shape[0]
    pieces = width // PIECE
    _, pair_count = pair_rows(levels)
    follows = earlier is not None
    smem = pl.BlockSpec(memory_space=pltpu.SMEM)
    vmem = pl.BlockSpec(memory_space=pltpu.VMEM)
    left = pl.BlockSpec(memory_space=pl.ANY)
    terms = jax.ShapeDtypeStruct((levels, LANES), jnp.float32)
    args = [base, before, here, after, place, measured, *cols]
    specs = [smem, left, left, left, vmem, left, vmem, vmem, vmem]
    if follows:
        args += [*earlier, spectrum]
        specs += [vmem, vmem, vmem, left]
    outs = pl.pallas_call(
        functools.partial(chunk_kernel, first=first, width=width, follows=follows),
        in_specs=specs,
        out_specs=[left, vmem, vmem, vmem],
        out_shape=(jax.ShapeDtypeStruct(measured.shape, jnp.float32), terms, terms, terms),
        scratch_shapes=[
            pltpu.VMEM((3 * levels + rays, width), jnp.bfloat16),
            pltpu.VMEM((rays, width), jnp.float32),
            pltpu.VMEM((rays, width), jnp.float32),
            pltpu.VMEM(((width + BLOCK) // LANES + 2, 3 * levels + rays, LANES), jnp.bfloat16),
            pltpu.VMEM((3, pair_count, BLOCK), jnp.bfloat16),
            pltpu.VMEM((rays, BLOCK), jnp.bfloat16),
            pltpu.VMEM((3, pair_count, rays), jnp.float32),
            pltpu.SemaphoreType.DMA((pieces, 4)),
            pltpu.SemaphoreType.DMA((pieces,)),
        ],
        input_output_aliases={12: 0} if follows else {},
        compiler_params=pltpu.CompilerParams(vmem_limit_bytes=VMEM_BYTES),
        cost_estimate=CHEAP,
        name="chunk",
    )(*args)
    return outs[0], outs[1:]


def solve_kernel(*refs, scale):
    parts = refs[:6]
    prior_ref, out_ref = refs[6:]
    levels = prior_ref.shape[1]
    total = parts[0][...]
    for part in parts[1:]:
        total = total + part[...]
    terms = total * scale
    row = iota((levels, LANES), 0)
    lane = iota((levels, LANES), 1)
    square = terms[:, :levels]
    flipped = jnp.concatenate([square.T, jnp.zeros((levels, LANES - levels), jnp.float32)], axis=1)
    lower = row // ROWS >= lane // ROWS
    work = jnp.where(lower | (lane >= levels), terms, flipped)
    diagonal = jnp.sum(jnp.where(row == lane, work, 0.0), axis=1, keepdims=True)
    mean = jnp.sum(diagonal, axis=0, keepdims=True) * (1.0 / levels) + 1e-06
    eye = iota((levels, levels), 0) == iota((levels, levels), 1)
    prior = jnp.sum(jnp.where(eye, prior_ref[...], 0.0), axis=1, keepdims=True)
    work = work + jnp.where(row == lane, prior * mean, 0.0)
    for i in range(levels):
        pivot_row = work[i : i + 1, :]
        scaled = pivot_row * (1.0 / pivot_row[:, i : i + 1])
        column = work[:, i : i + 1]
        factor = jnp.where(row[:, :1] == i, column - 1.0, column)
        work = work - factor * scaled
    column = work[:, levels : levels + 1]
    out_ref[...] = -jnp.sum(jnp.where(eye, column, 0.0), axis=0, keepdims=True)


def solve(parts, prior_weight, scale):
    return pl.pallas_call(
        functools.partial(solve_kernel, scale=scale),
        out_shape=jax.ShapeDtypeStruct((1, prior_weight.shape[1]), jnp.float32),
        cost_estimate=CHEAP,
        name="solve",
    )(*parts, prior_weight)


def swapped(block, axis):
    size = lax.axis_size(axis)
    return lax.ppermute(block, axis, [(i, size - 1 - i) for i in range(size)])


def shards(absorption, absorber, seg_level, seg_count, seg_length, measured, window_mask, prior_weight):
    table = absorption[0]
    levels, points = table.shape
    rays = measured.shape[1]
    widths = [w * points // sum(WIDTHS) for w in WIDTHS]
    firsts = [sum(widths[:c]) for c in range(len(widths))]
    below = []
    above = []
    for first, width in zip(firsts, widths, strict=True):
        piece = table[:, first : first + width]
        below.append(passed_along(piece, "sector", 1))
        above.append(passed_along(piece, "sector", -1))
    mask = window_mask.reshape(points // LANES, LANES)
    level = jnp.swapaxes(seg_level[0], 1, 2)
    length = jnp.swapaxes(seg_length[0], 1, 2)
    count = seg_count.reshape(3, 1, rays)
    cols_low, cols_here, cols_high, place, base = prepare(level, count, length, absorber, mask)
    base = base[:, :1]
    cols = (passed_along(cols_high, "sector", 1), cols_here, passed_along(cols_low, "sector", -1))
    terms = spectrum = None
    for c, (first, width) in enumerate(zip(firsts, widths, strict=True)):
        spectrum, terms = chunk(base, below[c], table, above[c], place, measured[0], cols, terms, spectrum, first, width)
    mine = (terms[1], passed_along(terms[0], "sector", -1), passed_along(terms[2], "sector", 1))
    others = tuple(swapped(part, "spec") for part in mine)
    scale = 1.0 / (rays * points * lax.axis_size("spec"))
    state_step = solve(mine + others, prior_weight[None, :], scale)
    return (spectrum[None], state_step)


def solution(mesh):
    return jax.shard_map(
        shards,
        mesh=mesh,
        in_specs=(
            P(("orbits", "sector"), None, "spec"),
            P(("orbits", "sector"), None),
            P(("orbits", "sector"), None, None, None),
            P(("orbits", "sector"), None, None),
            P(("orbits", "sector"), None, None, None),
            P(("orbits", "sector"), None, "spec"),
            P("spec"),
            P(),
        ),
        out_specs=(P(("orbits", "sector"), None, "spec"), P(("orbits", "sector"), None)),
        check_vma=False,
    )
```

profile of v0, /device:TPU:0, one launch (start us, length us, event | category | flops | bytes accessed | tf_op | source)
XLA Modules:
  0.0 83.2 jit_solution(10275191449126754043)
XLA Ops:
  0.6 1.1 %fusion = (bf16[64,1536]{1,0:T(8,128)(2,1)S(1)}, bf16[64,1536]{1,0:T(8,128)(2,1)S(1)}) fusion(bf16[64,4096]{1,0:T(8,128)(2,1)} %bitcast.16), kind=kLoop, calls=%fused_computation | loop fusion | bytes 786432 | tf_op jit(solution)/shard_map/slice | solution.py:291
  1.7 3.0 %collective-permute-start.6 = (bf16[64,1536]{1,0:T(8,128)(2,1)S(1)}, bf16[64,1536]{1,0:T(8,128)(2,1)S(1)}, u32[]{:S(2)}, u32[]{:S(2)}) collective-permute-start(bf16[64,1536]{1,0:T(8,128)(2,1)S(1)} %get-tuple-element.36), channel_id=1, source_target_pairs={{14,0},{0,2},{2,4},{4,6},{6,8},{8,10},{10,12},{12,14},{15,1},{1,3}... | collective-permute-start | bytes 589832 | tf_op jit(solution)/shard_map/ppermute | solution.py:22
  4.7 3.1 %collective-permute-start.7 = (bf16[64,1536]{1,0:T(8,128)(2,1)S(1)}, bf16[64,1536]{1,0:T(8,128)(2,1)S(1)}, u32[]{:S(2)}, u32[]{:S(2)}) collective-permute-start(bf16[64,1536]{1,0:T(8,128)(2,1)S(1)} %get-tuple-element.36), channel_id=1, source_target_pairs={{2,0},{4,2},{6,4},{8,6},{10,8},{12,10},{14,12},{0,14},{3,1},{5,3},... | collective-permute-start | bytes 589832 | tf_op jit(solution)/shard_map/ppermute | solution.py:22
  7.8 4.7 %collective-permute-start.5 = (bf16[64,1536]{1,0:T(8,128)(2,1)S(1)}, bf16[64,1536]{1,0:T(8,128)(2,1)S(1)}, u32[]{:S(2)}, u32[]{:S(2)}) collective-permute-start(bf16[64,1536]{1,0:T(8,128)(2,1)S(1)} %get-tuple-element.37), channel_id=1, source_target_pairs={{2,0},{4,2},{6,4},{8,6},{10,8},{12,10},{14,12},{0,14},{3,1},{5,3},... | collective-permute-start | bytes 589832 | tf_op jit(solution)/shard_map/ppermute | solution.py:22
  12.5 1.9 %prepare.1 = (bf16[64,128]{1,0:T(8,128)(2,1)}, bf16[64,128]{1,0:T(8,128)(2,1)}, bf16[64,128]{1,0:T(8,128)(2,1)}, s32[32,128]{1,0:T(8,128)}, s32[40,128]{1,0:T(8,128)}) custom-call(s32[3,32,128]{2,1,0:T(8,128)} %bitcast.25, s32[3,1,128]{2,1,0:T(1,128)} %bitcast.28, f32[3,32,128]{2,1,0:T(8,128)} %bitcast.26, f32[1,64]{1,0:T(1,128)} %absorber_ref.1, ...), custom_call_target="tpu_custom_call" | custom-call | flops 1 | bytes 1 | tf_op jit(solution)/shard_map/prepare/pallas_call | solution.py:66
  14.5 7.4 %collective-permute-done.2.refs_6_ = bf16[64,128]{1,0:T(8,128)(2,1)S(1)} collective-permute-done((bf16[64,128]{1,0:T(8,128)(2,1)}, bf16[64,128]{1,0:T(8,128)(2,1)S(1)}, u32[]{:S(2)}, u32[]{:S(2)}) %collective-permute-start.2) | collective-permute-done | bytes 16416 | tf_op jit(solution)/shard_map/ppermute | solution.py:22
  21.9 5.5 %collective-permute-start.3 = (bf16[64,128]{1,0:T(8,128)(2,1)}, bf16[64,128]{1,0:T(8,128)(2,1)S(1)}, u32[]{:S(2)}, u32[]{:S(2)}) collective-permute-start(bf16[64,128]{1,0:T(8,128)(2,1)} %get-tuple-element.23), channel_id=1, source_target_pairs={{2,0},{4,2},{6,4},{8,6},{10,8},{12,10},{14,12},{0,14},{3,1},{5,3},... | collective-permute-start | bytes 49160 | tf_op jit(solution)/shard_map/ppermute | solution.py:22
  27.4 0.9 %slice.16 = bf16[64,1024]{1,0:T(8,128)(2,1)S(1)} slice(bf16[64,4096]{1,0:T(8,128)(2,1)} %bitcast.17), slice={[0:64], [3072:4096]} | slice | bytes 262144 | tf_op jit(solution)/shard_map/slice | solution.py:291
  28.3 0.7 collective-permute-done.3.refs_8_
  29.0 0.2 collective-permute-start
  29.2 4.9 %collective-permute-start.1 = (bf16[64,1024]{1,0:T(8,128)(2,1)S(1)}, bf16[64,1024]{1,0:T(8,128)(2,1)S(1)}, u32[]{:S(2)}, u32[]{:S(2)}) collective-permute-start(bf16[64,1024]{1,0:T(8,128)(2,1)S(1)} %slice.16), channel_id=1, source_target_pairs={{2,0},{4,2},{6,4},{8,6},{10,8},{12,10},{14,12},{0,14},{3,1},{5,3},... | collective-permute-start | bytes 393224 | tf_op jit(solution)/shard_map/ppermute | solution.py:22
  34.1 0.7 copy-done.3
  34.8 10.0 %chunk.3 = (f32[128,4096]{1,0:T(8,128)}, f32[64,128]{1,0:T(8,128)}, f32[64,128]{1,0:T(8,128)}, f32[64,128]{1,0:T(8,128)}) custom-call(s32[40,1]{1,0:T(8,128)} %bitcast.22, bf16[64,1536]{1,0:T(8,128)(2,1)} %copy-done.2, bf16[64,4096]{1,0:T(8,128)(2,1)} %bitcast.18, bf16[64,1536]{1,0:T(8,128)(2,1)} %copy-done.3, s32[32,128]{1,0:T(8,128)} %get-tuple-element.20.refs_4_, ...), custom_call_target="tpu_custom_call" | custom-call | flops 1 | bytes 1 | tf_op jit(solution)/shard_map/chunk/pallas_call | solution.py:215
  44.8 0.7 copy-done
  45.5 0.1 copy-done.1
  45.5 10.0 %chunk.4 = (f32[128,4096]{1,0:T(8,128)}, f32[64,128]{1,0:T(8,128)}, f32[64,128]{1,0:T(8,128)}, f32[64,128]{1,0:T(8,128)}) custom-call(s32[40,1]{1,0:T(8,128)} %bitcast.23, bf16[64,1536]{1,0:T(8,128)(2,1)} %copy-done, bf16[64,4096]{1,0:T(8,128)(2,1)} %bitcast.19, bf16[64,1536]{1,0:T(8,128)(2,1)} %copy-done.1, ...), custom_call_target="tpu_custom_call", output_to_operand_aliasing={{0}: (12, {})} | custom-call | flops 1 | bytes 1 | tf_op jit(solution)/shard_map/chunk/pallas_call | solution.py:215
  55.6 0.6 copy-done.6
  56.3 9.2 %chunk.5 = (f32[128,4096]{1,0:T(8,128)}, f32[64,128]{1,0:T(8,128)}, f32[64,128]{1,0:T(8,128)}, f32[64,128]{1,0:T(8,128)}) custom-call(s32[40,1]{1,0:T(8,128)} %bitcast.24, bf16[64,1024]{1,0:T(8,128)(2,1)} %copy-done.6, bf16[64,4096]{1,0:T(8,128)(2,1)} %bitcast.20, bf16[64,1024]{1,0:T(8,128)(2,1)} %copy-done.7, ...), custom_call_target="tpu_custom_call", output_to_operand_aliasing={{0}: (12, {})} | custom-call | flops 1 | bytes 1 | tf_op jit(solution)/shard_map/chunk/pallas_call | solution.py:215
  65.5 2.0 %collective-permute-start.8 = (f32[64,128]{1,0:T(8,128)}, f32[64,128]{1,0:T(8,128)S(1)}, u32[]{:S(2)}, u32[]{:S(2)}) collective-permute-start(f32[64,128]{1,0:T(8,128)} %get-tuple-element.34), channel_id=1, source_target_pairs={{2,0},{4,2},{6,4},{8,6},{10,8},{12,10},{14,12},{0,14},{3,1},{5,3},... | collective-permute-start | bytes 98312 | tf_op jit(solution)/shard_map/ppermute | solution.py:22
  67.6 2.1 %collective-permute-done.8.refs_1_ = f32[64,128]{1,0:T(8,128)S(1)} collective-permute-done((f32[64,128]{1,0:T(8,128)}, f32[64,128]{1,0:T(8,128)S(1)}, u32[]{:S(2)}, u32[]{:S(2)}) %collective-permute-start.8) | collective-permute-done | bytes 32800 | tf_op jit(solution)/shard_map/ppermute | solution.py:22
  69.7 4.7 %collective-permute-done.9.refs_2_ = f32[64,128]{1,0:T(8,128)S(1)} collective-permute-done((f32[64,128]{1,0:T(8,128)}, f32[64,128]{1,0:T(8,128)S(1)}, u32[]{:S(2)}, u32[]{:S(2)}) %collective-permute-start.9) | collective-permute-done | bytes 32800 | tf_op jit(solution)/shard_map/ppermute | solution.py:22
  74.4 1.2 %collective-permute-done.12.refs_5_ = f32[64,128]{1,0:T(8,128)S(1)} collective-permute-done((f32[64,128]{1,0:T(8,128)S(1)}, f32[64,128]{1,0:T(8,128)S(1)}, u32[]{:S(2)}, u32[]{:S(2)}) %collective-permute-start.12) | collective-permute-done | bytes 32800 | tf_op jit(solution)/shard_map/ppermute | solution.py:279
  75.6 0.6 copy-done.12
  76.2 7.0 %solve.1 = f32[1,64]{1,0:T(1,128)} custom-call(f32[64,128]{1,0:T(8,128)} %get-tuple-element.33.refs_0_, f32[64,128]{1,0:T(8,128)} %copy-done.8, f32[64,128]{1,0:T(8,128)} %copy-done.9, f32[64,128]{1,0:T(8,128)} %copy-done.10, f32[64,128]{1,0:T(8,128)} %copy-done.11, f32[64,128]{1,0:T(8,128)} %copy-done.12, f32[1,64]{1,0:T(1,128)} %bitcast.29), custom_call_target="tpu_custom_call" | custom-call | flops 1 | bytes 1 | tf_op jit(solution)/shard_map/solve/pallas_call | solution.py:269
  (35 shorter events, 0.2 us)
Async XLA Ops:
  1.7 27.5 %collective-permute-start.6 = (bf16[64,1536]{1,0:T(8,128)(2,1)S(1)}, bf16[64,1536]{1,0:T(8,128)(2,1)S(1)}, u32[]{:S(2)}, u32[]{:S(2)}) collective-permute-start(bf16[64,1536]{1,0:T(8,128)(2,1)S(1)} %get-tuple-element.36), channel_id=1, source_target_pairs={{14,0},{0,2},{2,4},{4,6},{6,8},{8,10},{10,12},{12,14},{15,1},{1,3}... | collective-permute-start | bytes 589832 | tf_op jit(solution)/shard_map/ppermute | solution.py:22
  4.7 29.4 %collective-permute-start.7 = (bf16[64,1536]{1,0:T(8,128)(2,1)S(1)}, bf16[64,1536]{1,0:T(8,128)(2,1)S(1)}, u32[]{:S(2)}, u32[]{:S(2)}) collective-permute-start(bf16[64,1536]{1,0:T(8,128)(2,1)S(1)} %get-tuple-element.36), channel_id=1, source_target_pairs={{2,0},{4,2},{6,4},{8,6},{10,8},{12,10},{14,12},{0,14},{3,1},{5,3},... | collective-permute-start | bytes 589832 | tf_op jit(solution)/shard_map/ppermute | solution.py:22
  7.8 37.0 %collective-permute-start.4 = (bf16[64,1536]{1,0:T(8,128)(2,1)S(1)}, bf16[64,1536]{1,0:T(8,128)(2,1)S(1)}, u32[]{:S(2)}, u32[]{:S(2)}) collective-permute-start(bf16[64,1536]{1,0:T(8,128)(2,1)S(1)} %get-tuple-element.37), channel_id=1, source_target_pairs={{14,0},{0,2},{2,4},{4,6},{6,8},{8,10},{10,12},{12,14},{15,1},{1,3}... | collective-permute-start | bytes 589832 | tf_op jit(solution)/shard_map/ppermute | solution.py:22
  7.8 37.0 %collective-permute-start.5 = (bf16[64,1536]{1,0:T(8,128)(2,1)S(1)}, bf16[64,1536]{1,0:T(8,128)(2,1)S(1)}, u32[]{:S(2)}, u32[]{:S(2)}) collective-permute-start(bf16[64,1536]{1,0:T(8,128)(2,1)S(1)} %get-tuple-element.37), channel_id=1, source_target_pairs={{2,0},{4,2},{6,4},{8,6},{10,8},{12,10},{14,12},{0,14},{3,1},{5,3},... | collective-permute-start | bytes 589832 | tf_op jit(solution)/shard_map/ppermute | solution.py:22
  14.5 7.4 %collective-permute-start.2 = (bf16[64,128]{1,0:T(8,128)(2,1)}, bf16[64,128]{1,0:T(8,128)(2,1)S(1)}, u32[]{:S(2)}, u32[]{:S(2)}) collective-permute-start(bf16[64,128]{1,0:T(8,128)(2,1)} %get-tuple-element.21), channel_id=1, source_target_pairs={{14,0},{0,2},{2,4},{4,6},{6,8},{8,10},{10,12},{12,14},{15,1},{1,3}... | collective-permute-start | bytes 49160 | tf_op jit(solution)/shard_map/ppermute | solution.py:22
  21.9 12.2 %copy-start.4 = (bf16[64,128]{1,0:T(8,128)(2,1)}, bf16[64,128]{1,0:T(8,128)(2,1)S(1)}, u32[]{:S(2)}) copy-start(bf16[64,128]{1,0:T(8,128)(2,1)S(1)} %collective-permute-done.2.refs_6_) | copy-start | bytes 49156
  21.9 7.2 %collective-permute-start.3 = (bf16[64,128]{1,0:T(8,128)(2,1)}, bf16[64,128]{1,0:T(8,128)(2,1)S(1)}, u32[]{:S(2)}, u32[]{:S(2)}) collective-permute-start(bf16[64,128]{1,0:T(8,128)(2,1)} %get-tuple-element.23), channel_id=1, source_target_pairs={{2,0},{4,2},{6,4},{8,6},{10,8},{12,10},{14,12},{0,14},{3,1},{5,3},... | collective-permute-start | bytes 49160 | tf_op jit(solution)/shard_map/ppermute | solution.py:22
  29.0 5.1 %copy-start.5 = (bf16[64,128]{1,0:T(8,128)(2,1)}, bf16[64,128]{1,0:T(8,128)(2,1)S(1)}, u32[]{:S(2)}) copy-start(bf16[64,128]{1,0:T(8,128)(2,1)S(1)} %collective-permute-done.3.refs_8_) | copy-start | bytes 49156
  29.0 26.5 %collective-permute-start = (bf16[64,1024]{1,0:T(8,128)(2,1)S(1)}, bf16[64,1024]{1,0:T(8,128)(2,1)S(1)}, u32[]{:S(2)}, u32[]{:S(2)}) collective-permute-start(bf16[64,1024]{1,0:T(8,128)(2,1)S(1)} %slice.16), channel_id=1, source_target_pairs={{14,0},{0,2},{2,4},{4,6},{6,8},{8,10},{10,12},{12,14},{15,1},{1,3}... | collective-permute-start | bytes 393224 | tf_op jit(solution)/shard_map/ppermute | solution.py:22
  29.2 4.9 %copy-start.2 = (bf16[64,1536]{1,0:T(8,128)(2,1)}, bf16[64,1536]{1,0:T(8,128)(2,1)S(1)}, u32[]{:S(2)}) copy-start(bf16[64,1536]{1,0:T(8,128)(2,1)S(1)} %collective-permute-done.6.refs_1_) | copy-start | bytes 589828
  29.2 26.4 %collective-permute-start.1 = (bf16[64,1024]{1,0:T(8,128)(2,1)S(1)}, bf16[64,1024]{1,0:T(8,128)(2,1)S(1)}, u32[]{:S(2)}, u32[]{:S(2)}) collective-permute-start(bf16[64,1024]{1,0:T(8,128)(2,1)S(1)} %slice.16), channel_id=1, source_target_pairs={{2,0},{4,2},{6,4},{8,6},{10,8},{12,10},{14,12},{0,14},{3,1},{5,3},... | collective-permute-start | bytes 393224 | tf_op jit(solution)/shard_map/ppermute | solution.py:22
  34.1 0.7 copy-start.3
  44.8 0.7 copy-start
  44.8 0.7 copy-start.1
  55.6 0.7 copy-start.7
  65.5 4.2 %collective-permute-start.8 = (f32[64,128]{1,0:T(8,128)}, f32[64,128]{1,0:T(8,128)S(1)}, u32[]{:S(2)}, u32[]{:S(2)}) collective-permute-start(f32[64,128]{1,0:T(8,128)} %get-tuple-element.34), channel_id=1, source_target_pairs={{2,0},{4,2},{6,4},{8,6},{10,8},{12,10},{14,12},{0,14},{3,1},{5,3},... | collective-permute-start | bytes 98312 | tf_op jit(solution)/shard_map/ppermute | solution.py:22
  67.5 6.8 %collective-permute-start.9 = (f32[64,128]{1,0:T(8,128)}, f32[64,128]{1,0:T(8,128)S(1)}, u32[]{:S(2)}, u32[]{:S(2)}) collective-permute-start(f32[64,128]{1,0:T(8,128)} %get-tuple-element.35), channel_id=1, source_target_pairs={{14,0},{0,2},{2,4},{4,6},{6,8},{8,10},{10,12},{12,14},{15,1},{1,3}... | collective-permute-start | bytes 98312 | tf_op jit(solution)/shard_map/ppermute | solution.py:22
  67.6 6.8 %collective-permute-start.10 = (f32[64,128]{1,0:T(8,128)}, f32[64,128]{1,0:T(8,128)S(1)}, u32[]{:S(2)}, u32[]{:S(2)}) collective-permute-start(f32[64,128]{1,0:T(8,128)} %get-tuple-element.33.refs_0_), channel_id=1, source_target_pairs={{0,1},{1,0},{2,3},{3,2},{4,5},{5,4},{6,7},{7,6},{8,9},{9,8},{10,11... | collective-permute-start | bytes 98312 | tf_op jit(solution)/shard_map/ppermute | solution.py:279
  69.7 5.9 %copy-start.8 = (f32[64,128]{1,0:T(8,128)}, f32[64,128]{1,0:T(8,128)S(1)}, u32[]{:S(2)}) copy-start(f32[64,128]{1,0:T(8,128)S(1)} %collective-permute-done.8.refs_1_) | copy-start | bytes 98308
  69.7 4.7 %collective-permute-start.11 = (f32[64,128]{1,0:T(8,128)S(1)}, f32[64,128]{1,0:T(8,128)S(1)}, u32[]{:S(2)}, u32[]{:S(2)}) collective-permute-start(f32[64,128]{1,0:T(8,128)S(1)} %collective-permute-done.8.refs_1_), channel_id=1, source_target_pairs={{0,1},{1,0},{2,3},{3,2},{4,5},{5,4},{6,7},{7,6},{8,9},{9,8},{10,11... | collective-permute-start | bytes 98312 | tf_op jit(solution)/shard_map/ppermute | solution.py:279
  74.4 1.2 %copy-start.9 = (f32[64,128]{1,0:T(8,128)}, f32[64,128]{1,0:T(8,128)S(1)}, u32[]{:S(2)}) copy-start(f32[64,128]{1,0:T(8,128)S(1)} %collective-permute-done.9.refs_2_) | copy-start | bytes 98308
  74.4 1.2 %collective-permute-start.12 = (f32[64,128]{1,0:T(8,128)S(1)}, f32[64,128]{1,0:T(8,128)S(1)}, u32[]{:S(2)}, u32[]{:S(2)}) collective-permute-start(f32[64,128]{1,0:T(8,128)S(1)} %collective-permute-done.9.refs_2_), channel_id=1, source_target_pairs={{0,1},{1,0},{2,3},{3,2},{4,5},{5,4},{6,7},{7,6},{8,9},{9,8},{10,11... | collective-permute-start | bytes 98312 | tf_op jit(solution)/shard_map/ppermute | solution.py:279
  74.4 1.2 %copy-start.10 = (f32[64,128]{1,0:T(8,128)}, f32[64,128]{1,0:T(8,128)S(1)}, u32[]{:S(2)}) copy-start(f32[64,128]{1,0:T(8,128)S(1)} %collective-permute-done.10.refs_3_) | copy-start | bytes 98308
  74.4 1.2 %copy-start.11 = (f32[64,128]{1,0:T(8,128)}, f32[64,128]{1,0:T(8,128)S(1)}, u32[]{:S(2)}) copy-start(f32[64,128]{1,0:T(8,128)S(1)} %collective-permute-done.11.refs_4_) | copy-start | bytes 98308
  (2 other events, 1.3 us)
where the time goes:
time: 84.4 us; the launch traced here: 83.2 us
  Pallas kernels  38.2 us (45%)
  starting transfers between devices  23.5 us (28%)
  waiting for transfers between devices  16.1 us (19%)
  local copies, waits for them, and re-layouts  4.65 us (6%)
    pallas_call x3, Pallas kernels, chunk(): pl.pallas_call(functools.partial(chunk_kernel, first=first, width=width,...  29.2 us
    ppermute x10, starting transfers between devices, passed_along(): return lax.ppermute(block, axis, route)  23.5 us
    ppermute x10, waiting for transfers between devices, passed_along(): return lax.ppermute(block, axis, route)  14.9 us
    pallas_call x1, Pallas kernels, solve(): pl.pallas_call(functools.partial(solve_kernel, scale=scale), out_shape=ja...  7.02 us
    unnamed x26, local copies, waits for them, and re-layouts  2.69 us
    slice x2, local copies, waits for them, and re-layouts, shards(): piece = table[:, first:first + width]  1.96 us
    pallas_call x1, Pallas kernels, prepare(): pl.pallas_call(prepare_kernel, out_shape=(cols, cols, cols, jax.ShapeDtyp...  1.94 us
  transfers between devices with their start and end apart: 13, of which 5 were waited for; matrix products, arithmetic and copies ran while one was open for 1% of the time, Pallas kernels for 26%

commit v1 on v0

v1 whole, which is shorter than its diff:
```python
import functools

import jax
import jax.numpy as jnp
from jax import lax
from jax.experimental import pallas as pl
from jax.experimental.pallas import tpu as pltpu
from jax.sharding import PartitionSpec as P

LANES = 128
ROWS = 16
PIECE = 512
BLOCK = 512
WIDTHS = (2, 2, 2, 2)
GROUPS = ((0, 1), (2,), (3,))
CARRIER = 1
SMALL_BYTES = 4 << 20
CHUNK_BYTES = 16 << 20
CHEAP = pl.CostEstimate(flops=1, transcendentals=0, bytes_accessed=1)


def passed_along(block, axis, distance):
    devices = range(lax.axis_size(axis))
    route = [((i - distance) % len(devices), i) for i in devices]
    return lax.ppermute(block, axis, route)


def iota(shape, dim):
    return lax.broadcasted_iota(jnp.int32, shape, dim)


def nt_dot(a, b):
    return lax.dot_general(a, b, (((1,), (1,)), ((), ())), preferred_element_type=jnp.float32)


def prepare_kernel(level_ref, count_ref, length_ref, absorber_ref, mask_ref, table_ref, *outs, first, width):
    up_ref, down_ref, cols_ref, place_ref, base_ref, sems = outs
    levels = absorber_ref.shape[1]
    sets, segs, rays = level_ref.shape
    copies = [
        pltpu.make_async_copy(table_ref.at[:, pl.ds(first, width)], ref.at[:, pl.ds(0, width)], sems.at[n])
        for n, ref in enumerate((up_ref, down_ref))
    ]
    for copy in copies:
        copy.start()
    eye = iota((levels, levels), 0) == iota((levels, levels), 1)
    amount = jnp.sum(jnp.where(eye, absorber_ref[...], 0.0), axis=1, keepdims=True)
    level_of = iota((levels, rays), 0)
    for k in range(sets):
        length = jnp.where(iota((segs, rays), 0) < count_ref[k], length_ref[k], 0.0)
        level = level_ref[k]
        path = jnp.zeros((levels, rays), jnp.float32)
        for j in range(segs):
            path += jnp.where(level[j : j + 1, :] == level_of, length[j : j + 1, :], 0.0)
        absorbed = (path * amount).astype(jnp.bfloat16)
        if k == 0:
            down_ref[:, width:] = absorbed
        elif k == 1:
            cols_ref[...] = absorbed
        else:
            up_ref[:, width:] = absorbed
    groups = mask_ref.shape[0]
    mask = mask_ref[...].astype(jnp.bfloat16)
    before = (iota((LANES, LANES), 0) < iota((LANES, LANES), 1)).astype(jnp.bfloat16)
    rank = jnp.dot(mask, before, preferred_element_type=jnp.float32)
    total = jnp.dot(mask, jnp.ones((LANES, LANES), jnp.bfloat16), preferred_element_type=jnp.float32)
    earlier = (iota((groups, groups), 1) < iota((groups, groups), 0)).astype(jnp.bfloat16)
    base = jnp.dot(earlier, total.astype(jnp.bfloat16), preferred_element_type=jnp.float32)
    place_ref[...] = jnp.where(mask_ref[...] > 0, (base + rank).astype(jnp.int32), -1)
    base_ref[pl.ds(0, groups), :] = base.astype(jnp.int32)
    last = base[groups - 1 : groups, :] + total[groups - 1 : groups, :]
    base_ref[pl.ds(groups, 8), :] = jnp.broadcast_to(last, (8, LANES)).astype(jnp.int32)
    for copy in copies:
        copy.wait()


def prepare(level, count, length, absorber, mask, table, first, width):
    rays = level.shape[2]
    levels = absorber.shape[1]
    groups = mask.shape[0]
    send = jax.ShapeDtypeStruct((levels, width + rays), jnp.bfloat16)
    vmem = pl.BlockSpec(memory_space=pltpu.VMEM)
    return pl.pallas_call(
        functools.partial(prepare_kernel, first=first, width=width),
        in_specs=[vmem] * 5 + [pl.BlockSpec(memory_space=pl.ANY)],
        out_shape=(
            send,
            send,
            jax.ShapeDtypeStruct((levels, rays), jnp.bfloat16),
            jax.ShapeDtypeStruct((groups, LANES), jnp.int32),
            jax.ShapeDtypeStruct((groups + 8, LANES), jnp.int32),
        ),
        scratch_shapes=[pltpu.SemaphoreType.DMA((2,))],
        compiler_params=pltpu.CompilerParams(vmem_limit_bytes=SMALL_BYTES),
        cost_estimate=CHEAP,
        name="prepare",
    )(level, count, length, absorber, mask, table)


def pair_rows(levels):
    spans = []
    offset = 0
    for m in range(levels):
        first = ROWS * (m // ROWS)
        spans.append((m, first, offset, levels - first))
        offset += levels - first
    return spans, offset


def chunk_kernel(*refs, spans_of, carrier, opens, closes):
    base_ref, place_ref, here_ref, measured_ref, cols_ref, carried_before, carried_after = refs[:7]
    refs = refs[7:]
    sources = []
    for _ in spans_of:
        sources.append(refs[:2])
        refs = refs[2:]
    if not opens:
        refs = refs[4:]
    spectrum_ref, packed, moment, projected = refs[:4]
    refs = refs[4:]
    if closes:
        terms_refs = refs[:3]
        refs = refs[3:]
    table, modelled, pairs, weights, sems = refs
    levels = here_ref.shape[0]
    rays = measured_ref.shape[0]
    high = 3 * levels
    begin = spans_of[0][0]
    end = spans_of[-1][0] + spans_of[-1][1]
    spans, pair_count = pair_rows(levels)
    cols = [ref.astype(jnp.float32) for ref in (carried_before[:, carrier:], cols_ref[...], carried_after[:, carrier:])]
    rows = jnp.concatenate([c.T for c in cols], axis=1).astype(jnp.bfloat16)

    if opens:
        moment[...] = jnp.zeros_like(moment)
        projected[...] = jnp.zeros_like(projected)
        packed[0] = jnp.zeros(packed.shape[1:], packed.dtype)

    copies = []
    for (first, width), (before_ref, after_ref) in zip(spans_of, sources, strict=True):
        for low_lane in range(0, width, PIECE):
            size = min(PIECE, width - low_lane)
            local = slice(low_lane, low_lane + size)
            overall = slice(first + low_lane, first + low_lane + size)
            table[0:levels, :size] = before_ref[:, local]
            table[levels : 2 * levels, :size] = here_ref[:, overall]
            table[2 * levels : high, :size] = after_ref[:, local]
            depth = jnp.dot(rows, table[:high, :size], preferred_element_type=jnp.float32)
            spectrum = jnp.exp(-depth)
            inside = slice(first + low_lane - begin, first + low_lane - begin + size)
            modelled[:, inside] = spectrum
            copy = pltpu.make_async_copy(modelled.at[:, inside], spectrum_ref.at[:, overall], sems.at[len(copies)])
            copy.start()
            copies.append(copy)
            table[high:, :size] = (spectrum * spectrum).astype(jnp.bfloat16)
            groups = range(overall.start // LANES, overall.stop // LANES)
            places = [place_ref[g : g + 1, :] for g in groups]
            kept = jnp.concatenate(places, axis=1) >= 0
            error = jnp.where(kept, (measured_ref[:, overall] - spectrum) * spectrum, 0.0).astype(jnp.bfloat16)
            projected[...] += nt_dot(table[:high, :size], error)
            for n, (g, place) in enumerate(zip(groups, places, strict=True)):
                at = base_ref[g, 0] // LANES
                chosen = (iota((2 * LANES, LANES), 0) + at * LANES == place).astype(jnp.bfloat16)
                moved = nt_dot(table[:, n * LANES : (n + 1) * LANES], chosen).astype(jnp.bfloat16)
                packed[at] = packed[at] + moved[:, :LANES]
                packed[at + 1] = moved[:, LANES:]

    def one_block(block, parts):
        wide = parts * LANES
        for p in range(parts):
            lane = slice(p * LANES, (p + 1) * LANES)
            weights[:, lane] = packed[block + p, high:, :]
            for k in range(3):
                level_rows = packed[block + p, k * levels : (k + 1) * levels, :]
                for m, low, offset, count in spans:
                    pairs[k, offset : offset + count, lane] = level_rows[low:, :] * level_rows[m : m + 1, :]
        for k in range(3):
            moment[k] += nt_dot(pairs[k, :, :wide], weights[:, :wide])

    parts = BLOCK // LANES
    done = base_ref[begin // LANES, 0] // BLOCK
    count = base_ref[end // LANES, 0]
    ready = count // BLOCK
    lax.fori_loop(done, ready, lambda block, carry: (one_block(block * parts, parts), carry)[1], 0)

    if closes:
        last = base_ref[end // LANES - 1, 0] // LANES
        for d in range(2, parts + 1):
            packed[last + d] = jnp.zeros(packed.shape[1:], packed.dtype)
        left = count - ready * BLOCK

        @pl.when(left > BLOCK // 2)
        def _():
            one_block(ready * parts, parts)

        @pl.when((left > 0) & (left <= BLOCK // 2))
        def _():
            one_block(ready * parts, parts // 2)

        lane = iota((levels, LANES), 1)
        for k in range(3):
            gradient = jnp.sum(cols[k] * projected[k * levels : (k + 1) * levels, :], axis=1, keepdims=True)
            result = jnp.where(lane == levels, gradient, 0.0)
            for m, low, offset, count in spans:
                column = jnp.sum(
                    moment[k, offset : offset + count, :] * (cols[k][low:, :] * cols[k][m : m + 1, :]),
                    axis=1,
                    keepdims=True,
                )
                if low:
                    column = jnp.concatenate([jnp.zeros((low, 1), jnp.float32), column], axis=0)
                result = jnp.where(lane == m, column, result)
            terms_refs[k][...] = result
    for copy in copies:
        copy.wait()


def chunk(base, place, here, measured, cols, carried, carrier, spans_of, sources, state, closes):
    levels, points = here.shape
    rays = measured.shape[0]
    _, pair_count = pair_rows(levels)
    opens = state is None
    smem = pl.BlockSpec(memory_space=pltpu.SMEM)
    vmem = pl.BlockSpec(memory_space=pltpu.VMEM)
    hbm = pl.BlockSpec(memory_space=pltpu.HBM)
    width = sum(w for _, w in spans_of)
    args = [base, place, here, measured, cols, *carried]
    specs = [smem] + [vmem] * 6
    for pair in sources:
        args += pair
        specs += [vmem, vmem]
    aliases = {}
    if not opens:
        aliases = {len(args) + n: n for n in range(4)}
        args += state
        specs += [hbm, vmem, vmem, vmem]
    shapes = [
        jax.ShapeDtypeStruct(measured.shape, jnp.float32),
        jax.ShapeDtypeStruct(((points + BLOCK) // LANES + 2, 3 * levels + rays, LANES), jnp.bfloat16),
        jax.ShapeDtypeStruct((3, pair_count, rays), jnp.float32),
        jax.ShapeDtypeStruct((3 * levels, rays), jnp.float32),
    ]
    out_specs = [hbm, vmem, vmem, vmem]
    if closes:
        shapes += [jax.ShapeDtypeStruct((levels, LANES), jnp.float32)] * 3
        out_specs += [vmem] * 3
    outs = pl.pallas_call(
        functools.partial(chunk_kernel, spans_of=spans_of, carrier=carrier, opens=opens, closes=closes),
        in_specs=specs,
        out_specs=out_specs,
        out_shape=shapes,
        scratch_shapes=[
            pltpu.VMEM((3 * levels + rays, PIECE), jnp.bfloat16),
            pltpu.VMEM((rays, width), jnp.float32),
            pltpu.VMEM((3, pair_count, BLOCK), jnp.bfloat16),
            pltpu.VMEM((rays, BLOCK), jnp.bfloat16),
            pltpu.SemaphoreType.DMA((sum(pl.cdiv(w, PIECE) for _, w in spans_of),)),
        ],
        input_output_aliases=aliases,
        compiler_params=pltpu.CompilerParams(vmem_limit_bytes=CHUNK_BYTES),
        cost_estimate=CHEAP,
        name="chunk",
    )(*args)
    return outs[:4], outs[4:]


def solve_kernel(*refs, scale):
    parts = refs[:6]
    prior_ref, out_ref = refs[6:]
    levels = prior_ref.shape[1]
    total = parts[0][...]
    for part in parts[1:]:
        total = total + part[...]
    terms = total * scale
    row = iota((levels, LANES), 0)
    lane = iota((levels, LANES), 1)
    square = terms[:, :levels]
    flipped = jnp.concatenate([square.T, jnp.zeros((levels, LANES - levels), jnp.float32)], axis=1)
    lower = row // ROWS >= lane // ROWS
    work = jnp.where(lower | (lane >= levels), terms, flipped)
    diagonal = jnp.sum(jnp.where(row == lane, work, 0.0), axis=1, keepdims=True)
    mean = jnp.sum(diagonal, axis=0, keepdims=True) * (1.0 / levels) + 1e-06
    eye = iota((levels, levels), 0) == iota((levels, levels), 1)
    prior = jnp.sum(jnp.where(eye, prior_ref[...], 0.0), axis=1, keepdims=True)
    work = work + jnp.where(row == lane, prior * mean, 0.0)
    for i in range(levels):
        pivot_row = work[i : i + 1, :]
        scaled = pivot_row * (1.0 / pivot_row[:, i : i + 1])
        column = work[:, i : i + 1]
        factor = jnp.where(row[:, :1] == i, column - 1.0, column)
        work = work - factor * scaled
    column = work[:, levels : levels + 1]
    out_ref[...] = -jnp.sum(jnp.where(eye, column, 0.0), axis=0, keepdims=True)


def solve(parts, prior_weight, scale):
    return pl.pallas_call(
        functools.partial(solve_kernel, scale=scale),
        out_shape=jax.ShapeDtypeStruct((1, prior_weight.shape[1]), jnp.float32),
        compiler_params=pltpu.CompilerParams(vmem_limit_bytes=SMALL_BYTES),
        cost_estimate=CHEAP,
        name="solve",
    )(*parts, prior_weight)


def swapped(block, axis):
    size = lax.axis_size(axis)
    return lax.ppermute(block, axis, [(i, size - 1 - i) for i in range(size)])


def shards(absorption, absorber, seg_level, seg_count, seg_length, measured, window_mask, prior_weight):
    table = absorption[0]
    levels, points = table.shape
    rays = measured.shape[1]
    unit = points // sum(WIDTHS)
    widths = [w * unit for w in WIDTHS]
    firsts = [sum(widths[:c]) for c in range(len(widths))]
    mask = window_mask.reshape(points // LANES, LANES)
    level = jnp.swapaxes(seg_level[0], 1, 2)
    length = jnp.swapaxes(seg_length[0], 1, 2)
    count = seg_count.reshape(3, 1, rays)
    upward, downward, cols, place, base = prepare(
        level, count, length, absorber, mask, table, firsts[CARRIER], widths[CARRIER]
    )
    base = base[:, :1]
    below = []
    above = []
    for c, (first, width) in enumerate(zip(firsts, widths, strict=True)):
        piece = table[:, first : first + width]
        below.append(passed_along(upward if c == CARRIER else piece, "sector", 1))
        above.append(passed_along(downward if c == CARRIER else piece, "sector", -1))
    state = None
    carried = (below[CARRIER], above[CARRIER])
    for n, group in enumerate(GROUPS):
        spans_of = tuple((firsts[c], widths[c]) for c in group)
        sources = [(below[c], above[c]) for c in group]
        closes = n == len(GROUPS) - 1
        state, terms = chunk(
            base, place, table, measured[0], cols, carried, widths[CARRIER], spans_of, sources, state, closes
        )
    spectrum = state[0]
    mine = (terms[1], passed_along(terms[0], "sector", -1), passed_along(terms[2], "sector", 1))
    others = tuple(swapped(part, "spec") for part in mine)
    scale = 1.0 / (rays * points * lax.axis_size("spec"))
    state_step = solve(mine + others, prior_weight[None, :], scale)
    return (spectrum[None], state_step)


def solution(mesh):
    return jax.shard_map(
        shards,
        mesh=mesh,
        in_specs=(
            P(("orbits", "sector"), None, "spec"),
            P(("orbits", "sector"), None),
            P(("orbits", "sector"), None, None, None),
            P(("orbits", "sector"), None, None),
            P(("orbits", "sector"), None, None, None),
            P(("orbits", "sector"), None, "spec"),
            P("spec"),
            P(),
        ),
        out_specs=(P(("orbits", "sector"), None, "spec"), P(("orbits", "sector"), None)),
        check_vma=False,
    )
```

time: 84.4 us -> 67.7 us (0.80)
  Pallas kernels: 38.2 us -> 24.9 us
  waiting for transfers between devices: 16.1 us -> 12.1 us
  local copies, waits for them, and re-layouts: 4.65 us -> 7.35 us
  starting transfers between devices: 23.5 us -> 22.1 us
    pallas_call x4, Pallas kernels: 31.2 us -> 18.7 us  [the longest x3 18.1 us: chunk(): pl.pallas_call(functools.partial(chunk_kernel, spans_of=spans_of, carrier...]
    unnamed x26 -> x18, local copies, waits for them, and re-layouts: 2.69 us -> 7.32 us
    ppermute x10, waiting for transfers between devices: 14.9 us -> 10.9 us  [passed_along(): return lax.ppermute(block, axis, route)]
    slice x2 -> x1, local copies, waits for them, and re-layouts: 1.96 us -> 0.03 us  [shards(): piece = table[:, first:first + width]]
    ppermute x10, starting transfers between devices: 23.5 us -> 22.1 us  [passed_along(): return lax.ppermute(block, axis, route)]
  transfers between devices with their start and end apart: 13 -> 13, of which waited for: 5 -> 4; matrix products, arithmetic and copies ran while one was open for 1% -> 0% of each run, Pallas kernels for 26% -> 14%
where the time goes in v1:
time: 67.7 us; the launch traced here: 67.2 us
  Pallas kernels  24.9 us (37%)
  starting transfers between devices  22.1 us (33%)
  waiting for transfers between devices  12.1 us (18%)
  local copies, waits for them, and re-layouts  7.35 us (11%)
  between operations  0.75 us (1%)
    ppermute x10, starting transfers between devices, passed_along(): return lax.ppermute(block, axis, route)  22.1 us
    pallas_call x3, Pallas kernels, chunk(): pl.pallas_call(functools.partial(chunk_kernel, spans_of=spans_of, carrier...  18.1 us
    ppermute x10, waiting for transfers between devices, passed_along(): return lax.ppermute(block, axis, route)  10.9 us
    unnamed x18, local copies, waits for them, and re-layouts  7.32 us
    pallas_call x1, Pallas kernels, solve(): pl.pallas_call(functools.partial(solve_kernel, scale=scale), out_shape=ja...  6.18 us
  transfers between devices with their start and end apart: 13, of which 4 were waited for; matrix products, arithmetic and copies ran while one was open for 0% of the time, Pallas kernels for 14%

profile of v1, /device:TPU:0, one launch (start us, length us, event | category | flops | bytes accessed | tf_op | source)
XLA Modules:
  0.0 67.2 jit_solution(13101335396021516725)
XLA Ops:
  0.6 1.0 %copy-done.1 = bf16[1,64,4096]{2,1,0:T(8,128)(2,1)S(1)} copy-done((bf16[1,64,4096]{2,1,0:T(8,128)(2,1)S(1)}, bf16[1,64,4096]{2,1,0:T(8,128)(2,1)}, u32[]{:S(2)}) %copy-start.1) | copy-done | bytes 524312
  1.7 0.8 %copy-done.3 = s32[1,3,128,32]{2,3,1,0:T(8,128)S(1)} copy-done((s32[1,3,128,32]{2,3,1,0:T(8,128)S(1)}, s32[1,3,128,32]{2,3,1,0:T(8,128)}, u32[]{:S(2)}) %copy-start.3) | copy-done | bytes 49176
  2.5 0.8 %copy-done.4 = f32[1,3,128,32]{2,3,1,0:T(8,128)S(1)} copy-done((f32[1,3,128,32]{2,3,1,0:T(8,128)S(1)}, f32[1,3,128,32]{2,3,1,0:T(8,128)}, u32[]{:S(2)}) %copy-start.4) | copy-done | bytes 49176
  3.3 0.7 %copy-done.5 = s32[4096]{0:T(1024)S(1)} copy-done((s32[4096]{0:T(1024)S(1)}, s32[4096]{0:T(1024)}, u32[]{:S(2)}) %copy-start.5) | copy-done | bytes 16408
  4.0 0.7 %copy-done.6 = s32[1,3,128]{2,0,1:T(1,128)S(1)} copy-done((s32[1,3,128]{2,0,1:T(1,128)S(1)}, s32[1,3,128]{2,0,1:T(1,128)}, u32[]{:S(2)}) %copy-start.6) | copy-done | bytes 1560
  4.7 0.7 copy-done.7
  5.3 0.6 prepare.1
  6.0 3.0 %collective-permute-start = (bf16[64,1152]{1,0:T(8,128)(2,1)S(1)}, bf16[64,1152]{1,0:T(8,128)(2,1)S(1)}, u32[]{:S(2)}, u32[]{:S(2)}) collective-permute-start(bf16[64,1152]{1,0:T(8,128)(2,1)S(1)} %get-tuple-element.22), channel_id=1, source_target_pairs={{14,0},{0,2},{2,4},{4,6},{6,8},{8,10},{10,12},{12,14},{15,1},{1,3}... | collective-permute-start | bytes 442376 | tf_op jit(solution)/shard_map/ppermute | solution.py:25
  9.0 1.6 %collective-permute-start.6 = (bf16[64,1024]{1,0:T(8,128)(2,1)S(1)}, bf16[64,1024]{1,0:T(8,128)(2,1)S(1)}, u32[]{:S(2)}, u32[]{:S(2)}) collective-permute-start(bf16[64,1024]{1,0:T(8,128)(2,1)S(1)} %get-tuple-element.36), channel_id=1, source_target_pairs={{14,0},{0,2},{2,4},{4,6},{6,8},{8,10},{10,12},{12,14},{15,1},{1,3}... | collective-permute-start | bytes 393224 | tf_op jit(solution)/shard_map/ppermute | solution.py:25
  10.6 3.2 %collective-permute-start.7 = (bf16[64,1024]{1,0:T(8,128)(2,1)S(1)}, bf16[64,1024]{1,0:T(8,128)(2,1)S(1)}, u32[]{:S(2)}, u32[]{:S(2)}) collective-permute-start(bf16[64,1024]{1,0:T(8,128)(2,1)S(1)} %get-tuple-element.36), channel_id=1, source_target_pairs={{2,0},{4,2},{6,4},{8,6},{10,8},{12,10},{14,12},{0,14},{3,1},{5,3},... | collective-permute-start | bytes 393224 | tf_op jit(solution)/shard_map/ppermute | solution.py:25
  14.2 1.6 %collective-permute-start.4 = (bf16[64,1024]{1,0:T(8,128)(2,1)S(1)}, bf16[64,1024]{1,0:T(8,128)(2,1)S(1)}, u32[]{:S(2)}, u32[]{:S(2)}) collective-permute-start(bf16[64,1024]{1,0:T(8,128)(2,1)S(1)} %get-tuple-element.37), channel_id=1, source_target_pairs={{14,0},{0,2},{2,4},{4,6},{6,8},{8,10},{10,12},{12,14},{15,1},{1,3}... | collective-permute-start | bytes 393224 | tf_op jit(solution)/shard_map/ppermute | solution.py:25
  15.8 6.2 %collective-permute-done.6.refs_7_ = bf16[64,1024]{1,0:T(8,128)(2,1)S(1)} collective-permute-done((bf16[64,1024]{1,0:T(8,128)(2,1)S(1)}, bf16[64,1024]{1,0:T(8,128)(2,1)S(1)}, u32[]{:S(2)}, u32[]{:S(2)}) %collective-permute-start.6) | collective-permute-done | bytes 131104 | tf_op jit(solution)/shard_map/ppermute | solution.py:25
  22.0 5.5 %collective-permute-start.5 = (bf16[64,1024]{1,0:T(8,128)(2,1)S(1)}, bf16[64,1024]{1,0:T(8,128)(2,1)S(1)}, u32[]{:S(2)}, u32[]{:S(2)}) collective-permute-start(bf16[64,1024]{1,0:T(8,128)(2,1)S(1)} %get-tuple-element.37), channel_id=1, source_target_pairs={{2,0},{4,2},{6,4},{8,6},{10,8},{12,10},{14,12},{0,14},{3,1},{5,3},... | collective-permute-start | bytes 393224 | tf_op jit(solution)/shard_map/ppermute | solution.py:25
  27.5 4.7 %collective-permute-start.3 = (bf16[64,1024]{1,0:T(8,128)(2,1)S(1)}, bf16[64,1024]{1,0:T(8,128)(2,1)S(1)}, u32[]{:S(2)}, u32[]{:S(2)}) collective-permute-start(bf16[64,1024]{1,0:T(8,128)(2,1)S(1)} %get-tuple-element.38), channel_id=1, source_target_pairs={{2,0},{4,2},{6,4},{8,6},{10,8},{12,10},{14,12},{0,14},{3,1},{5,3},... | collective-permute-start | bytes 393224 | tf_op jit(solution)/shard_map/ppermute | solution.py:25
  32.3 1.6 %copy-done = f32[1,128,4096]{2,1,0:T(8,128)S(1)} copy-done((f32[1,128,4096]{2,1,0:T(8,128)S(1)}, f32[1,128,4096]{2,1,0:T(8,128)}, u32[]{:S(2)}) %copy-start) | copy-done | bytes 2097176
  33.9 1.0 %copy-done.2 = bf16[1,64,4096]{2,1,0:T(8,128)(2,1)S(1)} copy-done((bf16[1,64,4096]{2,1,0:T(8,128)(2,1)S(1)}, bf16[1,64,4096]{2,1,0:T(8,128)(2,1)}, u32[]{:S(2)}) %copy-start.2) | copy-done | bytes 524312
  34.9 5.3 %chunk.3 = (f32[128,4096]{1,0:T(8,128)}, bf16[38,320,128]{2,1,0:T(8,128)(2,1)S(1)}, f32[3,2560,128]{2,1,0:T(8,128)S(1)}, f32[192,128]{1,0:T(8,128)S(1)}) custom-call(s32[40,1]{1,0:T(8,128)S(1)} %bitcast.21, s32[32,128]{1,0:T(8,128)S(1)} %get-tuple-element.20.refs_1_, bf16[64,4096]{1,0:T(8,128)(2,1)S(1)} %bitcast.18, f32[128,4096]{1,0:T(8,128)S(1)} %bitcast.13, ...), custom_call_target="tpu_custom_call" | custom-call | flops 1 | bytes 1 | tf_op jit(solution)/shard_map/chunk/pallas_call | solution.py:247
  40.3 4.3 %chunk.4 = (f32[128,4096]{1,0:T(8,128)}, bf16[38,320,128]{2,1,0:T(8,128)(2,1)S(1)}, f32[3,2560,128]{2,1,0:T(8,128)S(1)}, f32[192,128]{1,0:T(8,128)S(1)}) custom-call(s32[40,1]{1,0:T(8,128)S(1)} %bitcast.22, s32[32,128]{1,0:T(8,128)S(1)} %get-tuple-element.20.refs_1_, ...), custom_call_target="tpu_custom_call", output_to_operand_aliasing={{0}: (9, {}), {1}: (10, {}), {2}: (11, {}), {3}: (12, {})} | custom-call | flops 1 | bytes 1 | tf_op jit(solution)/shard_map/chunk/pallas_call | solution.py:247
  44.6 8.5 %chunk.5 = (f32[128,4096]{1,0:T(8,128)}, bf16[38,320,128]{2,1,0:T(8,128)(2,1)S(1)}, f32[3,2560,128]{2,1,0:T(8,128)S(1)}, f32[192,128]{1,0:T(8,128)S(1)}, f32[64,...) custom-call(s32[40,1]{1,0:T(8,128)S(1)} %bitcast.23, ...), custom_call_target="tpu_custom_call", output_to_operand_aliasing={{0}: (9, {}), {1}: (10, {}), {2}: (11, {}), {3}: (12, {})} | custom-call | flops 1 | bytes 1 | tf_op jit(solution)/shard_map/chunk/pallas_call | solution.py:247
  53.2 2.0 %collective-permute-start.9 = (f32[64,128]{1,0:T(8,128)S(1)}, f32[64,128]{1,0:T(8,128)S(1)}, u32[]{:S(2)}, u32[]{:S(2)}) collective-permute-start(f32[64,128]{1,0:T(8,128)S(1)} %get-tuple-element.35), channel_id=1, source_target_pairs={{14,0},{0,2},{2,4},{4,6},{6,8},{8,10},{10,12},{12,14},{15,1},{1,3}... | collective-permute-start | bytes 98312 | tf_op jit(solution)/shard_map/ppermute | solution.py:25
  55.2 1.9 %collective-permute-done.8.refs_1_ = f32[64,128]{1,0:T(8,128)S(1)} collective-permute-done((f32[64,128]{1,0:T(8,128)S(1)}, f32[64,128]{1,0:T(8,128)S(1)}, u32[]{:S(2)}, u32[]{:S(2)}) %collective-permute-start.8) | collective-permute-done | bytes 32800 | tf_op jit(solution)/shard_map/ppermute | solution.py:25
  57.1 2.8 %collective-permute-done.9.refs_2_ = f32[64,128]{1,0:T(8,128)S(1)} collective-permute-done((f32[64,128]{1,0:T(8,128)S(1)}, f32[64,128]{1,0:T(8,128)S(1)}, u32[]{:S(2)}, u32[]{:S(2)}) %collective-permute-start.9) | collective-permute-done | bytes 32800 | tf_op jit(solution)/shard_map/ppermute | solution.py:25
  59.8 1.2 %collective-permute-done.12.refs_5_ = f32[64,128]{1,0:T(8,128)S(1)} collective-permute-done((f32[64,128]{1,0:T(8,128)S(1)}, f32[64,128]{1,0:T(8,128)S(1)}, u32[]{:S(2)}, u32[]{:S(2)}) %collective-permute-start.12) | collective-permute-done | bytes 32800 | tf_op jit(solution)/shard_map/ppermute | solution.py:308
  61.0 6.2 %solve.1 = f32[1,64]{1,0:T(1,128)} custom-call(f32[64,128]{1,0:T(8,128)S(1)} %get-tuple-element.33.refs_0_, f32[64,128]{1,0:T(8,128)S(1)} %collective-permute-done.8.refs_1_, f32[64,128]{1,0:T(8,128)S(1)} %collective-permute-done.9.refs_2_, f32[64,128]{1,0:T(8,128)S(1)} %collective-permute-done.10.refs_3_, f32[64,128]{1,0:T(8,128)S(1)} %collective-permute-done.11.refs_4_, ...), custom_call_target="tpu_custom_call" | custom-call | flops 1 | bytes 1 | tf_op jit(solution)/shard_map/solve/pallas_call | solution.py:297
  (26 shorter events, 0.6 us)
Async XLA Ops:
  0.6 1.0 %copy-start.1 = (bf16[1,64,4096]{2,1,0:T(8,128)(2,1)S(1)}, bf16[1,64,4096]{2,1,0:T(8,128)(2,1)}, u32[]{:S(2)}) copy-start(bf16[1,64,4096]{2,1,0:T(8,128)(2,1)} %param.8) | copy-start | bytes 1572868
  1.7 0.8 %copy-start.3 = (s32[1,3,128,32]{2,3,1,0:T(8,128)S(1)}, s32[1,3,128,32]{2,3,1,0:T(8,128)}, u32[]{:S(2)}) copy-start(s32[1,3,128,32]{2,3,1,0:T(8,128)} %param.10) | copy-start | bytes 147460
  2.5 0.8 %copy-start.4 = (f32[1,3,128,32]{2,3,1,0:T(8,128)S(1)}, f32[1,3,128,32]{2,3,1,0:T(8,128)}, u32[]{:S(2)}) copy-start(f32[1,3,128,32]{2,3,1,0:T(8,128)} %param.12) | copy-start | bytes 147460
  3.3 0.7 %copy-start.5 = (s32[4096]{0:T(1024)S(1)}, s32[4096]{0:T(1024)}, u32[]{:S(2)}) copy-start(s32[4096]{0:T(1024)} %param.14) | copy-start | bytes 49156
  4.0 0.7 %copy-start.6 = (s32[1,3,128]{2,0,1:T(1,128)S(1)}, s32[1,3,128]{2,0,1:T(1,128)}, u32[]{:S(2)}) copy-start(s32[1,3,128]{2,0,1:T(1,128)} %param.11) | copy-start | bytes 4612
  4.7 0.7 copy-start.7
  6.0 21.6 %collective-permute-start = (bf16[64,1152]{1,0:T(8,128)(2,1)S(1)}, bf16[64,1152]{1,0:T(8,128)(2,1)S(1)}, u32[]{:S(2)}, u32[]{:S(2)}) collective-permute-start(bf16[64,1152]{1,0:T(8,128)(2,1)S(1)} %get-tuple-element.22), channel_id=1, source_target_pairs={{14,0},{0,2},{2,4},{4,6},{6,8},{8,10},{10,12},{12,14},{15,1},{1,3}... | collective-permute-start | bytes 442376 | tf_op jit(solution)/shard_map/ppermute | solution.py:25
  9.0 13.0 %collective-permute-start.6 = (bf16[64,1024]{1,0:T(8,128)(2,1)S(1)}, bf16[64,1024]{1,0:T(8,128)(2,1)S(1)}, u32[]{:S(2)}, u32[]{:S(2)}) collective-permute-start(bf16[64,1024]{1,0:T(8,128)(2,1)S(1)} %get-tuple-element.36), channel_id=1, source_target_pairs={{14,0},{0,2},{2,4},{4,6},{6,8},{8,10},{10,12},{12,14},{15,1},{1,3}... | collective-permute-start | bytes 393224 | tf_op jit(solution)/shard_map/ppermute | solution.py:25
  10.6 16.9 %collective-permute-start.7 = (bf16[64,1024]{1,0:T(8,128)(2,1)S(1)}, bf16[64,1024]{1,0:T(8,128)(2,1)S(1)}, u32[]{:S(2)}, u32[]{:S(2)}) collective-permute-start(bf16[64,1024]{1,0:T(8,128)(2,1)S(1)} %get-tuple-element.36), channel_id=1, source_target_pairs={{2,0},{4,2},{6,4},{8,6},{10,8},{12,10},{14,12},{0,14},{3,1},{5,3},... | collective-permute-start | bytes 393224 | tf_op jit(solution)/shard_map/ppermute | solution.py:25
  13.8 18.5 %collective-permute-start.1 = (bf16[64,1152]{1,0:T(8,128)(2,1)S(1)}, bf16[64,1152]{1,0:T(8,128)(2,1)S(1)}, u32[]{:S(2)}, u32[]{:S(2)}) collective-permute-start(bf16[64,1152]{1,0:T(8,128)(2,1)S(1)} %get-tuple-element.23), channel_id=1, source_target_pairs={{2,0},{4,2},{6,4},{8,6},{10,8},{12,10},{14,12},{0,14},{3,1},{5,3},... | collective-permute-start | bytes 442376 | tf_op jit(solution)/shard_map/ppermute | solution.py:25
  14.2 26.0 %collective-permute-start.4 = (bf16[64,1024]{1,0:T(8,128)(2,1)S(1)}, bf16[64,1024]{1,0:T(8,128)(2,1)S(1)}, u32[]{:S(2)}, u32[]{:S(2)}) collective-permute-start(bf16[64,1024]{1,0:T(8,128)(2,1)S(1)} %get-tuple-element.37), channel_id=1, source_target_pairs={{14,0},{0,2},{2,4},{4,6},{6,8},{8,10},{10,12},{12,14},{15,1},{1,3}... | collective-permute-start | bytes 393224 | tf_op jit(solution)/shard_map/ppermute | solution.py:25
  22.0 18.2 %collective-permute-start.5 = (bf16[64,1024]{1,0:T(8,128)(2,1)S(1)}, bf16[64,1024]{1,0:T(8,128)(2,1)S(1)}, u32[]{:S(2)}, u32[]{:S(2)}) collective-permute-start(bf16[64,1024]{1,0:T(8,128)(2,1)S(1)} %get-tuple-element.37), channel_id=1, source_target_pairs={{2,0},{4,2},{6,4},{8,6},{10,8},{12,10},{14,12},{0,14},{3,1},{5,3},... | collective-permute-start | bytes 393224 | tf_op jit(solution)/shard_map/ppermute | solution.py:25
  27.5 17.0 %collective-permute-start.2 = (bf16[64,1024]{1,0:T(8,128)(2,1)S(1)}, bf16[64,1024]{1,0:T(8,128)(2,1)S(1)}, u32[]{:S(2)}, u32[]{:S(2)}) collective-permute-start(bf16[64,1024]{1,0:T(8,128)(2,1)S(1)} %get-tuple-element.38), channel_id=1, source_target_pairs={{14,0},{0,2},{2,4},{4,6},{6,8},{8,10},{10,12},{12,14},{15,1},{1,3}... | collective-permute-start | bytes 393224 | tf_op jit(solution)/shard_map/ppermute | solution.py:25
  27.5 17.0 %collective-permute-start.3 = (bf16[64,1024]{1,0:T(8,128)(2,1)S(1)}, bf16[64,1024]{1,0:T(8,128)(2,1)S(1)}, u32[]{:S(2)}, u32[]{:S(2)}) collective-permute-start(bf16[64,1024]{1,0:T(8,128)(2,1)S(1)} %get-tuple-element.38), channel_id=1, source_target_pairs={{2,0},{4,2},{6,4},{8,6},{10,8},{12,10},{14,12},{0,14},{3,1},{5,3},... | collective-permute-start | bytes 393224 | tf_op jit(solution)/shard_map/ppermute | solution.py:25
  32.3 1.6 %copy-start = (f32[1,128,4096]{2,1,0:T(8,128)S(1)}, f32[1,128,4096]{2,1,0:T(8,128)}, u32[]{:S(2)}) copy-start(f32[1,128,4096]{2,1,0:T(8,128)} %param.13) | copy-start | bytes 6291460
  33.9 1.0 %copy-start.2 = (bf16[1,64,4096]{2,1,0:T(8,128)(2,1)S(1)}, bf16[1,64,4096]{2,1,0:T(8,128)(2,1)}, u32[]{:S(2)}) copy-start(bf16[1,64,4096]{2,1,0:T(8,128)(2,1)} %param.8) | copy-start | bytes 1572868
  44.6 16.5 %copy-start.8 = (f32[64]{0:T(128)S(1)}, f32[64]{0:T(128)}, u32[]{:S(2)}) copy-start(f32[64]{0:T(128)} %param.15) | copy-start | bytes 772
  53.1 4.0 %collective-permute-start.8 = (f32[64,128]{1,0:T(8,128)S(1)}, f32[64,128]{1,0:T(8,128)S(1)}, u32[]{:S(2)}, u32[]{:S(2)}) collective-permute-start(f32[64,128]{1,0:T(8,128)S(1)} %get-tuple-element.34), channel_id=1, source_target_pairs={{2,0},{4,2},{6,4},{8,6},{10,8},{12,10},{14,12},{0,14},{3,1},{5,3},... | collective-permute-start | bytes 98312 | tf_op jit(solution)/shard_map/ppermute | solution.py:25
  53.2 6.7 %collective-permute-start.9 = (f32[64,128]{1,0:T(8,128)S(1)}, f32[64,128]{1,0:T(8,128)S(1)}, u32[]{:S(2)}, u32[]{:S(2)}) collective-permute-start(f32[64,128]{1,0:T(8,128)S(1)} %get-tuple-element.35), channel_id=1, source_target_pairs={{14,0},{0,2},{2,4},{4,6},{6,8},{8,10},{10,12},{12,14},{15,1},{1,3}... | collective-permute-start | bytes 98312 | tf_op jit(solution)/shard_map/ppermute | solution.py:25
  55.2 4.7 %collective-permute-start.10 = (f32[64,128]{1,0:T(8,128)S(1)}, f32[64,128]{1,0:T(8,128)S(1)}, u32[]{:S(2)}, u32[]{:S(2)}) collective-permute-start(f32[64,128]{1,0:T(8,128)S(1)} %get-tuple-element.33.refs_0_), channel_id=1, source_target_pairs={{0,1},{1,0},{2,3},{3,2},{4,5},{5,4},{6,7},{7,6},{8,9},{9,8},{10,11... | collective-permute-start | bytes 98312 | tf_op jit(solution)/shard_map/ppermute | solution.py:308
  57.1 2.8 %collective-permute-start.11 = (f32[64,128]{1,0:T(8,128)S(1)}, f32[64,128]{1,0:T(8,128)S(1)}, u32[]{:S(2)}, u32[]{:S(2)}) collective-permute-start(f32[64,128]{1,0:T(8,128)S(1)} %collective-permute-done.8.refs_1_), channel_id=1, source_target_pairs={{0,1},{1,0},{2,3},{3,2},{4,5},{5,4},{6,7},{7,6},{8,9},{9,8},{10,11... | collective-permute-start | bytes 98312 | tf_op jit(solution)/shard_map/ppermute | solution.py:308
  59.8 1.2 %collective-permute-start.12 = (f32[64,128]{1,0:T(8,128)S(1)}, f32[64,128]{1,0:T(8,128)S(1)}, u32[]{:S(2)}, u32[]{:S(2)}) collective-permute-start(f32[64,128]{1,0:T(8,128)S(1)} %collective-permute-done.9.refs_2_), channel_id=1, source_target_pairs={{0,1},{1,0},{2,3},{3,2},{4,5},{5,4},{6,7},{7,6},{8,9},{9,8},{10,11... | collective-permute-start | bytes 98312 | tf_op jit(solution)/shard_map/ppermute | solution.py:308

commit v2 on v1

--- a/solution.py
+++ b/solution.py
@@ -11,9 +11,9 @@
 ROWS = 16
 PIECE = 512
 BLOCK = 512
-WIDTHS = (2, 2, 2, 2)
-GROUPS = ((0, 1), (2,), (3,))
-CARRIER = 1
+WIDTHS = (20, 12)
+GROUPS = ((0,), (1,))
+CARRIER = 0
 SMALL_BYTES = 4 << 20
 CHUNK_BYTES = 16 << 20
 CHEAP = pl.CostEstimate(flops=1, transcendentals=0, bytes_accessed=1)
@@ -33,16 +33,23 @@
     return lax.dot_general(a, b, (((1,), (1,)), ((), ())), preferred_element_type=jnp.float32)
 
 
-def prepare_kernel(level_ref, count_ref, length_ref, absorber_ref, mask_ref, table_ref, *outs, first, width):
-    up_ref, down_ref, cols_ref, place_ref, base_ref, sems = outs
+def pinned(*arrays):
+    return [pltpu.with_memory_space_constraint(array, pltpu.HBM) for array in arrays]
+
+
+def prepare_kernel(level_hbm, count_hbm, length_hbm, absorber_hbm, table_hbm, *outs, first, width):
+    up_ref, down_ref, cols_ref, level_ref, count_ref, length_ref, absorber_ref, sems = outs
     levels = absorber_ref.shape[1]
     sets, segs, rays = level_ref.shape
-    copies = [
-        pltpu.make_async_copy(table_ref.at[:, pl.ds(first, width)], ref.at[:, pl.ds(0, width)], sems.at[n])
-        for n, ref in enumerate((up_ref, down_ref))
-    ]
+    arguments = ((level_hbm, level_ref), (length_hbm, length_ref), (count_hbm, count_ref), (absorber_hbm, absorber_ref))
+    copies = [pltpu.make_async_copy(a, b, sems.at[n]) for n, (a, b) in enumerate(arguments)]
+    for n, ref in enumerate((up_ref, down_ref)):
+        source = table_hbm.at[:, pl.ds(first, width)]
+        copies.append(pltpu.make_async_copy(source, ref.at[:, pl.ds(0, width)], sems.at[len(arguments) + n]))
     for copy in copies:
         copy.start()
+    for copy in copies[: len(arguments)]:
+        copy.wait()
     eye = iota((levels, levels), 0) == iota((levels, levels), 1)
     amount = jnp.sum(jnp.where(eye, absorber_ref[...], 0.0), axis=1, keepdims=True)
     level_of = iota((levels, rays), 0)
@@ -59,6 +66,39 @@
             cols_ref[...] = absorbed
         else:
             up_ref[:, width:] = absorbed
+    for copy in copies[len(arguments) :]:
+        copy.wait()
+
+
+def prepare(level, count, length, absorber, table, first, width):
+    rays = level.shape[2]
+    levels = absorber.shape[1]
+    send = jax.ShapeDtypeStruct((levels, width + rays), jnp.bfloat16)
+    hbm = pl.BlockSpec(memory_space=pltpu.HBM)
+    return pl.pallas_call(
+        functools.partial(prepare_kernel, first=first, width=width),
+        in_specs=[hbm] * 5,
+        out_shape=(send, send, jax.ShapeDtypeStruct((levels, rays), jnp.bfloat16)),
+        scratch_shapes=[
+            pltpu.VMEM(level.shape, level.dtype),
+            pltpu.VMEM(count.shape, count.dtype),
+            pltpu.VMEM(length.shape, length.dtype),
+            pltpu.VMEM(absorber.shape, absorber.dtype),
+            pltpu.SemaphoreType.DMA((6,)),
+        ],
+        compiler_params=pltpu.CompilerParams(vmem_limit_bytes=SMALL_BYTES),
+        cost_estimate=CHEAP,
+        name="prepare",
+    )(*pinned(level, count, length, absorber, table))
+
+
+def stage_kernel(cols_ref, mask_hbm, table_hbm, measured_hbm, place_ref, base_ref, table_ref, measured_ref, mask_ref, sems):
+    del cols_ref
+    moves = ((mask_hbm, mask_ref), (table_hbm, table_ref), (measured_hbm, measured_ref))
+    copies = [pltpu.make_async_copy(a, b, sems.at[n]) for n, (a, b) in enumerate(moves)]
+    for copy in copies:
+        copy.start()
+    copies[0].wait()
     groups = mask_ref.shape[0]
     mask = mask_ref[...].astype(jnp.bfloat16)
     before = (iota((LANES, LANES), 0) < iota((LANES, LANES), 1)).astype(jnp.bfloat16)
@@ -70,31 +110,28 @@
     base_ref[pl.ds(0, groups), :] = base.astype(jnp.int32)
     last = base[groups - 1 : groups, :] + total[groups - 1 : groups, :]
     base_ref[pl.ds(groups, 8), :] = jnp.broadcast_to(last, (8, LANES)).astype(jnp.int32)
-    for copy in copies:
+    for copy in copies[1:]:
         copy.wait()
 
 
-def prepare(level, count, length, absorber, mask, table, first, width):
-    rays = level.shape[2]
-    levels = absorber.shape[1]
+def stage(cols, mask, table, measured):
     groups = mask.shape[0]
-    send = jax.ShapeDtypeStruct((levels, width + rays), jnp.bfloat16)
     vmem = pl.BlockSpec(memory_space=pltpu.VMEM)
+    hbm = pl.BlockSpec(memory_space=pltpu.HBM)
     return pl.pallas_call(
-        functools.partial(prepare_kernel, first=first, width=width),
-        in_specs=[vmem] * 5 + [pl.BlockSpec(memory_space=pl.ANY)],
+        stage_kernel,
+        in_specs=[vmem, hbm, hbm, hbm],
         out_shape=(
-            send,
-            send,
-            jax.ShapeDtypeStruct((levels, rays), jnp.bfloat16),
             jax.ShapeDtypeStruct((groups, LANES), jnp.int32),
             jax.ShapeDtypeStruct((groups + 8, LANES), jnp.int32),
+            jax.ShapeDtypeStruct(table.shape, table.dtype),
+            jax.ShapeDtypeStruct(measured.shape, measured.dtype),
         ),
-        scratch_shapes=[pltpu.SemaphoreType.DMA((2,))],
+        scratch_shapes=[pltpu.VMEM(mask.shape, mask.dtype), pltpu.SemaphoreType.DMA((3,))],
         compiler_params=pltpu.CompilerParams(vmem_limit_bytes=SMALL_BYTES),
         cost_estimate=CHEAP,
-        name="prepare",
-    )(level, count, length, absorber, mask, table)
+        name="stage",
+    )(cols, *pinned(mask, table, measured))
 
 
 def pair_rows(levels):
@@ -264,6 +301,34 @@
     return outs[:4], outs[4:]
 
 
+def quad_step(work, row, p):
+    r = [work[p + i : p + i + 1, :] for i in range(4)]
+
+    def entry(i, j):
+        return jnp.broadcast_to(r[i][:, p + j : p + j + 1], r[i].shape)
+
+    a, b, d = entry(0, 0), entry(0, 1), entry(1, 1)
+    f0, f1, g0, g1 = entry(0, 2), entry(0, 3), entry(1, 2), entry(1, 3)
+    h, q, v = entry(2, 2), entry(2, 3), entry(3, 3)
+    inverse = 1.0 / (a * d - b * b)
+    a, b, d = d * inverse, -b * inverse, a * inverse
+    w00, w01 = a * f0 + b * g0, a * f1 + b * g1
+    w10, w11 = b * f0 + d * g0, b * f1 + d * g1
+    h, q, v = h - (f0 * w00 + g0 * w10), q - (f0 * w01 + g0 * w11), v - (f1 * w01 + g1 * w11)
+    inverse = 1.0 / (h * v - q * q)
+    h, q, v = v * inverse, -q * inverse, h * inverse
+    t0, t1 = a * r[0] + b * r[1], b * r[0] + d * r[1]
+    u0, u1 = r[2] - (f0 * t0 + g0 * t1), r[3] - (f1 * t0 + g1 * t1)
+    s2, s3 = h * u0 + q * u1, q * u0 + v * u1
+    s0, s1 = t0 - (w00 * s2 + w01 * s3), t1 - (w10 * s2 + w11 * s3)
+    update = None
+    for i, s in enumerate((s0, s1, s2, s3)):
+        column = work[:, p + i : p + i + 1]
+        term = jnp.where(row[:, :1] == p + i, column - 1.0, column) * s
+        update = term if update is None else update + term
+    return work - update
+
+
 def solve_kernel(*refs, scale):
     parts = refs[:6]
     prior_ref, out_ref = refs[6:]
@@ -283,12 +348,8 @@
     eye = iota((levels, levels), 0) == iota((levels, levels), 1)
     prior = jnp.sum(jnp.where(eye, prior_ref[...], 0.0), axis=1, keepdims=True)
     work = work + jnp.where(row == lane, prior * mean, 0.0)
-    for i in range(levels):
-        pivot_row = work[i : i + 1, :]
-        scaled = pivot_row * (1.0 / pivot_row[:, i : i + 1])
-        column = work[:, i : i + 1]
-        factor = jnp.where(row[:, :1] == i, column - 1.0, column)
-        work = work - factor * scaled
+    for p in range(0, levels, 4):
+        work = quad_step(work, row, p)
     column = work[:, levels : levels + 1]
     out_ref[...] = -jnp.sum(jnp.where(eye, column, 0.0), axis=0, keepdims=True)
 
@@ -319,9 +380,8 @@
     level = jnp.swapaxes(seg_level[0], 1, 2)
     length = jnp.swapaxes(seg_length[0], 1, 2)
     count = seg_count.reshape(3, 1, rays)
-    upward, downward, cols, place, base = prepare(
-        level, count, length, absorber, mask, table, firsts[CARRIER], widths[CARRIER]
-    )
+    upward, downward, cols = prepare(level, count, length, absorber, table, firsts[CARRIER], widths[CARRIER])
+    place, base, table_here, measured_here = stage(cols, mask, table, measured[0])
     base = base[:, :1]
     below = []
     above = []
@@ -336,7 +396,7 @@
         sources = [(below[c], above[c]) for c in group]
         closes = n == len(GROUPS) - 1
         state, terms = chunk(
-            base, place, table, measured[0], cols, carried, widths[CARRIER], spans_of, sources, state, closes
+            base, place, table_here, measured_here, cols, carried, widths[CARRIER], spans_of, sources, state, closes
         )
     spectrum = state[0]
     mine = (terms[1], passed_along(terms[0], "sector", -1), passed_along(terms[2], "sector", 1))

time: 67.7 us -> 59.7 us (0.88)
  starting transfers between devices: 22.1 us -> 11.3 us
  waiting for transfers between devices: 12.1 us -> 22.4 us
  local copies, waits for them, and re-layouts: 7.35 us -> 0.95 us
  Pallas kernels: 24.9 us -> 23.5 us
    ppermute x10 -> x6, starting transfers between devices: 22.1 us -> 11.3 us  [passed_along(): return lax.ppermute(block, axis, route)]
    ppermute x10 -> x6, waiting for transfers between devices: 10.9 us -> 21.2 us  [passed_along(): return lax.ppermute(block, axis, route)]
    unnamed x18 -> x2, local copies, waits for them, and re-layouts: 7.32 us -> 0.01 us
    pallas_call x1, Pallas kernels: 6.18 us -> 3.08 us  [solve(): pl.pallas_call(functools.partial(solve_kernel, scale=scale), out_shape=ja...]
    pallas_call x0 -> x1, Pallas kernels: none -> 1.81 us  [stage(): pl.pallas_call(stage_kernel, in_specs=[vmem, hbm, hbm, hbm], out_shape=(j...]
    slice x1, local copies, waits for them, and re-layouts: 0.03 us -> 0.94 us  [shards(): piece = table[:, first:first + width]]
    pallas_call x3 -> x2, Pallas kernels: 18.1 us -> 17.4 us  [chunk(): pl.pallas_call(functools.partial(chunk_kernel, spans_of=spans_of, carrier...]
  transfers between devices with their start and end apart: 13 -> 9, of which waited for: 4 -> 5; matrix products, arithmetic and copies ran while one was open for 0% -> 2% of each run, Pallas kernels for 14% -> 17%
where the time goes in v2:
time: 59.7 us; the launch traced here: 58.8 us
  Pallas kernels  23.5 us (39%)
  waiting for transfers between devices  22.4 us (38%)
  starting transfers between devices  11.3 us (19%)
  local copies, waits for them, and re-layouts  0.95 us (2%)
  between operations  0.7 us (1%)
    ppermute x6, waiting for transfers between devices, passed_along(): return lax.ppermute(block, axis, route)  21.2 us
    pallas_call x2, Pallas kernels, chunk(): pl.pallas_call(functools.partial(chunk_kernel, spans_of=spans_of, carrier...  17.4 us
    ppermute x6, starting transfers between devices, passed_along(): return lax.ppermute(block, axis, route)  11.3 us
    pallas_call x1, Pallas kernels, solve(): pl.pallas_call(functools.partial(solve_kernel, scale=scale), out_shape=ja...  3.08 us
    pallas_call x1, Pallas kernels, stage(): pl.pallas_call(stage_kernel, in_specs=[vmem, hbm, hbm, hbm], out_shape=(j...  1.81 us
    pallas_call x1, Pallas kernels, prepare(): pl.pallas_call(functools.partial(prepare_kernel, first=first, width=width...  1.22 us
    ppermute x3, waiting for transfers between devices, swapped(): return lax.ppermute(block, axis, [(i, size - 1 - i) for i in range(size)])  1.2 us
  transfers between devices with their start and end apart: 9, of which 5 were waited for; matrix products, arithmetic and copies ran while one was open for 2% of the time, Pallas kernels for 17%

profile of v2, /device:TPU:0, one launch (start us, length us, event | category | flops | bytes accessed | tf_op | source)
XLA Modules:
  0.0 58.8 jit_solution(13891188230498029984)
XLA Ops:
  0.6 1.2 %prepare.1 = (bf16[64,2688]{1,0:T(8,128)(2,1)S(1)}, bf16[64,2688]{1,0:T(8,128)(2,1)S(1)}, bf16[64,128]{1,0:T(8,128)(2,1)S(1)}) custom-call(s32[3,32,128]{2,1,0:T(8,128)} %bitcast.21, s32[3,1,128]{2,1,0:T(1,128)} %bitcast.24, f32[3,32,128]{2,1,0:T(8,128)} %bitcast.22, f32[1,64]{1,0:T(1,128)} %absorber_hbm.1, bf16[64,4096]{1,0:T(8,128)(2,1)} %bitcast.16), custom_call_target="tpu_custom_call" | custom-call | flops 1 | bytes 1 | tf_op jit(solution)/shard_map/prepare/pallas_call | solution.py:78
  1.9 3.0 %collective-permute-start = (bf16[64,2688]{1,0:T(8,128)(2,1)S(1)}, bf16[64,2688]{1,0:T(8,128)(2,1)S(1)}, u32[]{:S(2)}, u32[]{:S(2)}) collective-permute-start(bf16[64,2688]{1,0:T(8,128)(2,1)S(1)} %get-tuple-element.22), channel_id=1, source_target_pairs={{14,0},{0,2},{2,4},{4,6},{6,8},{8,10},{10,12},{12,14},{15,1},{1,3}... | collective-permute-start | bytes 1032200 | tf_op jit(solution)/shard_map/ppermute | solution.py:25
  4.9 3.1 %collective-permute-start.1 = (bf16[64,2688]{1,0:T(8,128)(2,1)S(1)}, bf16[64,2688]{1,0:T(8,128)(2,1)S(1)}, u32[]{:S(2)}, u32[]{:S(2)}) collective-permute-start(bf16[64,2688]{1,0:T(8,128)(2,1)S(1)} %get-tuple-element.23), channel_id=1, source_target_pairs={{2,0},{4,2},{6,4},{8,6},{10,8},{12,10},{14,12},{0,14},{3,1},{5,3},... | collective-permute-start | bytes 1032200 | tf_op jit(solution)/shard_map/ppermute | solution.py:25
  8.0 0.9 %slice.8 = bf16[64,1536]{1,0:T(8,128)(2,1)S(1)} slice(bf16[64,4096]{1,0:T(8,128)(2,1)} %bitcast.17), slice={[0:64], [2560:4096]} | slice | bytes 393216 | tf_op jit(solution)/shard_map/slice | solution.py:389
  8.9 2.0 %collective-permute-start.3 = (bf16[64,1536]{1,0:T(8,128)(2,1)S(1)}, bf16[64,1536]{1,0:T(8,128)(2,1)S(1)}, u32[]{:S(2)}, u32[]{:S(2)}) collective-permute-start(bf16[64,1536]{1,0:T(8,128)(2,1)S(1)} %slice.8), channel_id=1, source_target_pairs={{2,0},{4,2},{6,4},{8,6},{10,8},{12,10},{14,12},{0,14},{3,1},{5,3},... | collective-permute-start | bytes 589832 | tf_op jit(solution)/shard_map/ppermute | solution.py:25
  10.9 0.1 collective-permute-start.2
  11.0 1.8 %stage.1 = (s32[32,128]{1,0:T(8,128)S(1)}, s32[40,128]{1,0:T(8,128)S(1)}, bf16[64,4096]{1,0:T(8,128)(2,1)S(1)}, f32[128,4096]{1,0:T(8,128)S(1)}) custom-call(bf16[64,128]{1,0:T(8,128)(2,1)S(1)} %get-tuple-element.17.cols_ref.refs_4_, s32[32,128]{1,0:T(8,128)} %bitcast.23, bf16[64,4096]{1,0:T(8,128)(2,1)} %bitcast.18, f32[128,4096]{1,0:T(8,128)} %bitcast.19), custom_call_target="tpu_custom_call" | custom-call | flops 1 | bytes 1 | tf_op jit(solution)/shard_map/stage/pallas_call | solution.py:121
  12.8 12.1 %collective-permute-done.refs_5_.refs_7_ = bf16[64,2688]{1,0:T(8,128)(2,1)S(1)} collective-permute-done((bf16[64,2688]{1,0:T(8,128)(2,1)S(1)}, bf16[64,2688]{1,0:T(8,128)(2,1)S(1)}, u32[]{:S(2)}, u32[]{:S(2)}) %collective-permute-start) | collective-permute-done | bytes 344096 | tf_op jit(solution)/shard_map/ppermute | solution.py:25
  24.9 2.5 %collective-permute-done.1.refs_6_.refs_8_ = bf16[64,2688]{1,0:T(8,128)(2,1)S(1)} collective-permute-done((bf16[64,2688]{1,0:T(8,128)(2,1)S(1)}, bf16[64,2688]{1,0:T(8,128)(2,1)S(1)}, u32[]{:S(2)}, u32[]{:S(2)}) %collective-permute-start.1) | collective-permute-done | bytes 344096 | tf_op jit(solution)/shard_map/ppermute | solution.py:25
  27.4 8.2 %chunk.2 = (f32[128,4096]{1,0:T(8,128)}, bf16[38,320,128]{2,1,0:T(8,128)(2,1)S(1)}, f32[3,2560,128]{2,1,0:T(8,128)S(1)}, f32[192,128]{1,0:T(8,128)S(1)}) custom-call(s32[40,1]{1,0:T(8,128)S(1)} %bitcast.13, s32[32,128]{1,0:T(8,128)S(1)} %get-tuple-element.19.refs_1_, bf16[64,4096]{1,0:T(8,128)(2,1)S(1)} %get-tuple-element.20.refs_2_, ...), custom_call_target="tpu_custom_call" | custom-call | flops 1 | bytes 1 | tf_op jit(solution)/shard_map/chunk/pallas_call | solution.py:284
  35.7 0.0 collective-permute-done.3.refs_8_
  35.7 0.0 collective-permute-done.2.refs_7_
  35.7 0.0 copy-start
  35.7 9.1 %chunk.3 = (f32[128,4096]{1,0:T(8,128)}, bf16[38,320,128]{2,1,0:T(8,128)(2,1)S(1)}, f32[3,2560,128]{2,1,0:T(8,128)S(1)}, f32[192,128]{1,0:T(8,128)S(1)}, f32[64,...) custom-call(s32[40,1]{1,0:T(8,128)S(1)} %bitcast.14, ...), custom_call_target="tpu_custom_call", output_to_operand_aliasing={{0}: (9, {}), {1}: (10, {}), {2}: (11, {}), {3}: (12, {})} | custom-call | flops 1 | bytes 1 | tf_op jit(solution)/shard_map/chunk/pallas_call | solution.py:284
  44.9 3.1 %collective-permute-start.4 = (f32[64,128]{1,0:T(8,128)S(1)}, f32[64,128]{1,0:T(8,128)S(1)}, u32[]{:S(2)}, u32[]{:S(2)}) collective-permute-start(f32[64,128]{1,0:T(8,128)S(1)} %get-tuple-element.30), channel_id=1, source_target_pairs={{2,0},{4,2},{6,4},{8,6},{10,8},{12,10},{14,12},{0,14},{3,1},{5,3},... | collective-permute-start | bytes 98312 | tf_op jit(solution)/shard_map/ppermute | solution.py:25
  47.9 0.0 collective-permute-start.5
  47.9 0.0 collective-permute-start.6
  47.9 1.6 %collective-permute-done.4.refs_1_ = f32[64,128]{1,0:T(8,128)S(1)} collective-permute-done((f32[64,128]{1,0:T(8,128)S(1)}, f32[64,128]{1,0:T(8,128)S(1)}, u32[]{:S(2)}, u32[]{:S(2)}) %collective-permute-start.4) | collective-permute-done | bytes 32800 | tf_op jit(solution)/shard_map/ppermute | solution.py:25
  49.5 0.0 collective-permute-start.7
  49.5 5.0 %collective-permute-done.5.refs_2_ = f32[64,128]{1,0:T(8,128)S(1)} collective-permute-done((f32[64,128]{1,0:T(8,128)S(1)}, f32[64,128]{1,0:T(8,128)S(1)}, u32[]{:S(2)}, u32[]{:S(2)}) %collective-permute-start.5) | collective-permute-done | bytes 32800 | tf_op jit(solution)/shard_map/ppermute | solution.py:25
  54.5 0.0 collective-permute-start.8
  54.5 0.0 collective-permute-done.6.refs_3_
  54.5 1.2 %collective-permute-done.8.refs_5_ = f32[64,128]{1,0:T(8,128)S(1)} collective-permute-done((f32[64,128]{1,0:T(8,128)S(1)}, f32[64,128]{1,0:T(8,128)S(1)}, u32[]{:S(2)}, u32[]{:S(2)}) %collective-permute-start.8) | collective-permute-done | bytes 32800 | tf_op jit(solution)/shard_map/ppermute | solution.py:369
  55.7 3.1 %solve.1 = f32[1,64]{1,0:T(1,128)} custom-call(f32[64,128]{1,0:T(8,128)S(1)} %get-tuple-element.29.refs_0_, f32[64,128]{1,0:T(8,128)S(1)} %collective-permute-done.4.refs_1_, f32[64,128]{1,0:T(8,128)S(1)} %collective-permute-done.5.refs_2_, f32[64,128]{1,0:T(8,128)S(1)} %collective-permute-done.6.refs_3_, f32[64,128]{1,0:T(8,128)S(1)} %collective-permute-done.7.refs_4_, ...), custom_call_target="tpu_custom_call" | custom-call | flops 1 | bytes 1 | tf_op jit(solution)/shard_map/solve/pallas_call | solution.py:358
  (2 shorter events, 0.0 us)
Async XLA Ops:
  1.9 23.1 %collective-permute-start = (bf16[64,2688]{1,0:T(8,128)(2,1)S(1)}, bf16[64,2688]{1,0:T(8,128)(2,1)S(1)}, u32[]{:S(2)}, u32[]{:S(2)}) collective-permute-start(bf16[64,2688]{1,0:T(8,128)(2,1)S(1)} %get-tuple-element.22), channel_id=1, source_target_pairs={{14,0},{0,2},{2,4},{4,6},{6,8},{8,10},{10,12},{12,14},{15,1},{1,3}... | collective-permute-start | bytes 1032200 | tf_op jit(solution)/shard_map/ppermute | solution.py:25
  4.9 22.6 %collective-permute-start.1 = (bf16[64,2688]{1,0:T(8,128)(2,1)S(1)}, bf16[64,2688]{1,0:T(8,128)(2,1)S(1)}, u32[]{:S(2)}, u32[]{:S(2)}) collective-permute-start(bf16[64,2688]{1,0:T(8,128)(2,1)S(1)} %get-tuple-element.23), channel_id=1, source_target_pairs={{2,0},{4,2},{6,4},{8,6},{10,8},{12,10},{14,12},{0,14},{3,1},{5,3},... | collective-permute-start | bytes 1032200 | tf_op jit(solution)/shard_map/ppermute | solution.py:25
  8.9 26.8 %collective-permute-start.3 = (bf16[64,1536]{1,0:T(8,128)(2,1)S(1)}, bf16[64,1536]{1,0:T(8,128)(2,1)S(1)}, u32[]{:S(2)}, u32[]{:S(2)}) collective-permute-start(bf16[64,1536]{1,0:T(8,128)(2,1)S(1)} %slice.8), channel_id=1, source_target_pairs={{2,0},{4,2},{6,4},{8,6},{10,8},{12,10},{14,12},{0,14},{3,1},{5,3},... | collective-permute-start | bytes 589832 | tf_op jit(solution)/shard_map/ppermute | solution.py:25
  10.9 24.8 %collective-permute-start.2 = (bf16[64,1536]{1,0:T(8,128)(2,1)S(1)}, bf16[64,1536]{1,0:T(8,128)(2,1)S(1)}, u32[]{:S(2)}, u32[]{:S(2)}) collective-permute-start(bf16[64,1536]{1,0:T(8,128)(2,1)S(1)} %slice.8), channel_id=1, source_target_pairs={{14,0},{0,2},{2,4},{4,6},{6,8},{8,10},{10,12},{12,14},{15,1},{1,3}... | collective-permute-start | bytes 589832 | tf_op jit(solution)/shard_map/ppermute | solution.py:25
  35.7 20.0 %copy-start = (f32[64]{0:T(128)S(1)}, f32[64]{0:T(128)}, u32[]{:S(2)}) copy-start(f32[64]{0:T(128)} %param.15) | copy-start | bytes 772
  44.9 4.7 %collective-permute-start.4 = (f32[64,128]{1,0:T(8,128)S(1)}, f32[64,128]{1,0:T(8,128)S(1)}, u32[]{:S(2)}, u32[]{:S(2)}) collective-permute-start(f32[64,128]{1,0:T(8,128)S(1)} %get-tuple-element.30), channel_id=1, source_target_pairs={{2,0},{4,2},{6,4},{8,6},{10,8},{12,10},{14,12},{0,14},{3,1},{5,3},... | collective-permute-start | bytes 98312 | tf_op jit(solution)/shard_map/ppermute | solution.py:25
  47.9 6.6 %collective-permute-start.5 = (f32[64,128]{1,0:T(8,128)S(1)}, f32[64,128]{1,0:T(8,128)S(1)}, u32[]{:S(2)}, u32[]{:S(2)}) collective-permute-start(f32[64,128]{1,0:T(8,128)S(1)} %get-tuple-element.31), channel_id=1, source_target_pairs={{14,0},{0,2},{2,4},{4,6},{6,8},{8,10},{10,12},{12,14},{15,1},{1,3}... | collective-permute-start | bytes 98312 | tf_op jit(solution)/shard_map/ppermute | solution.py:25
  47.9 6.6 %collective-permute-start.6 = (f32[64,128]{1,0:T(8,128)S(1)}, f32[64,128]{1,0:T(8,128)S(1)}, u32[]{:S(2)}, u32[]{:S(2)}) collective-permute-start(f32[64,128]{1,0:T(8,128)S(1)} %get-tuple-element.29.refs_0_), channel_id=1, source_target_pairs={{0,1},{1,0},{2,3},{3,2},{4,5},{5,4},{6,7},{7,6},{8,9},{9,8},{10,11... | collective-permute-start | bytes 98312 | tf_op jit(solution)/shard_map/ppermute | solution.py:369
  49.5 5.0 %collective-permute-start.7 = (f32[64,128]{1,0:T(8,128)S(1)}, f32[64,128]{1,0:T(8,128)S(1)}, u32[]{:S(2)}, u32[]{:S(2)}) collective-permute-start(f32[64,128]{1,0:T(8,128)S(1)} %collective-permute-done.4.refs_1_), channel_id=1, source_target_pairs={{0,1},{1,0},{2,3},{3,2},{4,5},{5,4},{6,7},{7,6},{8,9},{9,8},{10,11... | collective-permute-start | bytes 98312 | tf_op jit(solution)/shard_map/ppermute | solution.py:369
  54.5 1.2 %collective-permute-start.8 = (f32[64,128]{1,0:T(8,128)S(1)}, f32[64,128]{1,0:T(8,128)S(1)}, u32[]{:S(2)}, u32[]{:S(2)}) collective-permute-start(f32[64,128]{1,0:T(8,128)S(1)} %collective-permute-done.5.refs_2_), channel_id=1, source_target_pairs={{0,1},{1,0},{2,3},{3,2},{4,5},{5,4},{6,7},{7,6},{8,9},{9,8},{10,11... | collective-permute-start | bytes 98312 | tf_op jit(solution)/shard_map/ppermute | solution.py:369

commit v3 on v2

--- a/solution.py
+++ b/solution.py
@@ -11,18 +11,18 @@
 ROWS = 16
 PIECE = 512
 BLOCK = 512
-WIDTHS = (20, 12)
-GROUPS = ((0,), (1,))
+WIDTHS = (14, 12, 6)
+GROUPS = ((0,), (1,), (2,))
 CARRIER = 0
 SMALL_BYTES = 4 << 20
 CHUNK_BYTES = 16 << 20
 CHEAP = pl.CostEstimate(flops=1, transcendentals=0, bytes_accessed=1)
 
 
-def passed_along(block, axis, distance):
-    devices = range(lax.axis_size(axis))
-    route = [((i - distance) % len(devices), i) for i in devices]
-    return lax.ppermute(block, axis, route)
+def traded(block, axis, side):
+    size = lax.axis_size(axis)
+    steps = [1 if (i + side) % 2 == 0 else -1 for i in range(size)]
+    return lax.ppermute(block, axis, [(i, (i + step) % size) for i, step in enumerate(steps)])
 
 
 def iota(shape, dim):
@@ -38,12 +38,12 @@
 
 
 def prepare_kernel(level_hbm, count_hbm, length_hbm, absorber_hbm, table_hbm, *outs, first, width):
-    up_ref, down_ref, cols_ref, level_ref, count_ref, length_ref, absorber_ref, sems = outs
+    first_ref, second_ref, cols_ref, level_ref, count_ref, length_ref, absorber_ref, sems = outs
     levels = absorber_ref.shape[1]
     sets, segs, rays = level_ref.shape
     arguments = ((level_hbm, level_ref), (length_hbm, length_ref), (count_hbm, count_ref), (absorber_hbm, absorber_ref))
     copies = [pltpu.make_async_copy(a, b, sems.at[n]) for n, (a, b) in enumerate(arguments)]
-    for n, ref in enumerate((up_ref, down_ref)):
+    for n, ref in enumerate((first_ref, second_ref)):
         source = table_hbm.at[:, pl.ds(first, width)]
         copies.append(pltpu.make_async_copy(source, ref.at[:, pl.ds(0, width)], sems.at[len(arguments) + n]))
     for copy in copies:
@@ -53,19 +53,19 @@
     eye = iota((levels, levels), 0) == iota((levels, levels), 1)
     amount = jnp.sum(jnp.where(eye, absorber_ref[...], 0.0), axis=1, keepdims=True)
     level_of = iota((levels, rays), 0)
+    odd = lax.axis_index("sector") % 2
+    absorbed = []
     for k in range(sets):
         length = jnp.where(iota((segs, rays), 0) < count_ref[k], length_ref[k], 0.0)
         level = level_ref[k]
         path = jnp.zeros((levels, rays), jnp.float32)
         for j in range(segs):
             path += jnp.where(level[j : j + 1, :] == level_of, length[j : j + 1, :], 0.0)
-        absorbed = (path * amount).astype(jnp.bfloat16)
-        if k == 0:
-            down_ref[:, width:] = absorbed
-        elif k == 1:
-            cols_ref[...] = absorbed
-        else:
-            up_ref[:, width:] = absorbed
+        absorbed.append(path * amount)
+    low, here, high = absorbed
+    cols_ref[...] = here.astype(jnp.bfloat16)
+    first_ref[:, width:] = jnp.where(odd == 1, low, high).astype(jnp.bfloat16)
+    second_ref[:, width:] = jnp.where(odd == 1, high, low).astype(jnp.bfloat16)
     for copy in copies[len(arguments) :]:
         copy.wait()
 
@@ -380,26 +380,26 @@
     level = jnp.swapaxes(seg_level[0], 1, 2)
     length = jnp.swapaxes(seg_length[0], 1, 2)
     count = seg_count.reshape(3, 1, rays)
-    upward, downward, cols = prepare(level, count, length, absorber, table, firsts[CARRIER], widths[CARRIER])
+    first_send, second_send, cols = prepare(level, count, length, absorber, table, firsts[CARRIER], widths[CARRIER])
     place, base, table_here, measured_here = stage(cols, mask, table, measured[0])
     base = base[:, :1]
-    below = []
-    above = []
+    first_tables = []
+    second_tables = []
     for c, (first, width) in enumerate(zip(firsts, widths, strict=True)):
         piece = table[:, first : first + width]
-        below.append(passed_along(upward if c == CARRIER else piece, "sector", 1))
-        above.append(passed_along(downward if c == CARRIER else piece, "sector", -1))
+        first_tables.append(traded(first_send if c == CARRIER else piece, "sector", 0))
+        second_tables.append(traded(second_send if c == CARRIER else piece, "sector", 1))
     state = None
-    carried = (below[CARRIER], above[CARRIER])
+    carried = (first_tables[CARRIER], second_tables[CARRIER])
     for n, group in enumerate(GROUPS):
         spans_of = tuple((firsts[c], widths[c]) for c in group)
-        sources = [(below[c], above[c]) for c in group]
+        sources = [(first_tables[c], second_tables[c]) for c in group]
         closes = n == len(GROUPS) - 1
         state, terms = chunk(
             base, place, table_here, measured_here, cols, carried, widths[CARRIER], spans_of, sources, state, closes
         )
     spectrum = state[0]
-    mine = (terms[1], passed_along(terms[0], "sector", -1), passed_along(terms[2], "sector", 1))
+    mine = (terms[1], traded(terms[0], "sector", 0), traded(terms[2], "sector", 1))
     others = tuple(swapped(part, "spec") for part in mine)
     scale = 1.0 / (rays * points * lax.axis_size("spec"))
     state_step = solve(mine + others, prior_weight[None, :], scale)

time: 59.7 us -> 58.9 us (0.987)
  waiting for transfers between devices: 22.4 us -> 15.6 us
  starting transfers between devices: 11.3 us -> 15 us
  Pallas kernels: 23.5 us -> 24.8 us
  local copies, waits for them, and re-layouts: 0.95 us -> 1.84 us
    ppermute x6 -> x8, waiting for transfers between devices: 21.2 us -> 14.7 us  [traded(): lax.ppermute(block, axis, [(i, (i + step) % size) for i, step in enumerat...]
    ppermute x6 -> x8, starting transfers between devices: 11.3 us -> 14.4 us  [traded(): lax.ppermute(block, axis, [(i, (i + step) % size) for i, step in enumerat...]
    pallas_call x2 -> x3, Pallas kernels: 17.4 us -> 18.7 us  [chunk(): pl.pallas_call(functools.partial(chunk_kernel, spans_of=spans_of, carrier...]
    slice x1 -> x2, local copies, waits for them, and re-layouts: 0.94 us -> 1.84 us  [shards(): piece = table[:, first:first + width]]
  transfers between devices with their start and end apart: 9 -> 11, of which waited for: 5 -> 4; matrix products, arithmetic and copies ran while one was open for 2% -> 3% of each run, Pallas kernels for 17% -> 24%
where the time goes in v3:
time: 58.9 us; the launch traced here: 58 us
  Pallas kernels  24.8 us (42%)
  waiting for transfers between devices  15.6 us (26%)
  starting transfers between devices  15 us (25%)
  local copies, waits for them, and re-layouts  1.84 us (3%)
  between operations  0.76 us (1%)
    pallas_call x3, Pallas kernels, chunk(): pl.pallas_call(functools.partial(chunk_kernel, spans_of=spans_of, carrier...  18.7 us
    ppermute x8, waiting for transfers between devices, traded(): lax.ppermute(block, axis, [(i, (i + step) % size) for i, step in enumerat...  14.7 us
    ppermute x8, starting transfers between devices, traded(): lax.ppermute(block, axis, [(i, (i + step) % size) for i, step in enumerat...  14.4 us
    pallas_call x1, Pallas kernels, solve(): pl.pallas_call(functools.partial(solve_kernel, scale=scale), out_shape=ja...  3.08 us
    slice x2, local copies, waits for them, and re-layouts, shards(): piece = table[:, first:first + width]  1.84 us
    pallas_call x1, Pallas kernels, stage(): pl.pallas_call(stage_kernel, in_specs=[vmem, hbm, hbm, hbm], out_shape=(j...  1.81 us
    pallas_call x1, Pallas kernels, prepare(): pl.pallas_call(functools.partial(prepare_kernel, first=first, width=width...  1.25 us
  transfers between devices with their start and end apart: 11, of which 4 were waited for; matrix products, arithmetic and copies ran while one was open for 3% of the time, Pallas kernels for 24%

profile of v3, /device:TPU:0, one launch (start us, length us, event | category | flops | bytes accessed | tf_op | source)
XLA Modules:
  0.0 58.0 jit_solution(8691052749624264137)
XLA Ops:
  0.6 1.2 %prepare.1 = (bf16[64,1920]{1,0:T(8,128)(2,1)S(1)}, bf16[64,1920]{1,0:T(8,128)(2,1)S(1)}, bf16[64,128]{1,0:T(8,128)(2,1)S(1)}) custom-call(s32[3,32,128]{2,1,0:T(8,128)} %bitcast.23, s32[3,1,128]{2,1,0:T(1,128)} %bitcast.26, f32[3,32,128]{2,1,0:T(8,128)} %bitcast.24, f32[1,64]{1,0:T(1,128)} %absorber_hbm.1, bf16[64,4096]{1,0:T(8,128)(2,1)} %bitcast.18), custom_call_target="tpu_custom_call" | custom-call | flops 1 | bytes 1 | tf_op jit(solution)/shard_map/prepare/pallas_call | solution.py:78
  1.9 3.0 %collective-permute-start = (bf16[64,1920]{1,0:T(8,128)(2,1)S(1)}, bf16[64,1920]{1,0:T(8,128)(2,1)S(1)}, u32[]{:S(2)}, u32[]{:S(2)}) collective-permute-start(bf16[64,1920]{1,0:T(8,128)(2,1)S(1)} %get-tuple-element.26), channel_id=1, source_target_pairs={{0,2},{2,0},{4,6},{6,4},{8,10},{10,8},{12,14},{14,12},{1,3},{3,1},... | collective-permute-start | bytes 737288 | tf_op jit(solution)/shard_map/ppermute | solution.py:25
  4.9 3.5 %collective-permute-start.1 = (bf16[64,1920]{1,0:T(8,128)(2,1)S(1)}, bf16[64,1920]{1,0:T(8,128)(2,1)S(1)}, u32[]{:S(2)}, u32[]{:S(2)}) collective-permute-start(bf16[64,1920]{1,0:T(8,128)(2,1)S(1)} %get-tuple-element.27), channel_id=1, source_target_pairs={{0,14},{2,4},{4,2},{6,8},{8,6},{10,12},{12,10},{14,0},{1,15},{3,5}... | collective-permute-start | bytes 737288 | tf_op jit(solution)/shard_map/ppermute | solution.py:25
  8.5 0.9 %slice.13 = bf16[64,1536]{1,0:T(8,128)(2,1)S(1)} slice(bf16[64,4096]{1,0:T(8,128)(2,1)} %bitcast.19), slice={[0:64], [1792:3328]} | slice | bytes 393216 | tf_op jit(solution)/shard_map/slice | solution.py:389
  9.4 0.1 collective-permute-start.4
  9.5 1.9 %collective-permute-start.5 = (bf16[64,1536]{1,0:T(8,128)(2,1)S(1)}, bf16[64,1536]{1,0:T(8,128)(2,1)S(1)}, u32[]{:S(2)}, u32[]{:S(2)}) collective-permute-start(bf16[64,1536]{1,0:T(8,128)(2,1)S(1)} %slice.13), channel_id=1, source_target_pairs={{0,14},{2,4},{4,2},{6,8},{8,6},{10,12},{12,10},{14,0},{1,15},{3,5}... | collective-permute-start | bytes 589832 | tf_op jit(solution)/shard_map/ppermute | solution.py:25
  11.4 0.9 %slice.12 = bf16[64,768]{1,0:T(8,128)(2,1)S(1)} slice(bf16[64,4096]{1,0:T(8,128)(2,1)} %bitcast.20), slice={[0:64], [3328:4096]} | slice | bytes 196608 | tf_op jit(solution)/shard_map/slice | solution.py:389
  12.3 0.6 %collective-permute-start.2 = (bf16[64,768]{1,0:T(8,128)(2,1)S(1)}, bf16[64,768]{1,0:T(8,128)(2,1)S(1)}, u32[]{:S(2)}, u32[]{:S(2)}) collective-permute-start(bf16[64,768]{1,0:T(8,128)(2,1)S(1)} %slice.12), channel_id=1, source_target_pairs={{0,2},{2,0},{4,6},{6,4},{8,10},{10,8},{12,14},{14,12},{1,3},{3,1},... | collective-permute-start | bytes 294920 | tf_op jit(solution)/shard_map/ppermute | solution.py:25
  12.9 8.3 %collective-permute-done.refs_5_.refs_7_ = bf16[64,1920]{1,0:T(8,128)(2,1)S(1)} collective-permute-done((bf16[64,1920]{1,0:T(8,128)(2,1)S(1)}, bf16[64,1920]{1,0:T(8,128)(2,1)S(1)}, u32[]{:S(2)}, u32[]{:S(2)}) %collective-permute-start) | collective-permute-done | bytes 245792 | tf_op jit(solution)/shard_map/ppermute | solution.py:25
  21.2 5.1 %collective-permute-start.3 = (bf16[64,768]{1,0:T(8,128)(2,1)S(1)}, bf16[64,768]{1,0:T(8,128)(2,1)S(1)}, u32[]{:S(2)}, u32[]{:S(2)}) collective-permute-start(bf16[64,768]{1,0:T(8,128)(2,1)S(1)} %slice.12), channel_id=1, source_target_pairs={{0,14},{2,4},{4,2},{6,8},{8,6},{10,12},{12,10},{14,0},{1,15},{3,5}... | collective-permute-start | bytes 294920 | tf_op jit(solution)/shard_map/ppermute | solution.py:25
  26.3 1.8 %stage.1 = (s32[32,128]{1,0:T(8,128)S(1)}, s32[40,128]{1,0:T(8,128)S(1)}, bf16[64,4096]{1,0:T(8,128)(2,1)S(1)}, f32[128,4096]{1,0:T(8,128)S(1)}) custom-call(bf16[64,128]{1,0:T(8,128)(2,1)S(1)} %get-tuple-element.21.cols_ref.refs_4_, s32[32,128]{1,0:T(8,128)} %bitcast.25, bf16[64,4096]{1,0:T(8,128)(2,1)} %bitcast.21, f32[128,4096]{1,0:T(8,128)} %bitcast.22), custom_call_target="tpu_custom_call" | custom-call | flops 1 | bytes 1 | tf_op jit(solution)/shard_map/stage/pallas_call | solution.py:121
  28.1 5.2 %chunk.3 = (f32[128,4096]{1,0:T(8,128)}, bf16[38,320,128]{2,1,0:T(8,128)(2,1)S(1)}, f32[3,2560,128]{2,1,0:T(8,128)S(1)}, f32[192,128]{1,0:T(8,128)S(1)}) custom-call(s32[40,1]{1,0:T(8,128)S(1)} %bitcast.13, s32[32,128]{1,0:T(8,128)S(1)} %get-tuple-element.23.refs_1_, bf16[64,4096]{1,0:T(8,128)(2,1)S(1)} %get-tuple-element.24.refs_2_, ...), custom_call_target="tpu_custom_call" | custom-call | flops 1 | bytes 1 | tf_op jit(solution)/shard_map/chunk/pallas_call | solution.py:284
  33.4 0.0 collective-permute-done.5.refs_8_
  33.4 7.2 %chunk.4 = (f32[128,4096]{1,0:T(8,128)}, bf16[38,320,128]{2,1,0:T(8,128)(2,1)S(1)}, f32[3,2560,128]{2,1,0:T(8,128)S(1)}, f32[192,128]{1,0:T(8,128)S(1)}) custom-call(s32[40,1]{1,0:T(8,128)S(1)} %bitcast.14, s32[32,128]{1,0:T(8,128)S(1)} %get-tuple-element.23.refs_1_, ...), custom_call_target="tpu_custom_call", output_to_operand_aliasing={{0}: (9, {}), {1}: (10, {}), {2}: (11, {}), {3}: (12, {})} | custom-call | flops 1 | bytes 1 | tf_op jit(solution)/shard_map/chunk/pallas_call | solution.py:284
  40.6 0.0 copy-start
  40.6 6.3 %chunk.5 = (f32[128,4096]{1,0:T(8,128)}, bf16[38,320,128]{2,1,0:T(8,128)(2,1)S(1)}, f32[3,2560,128]{2,1,0:T(8,128)S(1)}, f32[192,128]{1,0:T(8,128)S(1)}, f32[64,...) custom-call(s32[40,1]{1,0:T(8,128)S(1)} %bitcast.15, ...), custom_call_target="tpu_custom_call", output_to_operand_aliasing={{0}: (9, {}), {1}: (10, {}), {2}: (11, {}), {3}: (12, {})} | custom-call | flops 1 | bytes 1 | tf_op jit(solution)/shard_map/chunk/pallas_call | solution.py:284
  46.8 0.1 collective-permute-start.7
  46.9 0.1 collective-permute-start.6
  47.0 0.1 collective-permute-start.8
  47.1 6.4 %collective-permute-done.7.refs_2_ = f32[64,128]{1,0:T(8,128)S(1)} collective-permute-done((f32[64,128]{1,0:T(8,128)S(1)}, f32[64,128]{1,0:T(8,128)S(1)}, u32[]{:S(2)}, u32[]{:S(2)}) %collective-permute-start.7) | collective-permute-done | bytes 32800 | tf_op jit(solution)/shard_map/ppermute | solution.py:25
  53.5 0.5 collective-permute-start.9
  54.0 0.7 %collective-permute-done.10.refs_5_ = f32[64,128]{1,0:T(8,128)S(1)} collective-permute-done((f32[64,128]{1,0:T(8,128)S(1)}, f32[64,128]{1,0:T(8,128)S(1)}, u32[]{:S(2)}, u32[]{:S(2)}) %collective-permute-start.10) | collective-permute-done | bytes 32800 | tf_op jit(solution)/shard_map/ppermute | solution.py:369
  54.7 0.2 collective-permute-done.9.refs_4_
  54.9 3.1 %solve.1 = f32[1,64]{1,0:T(1,128)} custom-call(f32[64,128]{1,0:T(8,128)S(1)} %get-tuple-element.37.refs_0_, f32[64,128]{1,0:T(8,128)S(1)} %collective-permute-done.6.refs_1_, f32[64,128]{1,0:T(8,128)S(1)} %collective-permute-done.7.refs_2_, f32[64,128]{1,0:T(8,128)S(1)} %collective-permute-done.8.refs_3_, f32[64,128]{1,0:T(8,128)S(1)} %collective-permute-done.9.refs_4_, ...), custom_call_target="tpu_custom_call" | custom-call | flops 1 | bytes 1 | tf_op jit(solution)/shard_map/solve/pallas_call | solution.py:358
  (8 shorter events, 0.0 us)
Async XLA Ops:
  1.9 19.3 %collective-permute-start = (bf16[64,1920]{1,0:T(8,128)(2,1)S(1)}, bf16[64,1920]{1,0:T(8,128)(2,1)S(1)}, u32[]{:S(2)}, u32[]{:S(2)}) collective-permute-start(bf16[64,1920]{1,0:T(8,128)(2,1)S(1)} %get-tuple-element.26), channel_id=1, source_target_pairs={{0,2},{2,0},{4,6},{6,4},{8,10},{10,8},{12,14},{14,12},{1,3},{3,1},... | collective-permute-start | bytes 737288 | tf_op jit(solution)/shard_map/ppermute | solution.py:25
  4.9 23.2 %collective-permute-start.1 = (bf16[64,1920]{1,0:T(8,128)(2,1)S(1)}, bf16[64,1920]{1,0:T(8,128)(2,1)S(1)}, u32[]{:S(2)}, u32[]{:S(2)}) collective-permute-start(bf16[64,1920]{1,0:T(8,128)(2,1)S(1)} %get-tuple-element.27), channel_id=1, source_target_pairs={{0,14},{2,4},{4,2},{6,8},{8,6},{10,12},{12,10},{14,0},{1,15},{3,5}... | collective-permute-start | bytes 737288 | tf_op jit(solution)/shard_map/ppermute | solution.py:25
  9.4 23.9 %collective-permute-start.4 = (bf16[64,1536]{1,0:T(8,128)(2,1)S(1)}, bf16[64,1536]{1,0:T(8,128)(2,1)S(1)}, u32[]{:S(2)}, u32[]{:S(2)}) collective-permute-start(bf16[64,1536]{1,0:T(8,128)(2,1)S(1)} %slice.13), channel_id=1, source_target_pairs={{0,2},{2,0},{4,6},{6,4},{8,10},{10,8},{12,14},{14,12},{1,3},{3,1},... | collective-permute-start | bytes 589832 | tf_op jit(solution)/shard_map/ppermute | solution.py:25
  9.5 23.9 %collective-permute-start.5 = (bf16[64,1536]{1,0:T(8,128)(2,1)S(1)}, bf16[64,1536]{1,0:T(8,128)(2,1)S(1)}, u32[]{:S(2)}, u32[]{:S(2)}) collective-permute-start(bf16[64,1536]{1,0:T(8,128)(2,1)S(1)} %slice.13), channel_id=1, source_target_pairs={{0,14},{2,4},{4,2},{6,8},{8,6},{10,12},{12,10},{14,0},{1,15},{3,5}... | collective-permute-start | bytes 589832 | tf_op jit(solution)/shard_map/ppermute | solution.py:25
  12.3 28.3 %collective-permute-start.2 = (bf16[64,768]{1,0:T(8,128)(2,1)S(1)}, bf16[64,768]{1,0:T(8,128)(2,1)S(1)}, u32[]{:S(2)}, u32[]{:S(2)}) collective-permute-start(bf16[64,768]{1,0:T(8,128)(2,1)S(1)} %slice.12), channel_id=1, source_target_pairs={{0,2},{2,0},{4,6},{6,4},{8,10},{10,8},{12,14},{14,12},{1,3},{3,1},... | collective-permute-start | bytes 294920 | tf_op jit(solution)/shard_map/ppermute | solution.py:25
  21.2 19.4 %collective-permute-start.3 = (bf16[64,768]{1,0:T(8,128)(2,1)S(1)}, bf16[64,768]{1,0:T(8,128)(2,1)S(1)}, u32[]{:S(2)}, u32[]{:S(2)}) collective-permute-start(bf16[64,768]{1,0:T(8,128)(2,1)S(1)} %slice.12), channel_id=1, source_target_pairs={{0,14},{2,4},{4,2},{6,8},{8,6},{10,12},{12,10},{14,0},{1,15},{3,5}... | collective-permute-start | bytes 294920 | tf_op jit(solution)/shard_map/ppermute | solution.py:25
  40.6 14.3 %copy-start = (f32[64]{0:T(128)S(1)}, f32[64]{0:T(128)}, u32[]{:S(2)}) copy-start(f32[64]{0:T(128)} %param.15) | copy-start | bytes 772
  46.8 6.7 %collective-permute-start.7 = (f32[64,128]{1,0:T(8,128)S(1)}, f32[64,128]{1,0:T(8,128)S(1)}, u32[]{:S(2)}, u32[]{:S(2)}) collective-permute-start(f32[64,128]{1,0:T(8,128)S(1)} %get-tuple-element.39), channel_id=1, source_target_pairs={{0,14},{2,4},{4,2},{6,8},{8,6},{10,12},{12,10},{14,0},{1,15},{3,5}... | collective-permute-start | bytes 98312 | tf_op jit(solution)/shard_map/ppermute | solution.py:25
  46.9 6.6 %collective-permute-start.6 = (f32[64,128]{1,0:T(8,128)S(1)}, f32[64,128]{1,0:T(8,128)S(1)}, u32[]{:S(2)}, u32[]{:S(2)}) collective-permute-start(f32[64,128]{1,0:T(8,128)S(1)} %get-tuple-element.38), channel_id=1, source_target_pairs={{0,2},{2,0},{4,6},{6,4},{8,10},{10,8},{12,14},{14,12},{1,3},{3,1},... | collective-permute-start | bytes 98312 | tf_op jit(solution)/shard_map/ppermute | solution.py:25
  47.0 7.0 %collective-permute-start.8 = (f32[64,128]{1,0:T(8,128)S(1)}, f32[64,128]{1,0:T(8,128)S(1)}, u32[]{:S(2)}, u32[]{:S(2)}) collective-permute-start(f32[64,128]{1,0:T(8,128)S(1)} %get-tuple-element.37.refs_0_), channel_id=1, source_target_pairs={{0,1},{1,0},{2,3},{3,2},{4,5},{5,4},{6,7},{7,6},{8,9},{9,8},{10,11... | collective-permute-start | bytes 98312 | tf_op jit(solution)/shard_map/ppermute | solution.py:369
  53.5 1.2 %collective-permute-start.10 = (f32[64,128]{1,0:T(8,128)S(1)}, f32[64,128]{1,0:T(8,128)S(1)}, u32[]{:S(2)}, u32[]{:S(2)}) collective-permute-start(f32[64,128]{1,0:T(8,128)S(1)} %collective-permute-done.7.refs_2_), channel_id=1, source_target_pairs={{0,1},{1,0},{2,3},{3,2},{4,5},{5,4},{6,7},{7,6},{8,9},{9,8},{10,11... | collective-permute-start | bytes 98312 | tf_op jit(solution)/shard_map/ppermute | solution.py:369
  53.5 1.4 %collective-permute-start.9 = (f32[64,128]{1,0:T(8,128)S(1)}, f32[64,128]{1,0:T(8,128)S(1)}, u32[]{:S(2)}, u32[]{:S(2)}) collective-permute-start(f32[64,128]{1,0:T(8,128)S(1)} %collective-permute-done.6.refs_1_), channel_id=1, source_target_pairs={{0,1},{1,0},{2,3},{3,2},{4,5},{5,4},{6,7},{7,6},{8,9},{9,8},{10,11... | collective-permute-start | bytes 98312 | tf_op jit(solution)/shard_map/ppermute | solution.py:369

commit v4 on v3

--- a/solution.py
+++ b/solution.py
@@ -11,9 +11,7 @@
 ROWS = 16
 PIECE = 512
 BLOCK = 512
-WIDTHS = (14, 12, 6)
-GROUPS = ((0,), (1,), (2,))
-CARRIER = 0
+WIDTHS = (12, 14, 6)
 SMALL_BYTES = 4 << 20
 CHUNK_BYTES = 16 << 20
 CHEAP = pl.CostEstimate(flops=1, transcendentals=0, bytes_accessed=1)
@@ -92,9 +90,10 @@
     )(*pinned(level, count, length, absorber, table))
 
 
-def stage_kernel(cols_ref, mask_hbm, table_hbm, measured_hbm, place_ref, base_ref, table_ref, measured_ref, mask_ref, sems):
+def stage_kernel(cols_ref, mask_hbm, table_hbm, measured_hbm, place_ref, base_ref, table_ref, measured_ref, send_ref, mask_ref, sems, *, first):
     del cols_ref
-    moves = ((mask_hbm, mask_ref), (table_hbm, table_ref), (measured_hbm, measured_ref))
+    part = table_hbm.at[:, pl.ds(first, send_ref.shape[1])]
+    moves = ((mask_hbm, mask_ref), (part, send_ref), (table_hbm, table_ref), (measured_hbm, measured_ref))
     copies = [pltpu.make_async_copy(a, b, sems.at[n]) for n, (a, b) in enumerate(moves)]
     for copy in copies:
         copy.start()
@@ -114,20 +113,21 @@
         copy.wait()
 
 
-def stage(cols, mask, table, measured):
+def stage(cols, mask, table, measured, first, width):
     groups = mask.shape[0]
     vmem = pl.BlockSpec(memory_space=pltpu.VMEM)
     hbm = pl.BlockSpec(memory_space=pltpu.HBM)
     return pl.pallas_call(
-        stage_kernel,
+        functools.partial(stage_kernel, first=first),
         in_specs=[vmem, hbm, hbm, hbm],
         out_shape=(
             jax.ShapeDtypeStruct((groups, LANES), jnp.int32),
             jax.ShapeDtypeStruct((groups + 8, LANES), jnp.int32),
             jax.ShapeDtypeStruct(table.shape, table.dtype),
             jax.ShapeDtypeStruct(measured.shape, measured.dtype),
+            jax.ShapeDtypeStruct((table.shape[0], width), table.dtype),
         ),
-        scratch_shapes=[pltpu.VMEM(mask.shape, mask.dtype), pltpu.SemaphoreType.DMA((3,))],
+        scratch_shapes=[pltpu.VMEM(mask.shape, mask.dtype), pltpu.SemaphoreType.DMA((4,))],
         compiler_params=pltpu.CompilerParams(vmem_limit_bytes=SMALL_BYTES),
         cost_estimate=CHEAP,
         name="stage",
@@ -144,7 +144,7 @@
     return spans, offset
 
 
-def chunk_kernel(*refs, spans_of, carrier, opens, closes):
+def chunk_kernel(*refs, spans_of, carrier, opens, closes, onward):
     base_ref, place_ref, here_ref, measured_ref, cols_ref, carried_before, carried_after = refs[:7]
     refs = refs[7:]
     sources = []
@@ -158,6 +158,9 @@
     if closes:
         terms_refs = refs[:3]
         refs = refs[3:]
+    if onward:
+        refs[0][...] = here_ref[:, onward[0] : onward[0] + onward[1]]
+        refs = refs[1:]
     table, modelled, pairs, weights, sems = refs
     levels = here_ref.shape[0]
     rays = measured_ref.shape[0]
@@ -252,7 +255,7 @@
         copy.wait()
 
 
-def chunk(base, place, here, measured, cols, carried, carrier, spans_of, sources, state, closes):
+def chunk(base, place, here, measured, cols, carried, carrier, spans_of, sources, state, closes, onward):
     levels, points = here.shape
     rays = measured.shape[0]
     _, pair_count = pair_rows(levels)
@@ -281,8 +284,11 @@
     if closes:
         shapes += [jax.ShapeDtypeStruct((levels, LANES), jnp.float32)] * 3
         out_specs += [vmem] * 3
+    if onward:
+        shapes.append(jax.ShapeDtypeStruct((levels, onward[1]), here.dtype))
+        out_specs.append(vmem)
     outs = pl.pallas_call(
-        functools.partial(chunk_kernel, spans_of=spans_of, carrier=carrier, opens=opens, closes=closes),
+        functools.partial(chunk_kernel, spans_of=spans_of, carrier=carrier, opens=opens, closes=closes, onward=onward),
         in_specs=specs,
         out_specs=out_specs,
         out_shape=shapes,
@@ -380,24 +386,23 @@
     level = jnp.swapaxes(seg_level[0], 1, 2)
     length = jnp.swapaxes(seg_length[0], 1, 2)
     count = seg_count.reshape(3, 1, rays)
-    first_send, second_send, cols = prepare(level, count, length, absorber, table, firsts[CARRIER], widths[CARRIER])
-    place, base, table_here, measured_here = stage(cols, mask, table, measured[0])
+    first_send, second_send, cols = prepare(level, count, length, absorber, table, firsts[0], widths[0])
+    carried = (traded(first_send, "sector", 0), traded(second_send, "sector", 1))
+    place, base, table_here, measured_here, send = stage(cols, mask, table, measured[0], firsts[1], widths[1])
     base = base[:, :1]
-    first_tables = []
-    second_tables = []
-    for c, (first, width) in enumerate(zip(firsts, widths, strict=True)):
-        piece = table[:, first : first + width]
-        first_tables.append(traded(first_send if c == CARRIER else piece, "sector", 0))
-        second_tables.append(traded(second_send if c == CARRIER else piece, "sector", 1))
     state = None
-    carried = (first_tables[CARRIER], second_tables[CARRIER])
-    for n, group in enumerate(GROUPS):
-        spans_of = tuple((firsts[c], widths[c]) for c in group)
-        sources = [(first_tables[c], second_tables[c]) for c in group]
-        closes = n == len(GROUPS) - 1
-        state, terms = chunk(
-            base, place, table_here, measured_here, cols, carried, widths[CARRIER], spans_of, sources, state, closes
+    sources = carried
+    for c, span in enumerate(zip(firsts, widths, strict=True)):
+        closes = c == len(widths) - 1
+        onward = (firsts[c + 2], widths[c + 2]) if c + 2 < len(widths) else None
+        following = None if closes else (traded(send, "sector", 0), traded(send, "sector", 1))
+        state, rest = chunk(
+            base, place, table_here, measured_here, cols, carried, widths[0], (span,), [sources], state, closes, onward
         )
+        sources = following
+        if onward:
+            send = rest[0]
+    terms = rest
     spectrum = state[0]
     mine = (terms[1], traded(terms[0], "sector", 0), traded(terms[2], "sector", 1))
     others = tuple(swapped(part, "spec") for part in mine)

time: 58.9 us -> 57.7 us (0.980); the launches traced: 58 us -> 57.5 us
  local copies, waits for them, and re-layouts: 1.84 us -> 0.01 us
  starting transfers between devices: 15 us -> 15.6 us
    slice x2 -> x0, local copies, waits for them, and re-layouts: 1.84 us -> none  [shards(): piece = table[:, first:first + width]]
    ppermute x8, starting transfers between devices: 14.4 us -> 15.6 us  [traded(): lax.ppermute(block, axis, [(i, (i + step) % size) for i, step in enumerat...]
  transfers between devices with their start and end apart: 11 -> 11, of which waited for: 4 -> 4; matrix products, arithmetic and copies ran while one was open for 3% -> 0% of each run, Pallas kernels for 24% -> 25%
where the time goes in v4:
time: 57.7 us; the launch traced here: 57.5 us
  Pallas kernels  25 us (43%)
  waiting for transfers between devices  16.1 us (28%)
  starting transfers between devices  15.6 us (27%)
  between operations  0.71 us (1%)
    pallas_call x3, Pallas kernels, chunk(): pl.pallas_call(functools.partial(chunk_kernel, spans_of=spans_of, carrier...  18.8 us
    ppermute x8, starting transfers between devices, traded(): lax.ppermute(block, axis, [(i, (i + step) % size) for i, step in enumerat...  15.6 us
    ppermute x8, waiting for transfers between devices, traded(): lax.ppermute(block, axis, [(i, (i + step) % size) for i, step in enumerat...  14.9 us
    pallas_call x1, Pallas kernels, solve(): pl.pallas_call(functools.partial(solve_kernel, scale=scale), out_shape=ja...  3.08 us
    pallas_call x1, Pallas kernels, stage(): pl.pallas_call(functools.partial(stage_kernel, first=first), in_specs=[vm...  1.94 us
    pallas_call x1, Pallas kernels, prepare(): pl.pallas_call(functools.partial(prepare_kernel, first=first, width=width...  1.25 us
    ppermute x3, waiting for transfers between devices, swapped(): return lax.ppermute(block, axis, [(i, size - 1 - i) for i in range(size)])  1.2 us
  transfers between devices with their start and end apart: 11, of which 4 were waited for; matrix products, arithmetic and copies ran while one was open for 0% of the time, Pallas kernels for 25%

profile of v4, /device:TPU:0, one launch (start us, length us, event | category | flops | bytes accessed | tf_op | source)
XLA Modules:
  0.0 57.5 jit_solution(3232749710983310862)
XLA Ops:
  0.6 1.2 %prepare.1 = (bf16[64,1664]{1,0:T(8,128)(2,1)S(1)}, bf16[64,1664]{1,0:T(8,128)(2,1)S(1)}, bf16[64,128]{1,0:T(8,128)(2,1)S(1)}) custom-call(s32[3,32,128]{2,1,0:T(8,128)} %bitcast.21, s32[3,1,128]{2,1,0:T(1,128)} %bitcast.24, f32[3,32,128]{2,1,0:T(8,128)} %bitcast.22, f32[1,64]{1,0:T(1,128)} %absorber_hbm.1, bf16[64,4096]{1,0:T(8,128)(2,1)} %bitcast.19), custom_call_target="tpu_custom_call" | custom-call | flops 1 | bytes 1 | tf_op jit(solution)/shard_map/prepare/pallas_call | solution.py:76
  1.9 3.0 %collective-permute-start = (bf16[64,1664]{1,0:T(8,128)(2,1)S(1)}, bf16[64,1664]{1,0:T(8,128)(2,1)S(1)}, u32[]{:S(2)}, u32[]{:S(2)}) collective-permute-start(bf16[64,1664]{1,0:T(8,128)(2,1)S(1)} %get-tuple-element.28), channel_id=1, source_target_pairs={{0,2},{2,0},{4,6},{6,4},{8,10},{10,8},{12,14},{14,12},{1,3},{3,1},... | collective-permute-start | bytes 638984 | tf_op jit(solution)/shard_map/ppermute | solution.py:23
  4.9 3.5 %collective-permute-start.1 = (bf16[64,1664]{1,0:T(8,128)(2,1)S(1)}, bf16[64,1664]{1,0:T(8,128)(2,1)S(1)}, u32[]{:S(2)}, u32[]{:S(2)}) collective-permute-start(bf16[64,1664]{1,0:T(8,128)(2,1)S(1)} %get-tuple-element.29), channel_id=1, source_target_pairs={{0,14},{2,4},{4,2},{6,8},{8,6},{10,12},{12,10},{14,0},{1,15},{3,5}... | collective-permute-start | bytes 638984 | tf_op jit(solution)/shard_map/ppermute | solution.py:23
  8.5 1.9 %stage.1 = (s32[32,128]{1,0:T(8,128)S(1)}, s32[40,128]{1,0:T(8,128)S(1)}, bf16[64,4096]{1,0:T(8,128)(2,1)S(1)}, f32[128,4096]{1,0:T(8,128)S(1)}, bf16[64,1792]{1,0:T(8,128)(2,1)S(1)}) custom-call(bf16[64,128]{1,0:T(8,128)(2,1)S(1)} %get-tuple-element.23.cols_ref.refs_4_, s32[32,128]{1,0:T(8,128)} %bitcast.23, bf16[64,4096]{1,0:T(8,128)(2,1)} %bitcast.20, ...), custom_call_target="tpu_custom_call" | custom-call | flops 1 | bytes 1 | tf_op jit(solution)/shard_map/stage/pallas_call | solution.py:120
  10.4 1.2 %collective-permute-start.5 = (bf16[64,1792]{1,0:T(8,128)(2,1)S(1)}, bf16[64,1792]{1,0:T(8,128)(2,1)S(1)}, u32[]{:S(2)}, u32[]{:S(2)}) collective-permute-start(bf16[64,1792]{1,0:T(8,128)(2,1)S(1)} %get-tuple-element.31), channel_id=1, source_target_pairs={{0,14},{2,4},{4,2},{6,8},{8,6},{10,12},{12,10},{14,0},{1,15},{3,5}... | collective-permute-start | bytes 688136 | tf_op jit(solution)/shard_map/ppermute | solution.py:23
  11.7 0.0 collective-permute-start.4
  11.7 8.4 %collective-permute-done.refs_5_.refs_7_ = bf16[64,1664]{1,0:T(8,128)(2,1)S(1)} collective-permute-done((bf16[64,1664]{1,0:T(8,128)(2,1)S(1)}, bf16[64,1664]{1,0:T(8,128)(2,1)S(1)}, u32[]{:S(2)}, u32[]{:S(2)}) %collective-permute-start) | collective-permute-done | bytes 213024 | tf_op jit(solution)/shard_map/ppermute | solution.py:23
  20.0 0.0 collective-permute-done.1.refs_6_.refs_8_
  20.0 5.0 %chunk.3 = (f32[128,4096]{1,0:T(8,128)}, bf16[38,320,128]{2,1,0:T(8,128)(2,1)S(1)}, f32[3,2560,128]{2,1,0:T(8,128)S(1)}, f32[192,128]{1,0:T(8,128)S(1)}, bf16[64,768]{1,0:T(8,128)(2,1)S(1)}) custom-call(s32[40,1]{1,0:T(8,128)S(1)} %bitcast.13, s32[32,128]{1,0:T(8,128)S(1)} %get-tuple-element.25.refs_1_, bf16[64,4096]{1,0:T(8,128)(2,1)S(1)} %get-tuple-element.26.refs_2_, ...), custom_call_target="tpu_custom_call" | custom-call | flops 1 | bytes 1 | tf_op jit(solution)/shard_map/chunk/pallas_call | solution.py:290
  25.1 5.6 %collective-permute-start.3 = (bf16[64,768]{1,0:T(8,128)(2,1)S(1)}, bf16[64,768]{1,0:T(8,128)(2,1)S(1)}, u32[]{:S(2)}, u32[]{:S(2)}) collective-permute-start(bf16[64,768]{1,0:T(8,128)(2,1)S(1)} %get-tuple-element.30), channel_id=1, source_target_pairs={{0,14},{2,4},{4,2},{6,8},{8,6},{10,12},{12,10},{14,0},{1,15},{3,5}... | collective-permute-start | bytes 294920 | tf_op jit(solution)/shard_map/ppermute | solution.py:23
  30.7 0.0 collective-permute-start.2
  30.7 0.0 collective-permute-done.5.refs_8_
  30.7 0.0 collective-permute-done.4.refs_7_
  30.7 7.5 %chunk.4 = (f32[128,4096]{1,0:T(8,128)}, bf16[38,320,128]{2,1,0:T(8,128)(2,1)S(1)}, f32[3,2560,128]{2,1,0:T(8,128)S(1)}, f32[192,128]{1,0:T(8,128)S(1)}) custom-call(s32[40,1]{1,0:T(8,128)S(1)} %bitcast.14, s32[32,128]{1,0:T(8,128)S(1)} %get-tuple-element.25.refs_1_, ...), custom_call_target="tpu_custom_call", output_to_operand_aliasing={{0}: (9, {}), {1}: (10, {}), {2}: (11, {}), {3}: (12, {})} | custom-call | flops 1 | bytes 1 | tf_op jit(solution)/shard_map/chunk/pallas_call | solution.py:290
  38.2 0.0 collective-permute-done.3.refs_8_
  38.2 0.0 copy-start
  38.2 6.3 %chunk.5 = (f32[128,4096]{1,0:T(8,128)}, bf16[38,320,128]{2,1,0:T(8,128)(2,1)S(1)}, f32[3,2560,128]{2,1,0:T(8,128)S(1)}, f32[192,128]{1,0:T(8,128)S(1)}, f32[64,...) custom-call(s32[40,1]{1,0:T(8,128)S(1)} %bitcast.15, ...), custom_call_target="tpu_custom_call", output_to_operand_aliasing={{0}: (9, {}), {1}: (10, {}), {2}: (11, {}), {3}: (12, {})} | custom-call | flops 1 | bytes 1 | tf_op jit(solution)/shard_map/chunk/pallas_call | solution.py:290
  44.5 2.1 %collective-permute-start.6 = (f32[64,128]{1,0:T(8,128)S(1)}, f32[64,128]{1,0:T(8,128)S(1)}, u32[]{:S(2)}, u32[]{:S(2)}) collective-permute-start(f32[64,128]{1,0:T(8,128)S(1)} %get-tuple-element.42), channel_id=1, source_target_pairs={{0,2},{2,0},{4,6},{6,4},{8,10},{10,8},{12,14},{14,12},{1,3},{3,1},... | collective-permute-start | bytes 98312 | tf_op jit(solution)/shard_map/ppermute | solution.py:23
  46.6 0.1 collective-permute-start.7
  46.6 0.0 collective-permute-start.8
  46.6 1.8 %collective-permute-done.6.refs_1_ = f32[64,128]{1,0:T(8,128)S(1)} collective-permute-done((f32[64,128]{1,0:T(8,128)S(1)}, f32[64,128]{1,0:T(8,128)S(1)}, u32[]{:S(2)}, u32[]{:S(2)}) %collective-permute-start.6) | collective-permute-done | bytes 32800 | tf_op jit(solution)/shard_map/ppermute | solution.py:23
  48.5 4.7 %collective-permute-done.7.refs_2_ = f32[64,128]{1,0:T(8,128)S(1)} collective-permute-done((f32[64,128]{1,0:T(8,128)S(1)}, f32[64,128]{1,0:T(8,128)S(1)}, u32[]{:S(2)}, u32[]{:S(2)}) %collective-permute-start.7) | collective-permute-done | bytes 32800 | tf_op jit(solution)/shard_map/ppermute | solution.py:23
  53.2 1.2 %collective-permute-done.10.refs_5_ = f32[64,128]{1,0:T(8,128)S(1)} collective-permute-done((f32[64,128]{1,0:T(8,128)S(1)}, f32[64,128]{1,0:T(8,128)S(1)}, u32[]{:S(2)}, u32[]{:S(2)}) %collective-permute-start.10) | collective-permute-done | bytes 32800 | tf_op jit(solution)/shard_map/ppermute | solution.py:375
  54.4 3.1 %solve.1 = f32[1,64]{1,0:T(1,128)} custom-call(f32[64,128]{1,0:T(8,128)S(1)} %get-tuple-element.41.refs_0_, f32[64,128]{1,0:T(8,128)S(1)} %collective-permute-done.6.refs_1_, f32[64,128]{1,0:T(8,128)S(1)} %collective-permute-done.7.refs_2_, f32[64,128]{1,0:T(8,128)S(1)} %collective-permute-done.8.refs_3_, f32[64,128]{1,0:T(8,128)S(1)} %collective-permute-done.9.refs_4_, ...), custom_call_target="tpu_custom_call" | custom-call | flops 1 | bytes 1 | tf_op jit(solution)/shard_map/solve/pallas_call | solution.py:364
  (6 shorter events, 0.0 us)
Async XLA Ops:
  1.9 18.2 %collective-permute-start = (bf16[64,1664]{1,0:T(8,128)(2,1)S(1)}, bf16[64,1664]{1,0:T(8,128)(2,1)S(1)}, u32[]{:S(2)}, u32[]{:S(2)}) collective-permute-start(bf16[64,1664]{1,0:T(8,128)(2,1)S(1)} %get-tuple-element.28), channel_id=1, source_target_pairs={{0,2},{2,0},{4,6},{6,4},{8,10},{10,8},{12,14},{14,12},{1,3},{3,1},... | collective-permute-start | bytes 638984 | tf_op jit(solution)/shard_map/ppermute | solution.py:23
  4.9 15.1 %collective-permute-start.1 = (bf16[64,1664]{1,0:T(8,128)(2,1)S(1)}, bf16[64,1664]{1,0:T(8,128)(2,1)S(1)}, u32[]{:S(2)}, u32[]{:S(2)}) collective-permute-start(bf16[64,1664]{1,0:T(8,128)(2,1)S(1)} %get-tuple-element.29), channel_id=1, source_target_pairs={{0,14},{2,4},{4,2},{6,8},{8,6},{10,12},{12,10},{14,0},{1,15},{3,5}... | collective-permute-start | bytes 638984 | tf_op jit(solution)/shard_map/ppermute | solution.py:23
  10.4 20.3 %collective-permute-start.5 = (bf16[64,1792]{1,0:T(8,128)(2,1)S(1)}, bf16[64,1792]{1,0:T(8,128)(2,1)S(1)}, u32[]{:S(2)}, u32[]{:S(2)}) collective-permute-start(bf16[64,1792]{1,0:T(8,128)(2,1)S(1)} %get-tuple-element.31), channel_id=1, source_target_pairs={{0,14},{2,4},{4,2},{6,8},{8,6},{10,12},{12,10},{14,0},{1,15},{3,5}... | collective-permute-start | bytes 688136 | tf_op jit(solution)/shard_map/ppermute | solution.py:23
  11.7 19.1 %collective-permute-start.4 = (bf16[64,1792]{1,0:T(8,128)(2,1)S(1)}, bf16[64,1792]{1,0:T(8,128)(2,1)S(1)}, u32[]{:S(2)}, u32[]{:S(2)}) collective-permute-start(bf16[64,1792]{1,0:T(8,128)(2,1)S(1)} %get-tuple-element.31), channel_id=1, source_target_pairs={{0,2},{2,0},{4,6},{6,4},{8,10},{10,8},{12,14},{14,12},{1,3},{3,1},... | collective-permute-start | bytes 688136 | tf_op jit(solution)/shard_map/ppermute | solution.py:23
  25.1 13.1 %collective-permute-start.3 = (bf16[64,768]{1,0:T(8,128)(2,1)S(1)}, bf16[64,768]{1,0:T(8,128)(2,1)S(1)}, u32[]{:S(2)}, u32[]{:S(2)}) collective-permute-start(bf16[64,768]{1,0:T(8,128)(2,1)S(1)} %get-tuple-element.30), channel_id=1, source_target_pairs={{0,14},{2,4},{4,2},{6,8},{8,6},{10,12},{12,10},{14,0},{1,15},{3,5}... | collective-permute-start | bytes 294920 | tf_op jit(solution)/shard_map/ppermute | solution.py:23
  30.7 7.5 %collective-permute-start.2 = (bf16[64,768]{1,0:T(8,128)(2,1)S(1)}, bf16[64,768]{1,0:T(8,128)(2,1)S(1)}, u32[]{:S(2)}, u32[]{:S(2)}) collective-permute-start(bf16[64,768]{1,0:T(8,128)(2,1)S(1)} %get-tuple-element.30), channel_id=1, source_target_pairs={{0,2},{2,0},{4,6},{6,4},{8,10},{10,8},{12,14},{14,12},{1,3},{3,1},... | collective-permute-start | bytes 294920 | tf_op jit(solution)/shard_map/ppermute | solution.py:23
  38.2 16.2 %copy-start = (f32[64]{0:T(128)S(1)}, f32[64]{0:T(128)}, u32[]{:S(2)}) copy-start(f32[64]{0:T(128)} %param.15) | copy-start | bytes 772
  44.5 4.0 %collective-permute-start.6 = (f32[64,128]{1,0:T(8,128)S(1)}, f32[64,128]{1,0:T(8,128)S(1)}, u32[]{:S(2)}, u32[]{:S(2)}) collective-permute-start(f32[64,128]{1,0:T(8,128)S(1)} %get-tuple-element.42), channel_id=1, source_target_pairs={{0,2},{2,0},{4,6},{6,4},{8,10},{10,8},{12,14},{14,12},{1,3},{3,1},... | collective-permute-start | bytes 98312 | tf_op jit(solution)/shard_map/ppermute | solution.py:23
  46.6 6.6 %collective-permute-start.7 = (f32[64,128]{1,0:T(8,128)S(1)}, f32[64,128]{1,0:T(8,128)S(1)}, u32[]{:S(2)}, u32[]{:S(2)}) collective-permute-start(f32[64,128]{1,0:T(8,128)S(1)} %get-tuple-element.43), channel_id=1, source_target_pairs={{0,14},{2,4},{4,2},{6,8},{8,6},{10,12},{12,10},{14,0},{1,15},{3,5}... | collective-permute-start | bytes 98312 | tf_op jit(solution)/shard_map/ppermute | solution.py:23
  46.6 6.5 %collective-permute-start.8 = (f32[64,128]{1,0:T(8,128)S(1)}, f32[64,128]{1,0:T(8,128)S(1)}, u32[]{:S(2)}, u32[]{:S(2)}) collective-permute-start(f32[64,128]{1,0:T(8,128)S(1)} %get-tuple-element.41.refs_0_), channel_id=1, source_target_pairs={{0,1},{1,0},{2,3},{3,2},{4,5},{5,4},{6,7},{7,6},{8,9},{9,8},{10,11... | collective-permute-start | bytes 98312 | tf_op jit(solution)/shard_map/ppermute | solution.py:375
  48.5 4.7 %collective-permute-start.9 = (f32[64,128]{1,0:T(8,128)S(1)}, f32[64,128]{1,0:T(8,128)S(1)}, u32[]{:S(2)}, u32[]{:S(2)}) collective-permute-start(f32[64,128]{1,0:T(8,128)S(1)} %collective-permute-done.6.refs_1_), channel_id=1, source_target_pairs={{0,1},{1,0},{2,3},{3,2},{4,5},{5,4},{6,7},{7,6},{8,9},{9,8},{10,11... | collective-permute-start | bytes 98312 | tf_op jit(solution)/shard_map/ppermute | solution.py:375
  53.2 1.2 %collective-permute-start.10 = (f32[64,128]{1,0:T(8,128)S(1)}, f32[64,128]{1,0:T(8,128)S(1)}, u32[]{:S(2)}, u32[]{:S(2)}) collective-permute-start(f32[64,128]{1,0:T(8,128)S(1)} %collective-permute-done.7.refs_2_), channel_id=1, source_target_pairs={{0,1},{1,0},{2,3},{3,2},{4,5},{5,4},{6,7},{7,6},{8,9},{9,8},{10,11... | collective-permute-start | bytes 98312 | tf_op jit(solution)/shard_map/ppermute | solution.py:375

commit v5 on v4

--- a/solution.py
+++ b/solution.py
@@ -9,9 +9,10 @@
 
 LANES = 128
 ROWS = 16
+HALF = 8
 PIECE = 512
 BLOCK = 512
-WIDTHS = (12, 14, 6)
+WIDTHS = (8, 8, 10, 6)
 SMALL_BYTES = 4 << 20
 CHUNK_BYTES = 16 << 20
 CHEAP = pl.CostEstimate(flops=1, transcendentals=0, bytes_accessed=1)
@@ -135,13 +136,37 @@
 
 
 def pair_rows(levels):
+    whole = []
+    shared = []
     spans = []
     offset = 0
     for m in range(levels):
-        first = ROWS * (m // ROWS)
-        spans.append((m, first, offset, levels - first))
-        offset += levels - first
-    return spans, offset
+        tile = ROWS * (m // ROWS)
+        low = tile if m % ROWS < HALF else tile + ROWS
+        if low < levels:
+            whole.append((m, low, offset))
+            spans.append((m, low, offset, levels - low))
+            offset += levels - low
+    for m in range(0, levels, 2):
+        if m % ROWS >= HALF:
+            low = ROWS * (m // ROWS) + HALF
+            shared.append((m, low, offset))
+            for n in range(2):
+                spans.append((m + n, low, offset + n * HALF, HALF))
+            offset += ROWS
+    return whole, shared, spans, offset
+
+
+def fill_pairs(target, k, lane, rows):
+    levels = rows.shape[0]
+    whole, shared, _, _ = pair_rows(levels)
+    for m, low, offset in whole:
+        target[k, offset : offset + levels - low, lane] = rows[low:, :] * rows[m : m + 1, :]
+    upper = iota((ROWS, rows.shape[1]), 0) < HALF
+    for m, low, offset in shared:
+        half = rows[low : low + HALF, :]
+        both = jnp.concatenate([half, half], axis=0)
+        target[k, offset : offset + ROWS, lane] = both * jnp.where(upper, rows[m : m + 1, :], rows[m + 1 : m + 2, :])
 
 
 def chunk_kernel(*refs, spans_of, carrier, opens, closes, onward):
@@ -167,7 +192,7 @@
     high = 3 * levels
     begin = spans_of[0][0]
     end = spans_of[-1][0] + spans_of[-1][1]
-    spans, pair_count = pair_rows(levels)
+    _, _, spans, pair_count = pair_rows(levels)
     cols = [ref.astype(jnp.float32) for ref in (carried_before[:, carrier:], cols_ref[...], carried_after[:, carrier:])]
     rows = jnp.concatenate([c.T for c in cols], axis=1).astype(jnp.bfloat16)
 
@@ -182,40 +207,42 @@
             size = min(PIECE, width - low_lane)
             local = slice(low_lane, low_lane + size)
             overall = slice(first + low_lane, first + low_lane + size)
-            table[0:levels, :size] = before_ref[:, local]
-            table[levels : 2 * levels, :size] = here_ref[:, overall]
-            table[2 * levels : high, :size] = after_ref[:, local]
-            depth = jnp.dot(rows, table[:high, :size], preferred_element_type=jnp.float32)
+            inside = slice(first + low_lane - begin, first + low_lane - begin + size)
+            table[0:levels, inside] = before_ref[:, local]
+            table[levels : 2 * levels, inside] = here_ref[:, overall]
+            table[2 * levels : high, inside] = after_ref[:, local]
+            depth = jnp.dot(rows, table[:high, inside], preferred_element_type=jnp.float32)
             spectrum = jnp.exp(-depth)
-            inside = slice(first + low_lane - begin, first + low_lane - begin + size)
             modelled[:, inside] = spectrum
             copy = pltpu.make_async_copy(modelled.at[:, inside], spectrum_ref.at[:, overall], sems.at[len(copies)])
             copy.start()
             copies.append(copy)
-            table[high:, :size] = (spectrum * spectrum).astype(jnp.bfloat16)
+            table[high:, inside] = (spectrum * spectrum).astype(jnp.bfloat16)
             groups = range(overall.start // LANES, overall.stop // LANES)
             places = [place_ref[g : g + 1, :] for g in groups]
             kept = jnp.concatenate(places, axis=1) >= 0
             error = jnp.where(kept, (measured_ref[:, overall] - spectrum) * spectrum, 0.0).astype(jnp.bfloat16)
-            projected[...] += nt_dot(table[:high, :size], error)
+            projected[...] += nt_dot(table[:high, inside], error)
             for n, (g, place) in enumerate(zip(groups, places, strict=True)):
                 at = base_ref[g, 0] // LANES
                 chosen = (iota((2 * LANES, LANES), 0) + at * LANES == place).astype(jnp.bfloat16)
-                moved = nt_dot(table[:, n * LANES : (n + 1) * LANES], chosen).astype(jnp.bfloat16)
+                moved = nt_dot(table[:, inside.start + n * LANES : inside.start + (n + 1) * LANES], chosen).astype(jnp.bfloat16)
                 packed[at] = packed[at] + moved[:, :LANES]
                 packed[at + 1] = moved[:, LANES:]
 
-    def one_block(block, parts):
+    def one_block(block, parts, then=None):
         wide = parts * LANES
         for p in range(parts):
             lane = slice(p * LANES, (p + 1) * LANES)
             weights[:, lane] = packed[block + p, high:, :]
             for k in range(3):
-                level_rows = packed[block + p, k * levels : (k + 1) * levels, :]
-                for m, low, offset, count in spans:
-                    pairs[k, offset : offset + count, lane] = level_rows[low:, :] * level_rows[m : m + 1, :]
+                fill_pairs(pairs, k, lane, packed[block + p, k * levels : (k + 1) * levels, :])
         for k in range(3):
             moment[k] += nt_dot(pairs[k, :, :wide], weights[:, :wide])
+            if then and k:
+                then(k - 1)
+        if then:
+            then(2)
 
     parts = BLOCK // LANES
     done = base_ref[begin // LANES, 0] // BLOCK
@@ -228,29 +255,33 @@
         for d in range(2, parts + 1):
             packed[last + d] = jnp.zeros(packed.shape[1:], packed.dtype)
         left = count - ready * BLOCK
+        lane = iota((levels, LANES), 1)
+
+        def contract(k):
+            gradient = jnp.sum(cols[k] * projected[k * levels : (k + 1) * levels, :], axis=1, keepdims=True)
+            result = jnp.where(lane == levels, gradient, 0.0)
+            columns = {}
+            for m, low, offset, size in spans:
+                scaled = cols[k][low : low + size, :] * cols[k][m : m + 1, :]
+                column = jnp.sum(moment[k, offset : offset + size, :] * scaled, axis=1, keepdims=True)
+                columns.setdefault(m, []).append((low, column))
+            for m, parts_of in columns.items():
+                parts_of = sorted(parts_of, key=lambda part: part[0])
+                low = parts_of[0][0]
+                stack = [column for _, column in parts_of]
+                if low:
+                    stack = [jnp.zeros((low, 1), jnp.float32), *stack]
+                result = jnp.where(lane == m, jnp.concatenate(stack, axis=0) if len(stack) > 1 else stack[0], result)
+            terms_refs[k][...] = result
 
         @pl.when(left > BLOCK // 2)
         def _():
-            one_block(ready * parts, parts)
-
-        @pl.when((left > 0) & (left <= BLOCK // 2))
+            one_block(ready * parts, parts, contract)
+
+        @pl.when(left <= BLOCK // 2)
         def _():
-            one_block(ready * parts, parts // 2)
-
-        lane = iota((levels, LANES), 1)
-        for k in range(3):
-            gradient = jnp.sum(cols[k] * projected[k * levels : (k + 1) * levels, :], axis=1, keepdims=True)
-            result = jnp.where(lane == levels, gradient, 0.0)
-            for m, low, offset, count in spans:
-                column = jnp.sum(
-                    moment[k, offset : offset + count, :] * (cols[k][low:, :] * cols[k][m : m + 1, :]),
-                    axis=1,
-                    keepdims=True,
-                )
-                if low:
-                    column = jnp.concatenate([jnp.zeros((low, 1), jnp.float32), column], axis=0)
-                result = jnp.where(lane == m, column, result)
-            terms_refs[k][...] = result
+            one_block(ready * parts, parts // 2, contract)
+
     for copy in copies:
         copy.wait()
 
@@ -258,7 +289,7 @@
 def chunk(base, place, here, measured, cols, carried, carrier, spans_of, sources, state, closes, onward):
     levels, points = here.shape
     rays = measured.shape[0]
-    _, pair_count = pair_rows(levels)
+    _, _, _, pair_count = pair_rows(levels)
     opens = state is None
     smem = pl.BlockSpec(memory_space=pltpu.SMEM)
     vmem = pl.BlockSpec(memory_space=pltpu.VMEM)
@@ -293,7 +324,7 @@
         out_specs=out_specs,
         out_shape=shapes,
         scratch_shapes=[
-            pltpu.VMEM((3 * levels + rays, PIECE), jnp.bfloat16),
+            pltpu.VMEM((3 * levels + rays, width), jnp.bfloat16),
             pltpu.VMEM((rays, width), jnp.float32),
             pltpu.VMEM((3, pair_count, BLOCK), jnp.bfloat16),
             pltpu.VMEM((rays, BLOCK), jnp.bfloat16),
@@ -347,7 +378,7 @@
     lane = iota((levels, LANES), 1)
     square = terms[:, :levels]
     flipped = jnp.concatenate([square.T, jnp.zeros((levels, LANES - levels), jnp.float32)], axis=1)
-    lower = row // ROWS >= lane // ROWS
+    lower = row // HALF >= lane // HALF
     work = jnp.where(lower | (lane >= levels), terms, flipped)
     diagonal = jnp.sum(jnp.where(row == lane, work, 0.0), axis=1, keepdims=True)
     mean = jnp.sum(diagonal, axis=0, keepdims=True) * (1.0 / levels) + 1e-06

time: 57.7 us -> 56.8 us (0.984)
  waiting for transfers between devices: 16.1 us -> 10.3 us
  starting transfers between devices: 15.6 us -> 18.8 us
  Pallas kernels: 25 us -> 26.9 us
    ppermute x8 -> x10, waiting for transfers between devices: 14.9 us -> 9.06 us  [traded(): lax.ppermute(block, axis, [(i, (i + step) % size) for i, step in enumerat...]
    ppermute x8 -> x10, starting transfers between devices: 15.6 us -> 18.8 us  [traded(): lax.ppermute(block, axis, [(i, (i + step) % size) for i, step in enumerat...]
    pallas_call x3 -> x4, Pallas kernels: 18.8 us -> 20.7 us  [chunk(): pl.pallas_call(functools.partial(chunk_kernel, spans_of=spans_of, carrier...]
  transfers between devices with their start and end apart: 11 -> 13, of which waited for: 4 -> 5; matrix products, arithmetic and copies ran while one was open for 0% -> 0% of each run, Pallas kernels for 25% -> 27%
where the time goes in v5:
time: 56.8 us; the launch traced here: 56.7 us
  Pallas kernels  26.9 us (47%)
  starting transfers between devices  18.8 us (33%)
  waiting for transfers between devices  10.3 us (18%)
  between operations  0.72 us (1%)
    pallas_call x4, Pallas kernels, chunk(): pl.pallas_call(functools.partial(chunk_kernel, spans_of=spans_of, carrier...  20.7 us
    ppermute x10, starting transfers between devices, traded(): lax.ppermute(block, axis, [(i, (i + step) % size) for i, step in enumerat...  18.8 us
    ppermute x10, waiting for transfers between devices, traded(): lax.ppermute(block, axis, [(i, (i + step) % size) for i, step in enumerat...  9.06 us
    pallas_call x1, Pallas kernels, solve(): pl.pallas_call(functools.partial(solve_kernel, scale=scale), out_shape=ja...  3.08 us
    pallas_call x1, Pallas kernels, stage(): pl.pallas_call(functools.partial(stage_kernel, first=first), in_specs=[vm...  1.88 us
    pallas_call x1, Pallas kernels, prepare(): pl.pallas_call(functools.partial(prepare_kernel, first=first, width=width...  1.25 us
    ppermute x3, waiting for transfers between devices, swapped(): return lax.ppermute(block, axis, [(i, size - 1 - i) for i in range(size)])  1.2 us
  transfers between devices with their start and end apart: 13, of which 5 were waited for; matrix products, arithmetic and copies ran while one was open for 0% of the time, Pallas kernels for 27%

profile of v5, /device:TPU:0, one launch (start us, length us, event | category | flops | bytes accessed | tf_op | source)
XLA Modules:
  0.0 56.7 jit_solution(176607622575337817)
XLA Ops:
  0.6 1.2 %prepare.1 = (bf16[64,1152]{1,0:T(8,128)(2,1)S(1)}, bf16[64,1152]{1,0:T(8,128)(2,1)S(1)}, bf16[64,128]{1,0:T(8,128)(2,1)S(1)}) custom-call(s32[3,32,128]{2,1,0:T(8,128)} %bitcast.22, s32[3,1,128]{2,1,0:T(1,128)} %bitcast.25, f32[3,32,128]{2,1,0:T(8,128)} %bitcast.23, f32[1,64]{1,0:T(1,128)} %absorber_hbm.1, bf16[64,4096]{1,0:T(8,128)(2,1)} %bitcast.20), custom_call_target="tpu_custom_call" | custom-call | flops 1 | bytes 1 | tf_op jit(solution)/shard_map/prepare/pallas_call | solution.py:77
  1.9 3.0 %collective-permute-start = (bf16[64,1152]{1,0:T(8,128)(2,1)S(1)}, bf16[64,1152]{1,0:T(8,128)(2,1)S(1)}, u32[]{:S(2)}, u32[]{:S(2)}) collective-permute-start(bf16[64,1152]{1,0:T(8,128)(2,1)S(1)} %get-tuple-element.33), channel_id=1, source_target_pairs={{0,2},{2,0},{4,6},{6,4},{8,10},{10,8},{12,14},{14,12},{1,3},{3,1},... | collective-permute-start | bytes 442376 | tf_op jit(solution)/shard_map/ppermute | solution.py:24
  4.9 3.5 %collective-permute-start.1 = (bf16[64,1152]{1,0:T(8,128)(2,1)S(1)}, bf16[64,1152]{1,0:T(8,128)(2,1)S(1)}, u32[]{:S(2)}, u32[]{:S(2)}) collective-permute-start(bf16[64,1152]{1,0:T(8,128)(2,1)S(1)} %get-tuple-element.34), channel_id=1, source_target_pairs={{0,14},{2,4},{4,2},{6,8},{8,6},{10,12},{12,10},{14,0},{1,15},{3,5}... | collective-permute-start | bytes 442376 | tf_op jit(solution)/shard_map/ppermute | solution.py:24
  8.5 1.9 %stage.1 = (s32[32,128]{1,0:T(8,128)S(1)}, s32[40,128]{1,0:T(8,128)S(1)}, bf16[64,4096]{1,0:T(8,128)(2,1)S(1)}, f32[128,4096]{1,0:T(8,128)S(1)}, bf16[64,1024]{1,0:T(8,128)(2,1)S(1)}) custom-call(bf16[64,128]{1,0:T(8,128)(2,1)S(1)} %get-tuple-element.28.cols_ref.refs_4_, s32[32,128]{1,0:T(8,128)} %bitcast.24, bf16[64,4096]{1,0:T(8,128)(2,1)} %bitcast.21, ...), custom_call_target="tpu_custom_call" | custom-call | flops 1 | bytes 1 | tf_op jit(solution)/shard_map/stage/pallas_call | solution.py:121
  10.4 1.2 %collective-permute-start.3 = (bf16[64,1024]{1,0:T(8,128)(2,1)S(1)}, bf16[64,1024]{1,0:T(8,128)(2,1)S(1)}, u32[]{:S(2)}, u32[]{:S(2)}) collective-permute-start(bf16[64,1024]{1,0:T(8,128)(2,1)S(1)} %get-tuple-element.35), channel_id=1, source_target_pairs={{0,14},{2,4},{4,2},{6,8},{8,6},{10,12},{12,10},{14,0},{1,15},{3,5}... | collective-permute-start | bytes 393224 | tf_op jit(solution)/shard_map/ppermute | solution.py:24
  11.6 3.2 %collective-permute-done.refs_5_.refs_7_ = bf16[64,1152]{1,0:T(8,128)(2,1)S(1)} collective-permute-done((bf16[64,1152]{1,0:T(8,128)(2,1)S(1)}, bf16[64,1152]{1,0:T(8,128)(2,1)S(1)}, u32[]{:S(2)}, u32[]{:S(2)}) %collective-permute-start) | collective-permute-done | bytes 147488 | tf_op jit(solution)/shard_map/ppermute | solution.py:24
  14.8 0.0 collective-permute-done.1.refs_6_.refs_8_
  14.8 4.4 %chunk.4 = (f32[128,4096]{1,0:T(8,128)}, bf16[38,320,128]{2,1,0:T(8,128)(2,1)S(1)}, f32[3,2304,128]{2,1,0:T(8,128)S(1)}, f32[192,128]{1,0:T(8,128)S(1)}, bf16[64,1280]{1,0:T(8,128)(2,1)S(1)}) custom-call(s32[40,1]{1,0:T(8,128)S(1)} %bitcast.13, s32[32,128]{1,0:T(8,128)S(1)} %get-tuple-element.30.refs_1_, bf16[64,4096]{1,0:T(8,128)(2,1)S(1)} %get-tuple-element.31.refs_2_, ...), custom_call_target="tpu_custom_call" | custom-call | flops 1 | bytes 1 | tf_op jit(solution)/shard_map/chunk/pallas_call | solution.py:321
  19.2 4.8 %collective-permute-start.7 = (bf16[64,1280]{1,0:T(8,128)(2,1)S(1)}, bf16[64,1280]{1,0:T(8,128)(2,1)S(1)}, u32[]{:S(2)}, u32[]{:S(2)}) collective-permute-start(bf16[64,1280]{1,0:T(8,128)(2,1)S(1)} %get-tuple-element.41), channel_id=1, source_target_pairs={{0,14},{2,4},{4,2},{6,8},{8,6},{10,12},{12,10},{14,0},{1,15},{3,5}... | collective-permute-start | bytes 491528 | tf_op jit(solution)/shard_map/ppermute | solution.py:24
  24.1 0.0 collective-permute-start.6
  24.1 0.0 collective-permute-done.3.refs_8_
  24.1 2.5 %chunk.5 = (f32[128,4096]{1,0:T(8,128)}, bf16[38,320,128]{2,1,0:T(8,128)(2,1)S(1)}, f32[3,2304,128]{2,1,0:T(8,128)S(1)}, f32[192,128]{1,0:T(8,128)S(1)}, bf16[64,768]{1,0:T(8,128)(2,1)S(1)}) custom-call(s32[40,1]{1,0:T(8,128)S(1)} %bitcast.14, ...), custom_call_target="tpu_custom_call", output_to_operand_aliasing={{0}: (9, {}), {1}: (10, {}), {2}: (11, {}), {3}: (12, {})} | custom-call | flops 1 | bytes 1 | tf_op jit(solution)/shard_map/chunk/pallas_call | solution.py:321
  26.5 3.0 %collective-permute-start.5 = (bf16[64,768]{1,0:T(8,128)(2,1)S(1)}, bf16[64,768]{1,0:T(8,128)(2,1)S(1)}, u32[]{:S(2)}, u32[]{:S(2)}) collective-permute-start(bf16[64,768]{1,0:T(8,128)(2,1)S(1)} %get-tuple-element.40), channel_id=1, source_target_pairs={{0,14},{2,4},{4,2},{6,8},{8,6},{10,12},{12,10},{14,0},{1,15},{3,5}... | collective-permute-start | bytes 294920 | tf_op jit(solution)/shard_map/ppermute | solution.py:24
  29.6 1.6 %collective-permute-done.6.refs_7_ = bf16[64,1280]{1,0:T(8,128)(2,1)S(1)} collective-permute-done((bf16[64,1280]{1,0:T(8,128)(2,1)S(1)}, bf16[64,1280]{1,0:T(8,128)(2,1)S(1)}, u32[]{:S(2)}, u32[]{:S(2)}) %collective-permute-start.6) | collective-permute-done | bytes 163872 | tf_op jit(solution)/shard_map/ppermute | solution.py:24
  31.2 6.6 %chunk.6 = (f32[128,4096]{1,0:T(8,128)}, bf16[38,320,128]{2,1,0:T(8,128)(2,1)S(1)}, f32[3,2304,128]{2,1,0:T(8,128)S(1)}, f32[192,128]{1,0:T(8,128)S(1)}) custom-call(s32[40,1]{1,0:T(8,128)S(1)} %bitcast.15, s32[32,128]{1,0:T(8,128)S(1)} %get-tuple-element.30.refs_1_, ...), custom_call_target="tpu_custom_call", output_to_operand_aliasing={{0}: (9, {}), {1}: (10, {}), {2}: (11, {}), {3}: (12, {})} | custom-call | flops 1 | bytes 1 | tf_op jit(solution)/shard_map/chunk/pallas_call | solution.py:321
  37.9 0.0 collective-permute-done.4.refs_7_
  37.9 0.0 copy-start
  37.9 7.2 %chunk.7 = (f32[128,4096]{1,0:T(8,128)}, bf16[38,320,128]{2,1,0:T(8,128)(2,1)S(1)}, f32[3,2304,128]{2,1,0:T(8,128)S(1)}, f32[192,128]{1,0:T(8,128)S(1)}, f32[64,...) custom-call(s32[40,1]{1,0:T(8,128)S(1)} %bitcast.16, ...), custom_call_target="tpu_custom_call", output_to_operand_aliasing={{0}: (9, {}), {1}: (10, {}), {2}: (11, {}), {3}: (12, {})} | custom-call | flops 1 | bytes 1 | tf_op jit(solution)/shard_map/chunk/pallas_call | solution.py:321
  45.1 0.7 %collective-permute-start.8 = (f32[64,128]{1,0:T(8,128)S(1)}, f32[64,128]{1,0:T(8,128)S(1)}, u32[]{:S(2)}, u32[]{:S(2)}) collective-permute-start(f32[64,128]{1,0:T(8,128)S(1)} %get-tuple-element.52), channel_id=1, source_target_pairs={{0,2},{2,0},{4,6},{6,4},{8,10},{10,8},{12,14},{14,12},{1,3},{3,1},... | collective-permute-start | bytes 98312 | tf_op jit(solution)/shard_map/ppermute | solution.py:24
  45.8 2.4 %collective-permute-start.9 = (f32[64,128]{1,0:T(8,128)S(1)}, f32[64,128]{1,0:T(8,128)S(1)}, u32[]{:S(2)}, u32[]{:S(2)}) collective-permute-start(f32[64,128]{1,0:T(8,128)S(1)} %get-tuple-element.53), channel_id=1, source_target_pairs={{0,14},{2,4},{4,2},{6,8},{8,6},{10,12},{12,10},{14,0},{1,15},{3,5}... | collective-permute-start | bytes 98312 | tf_op jit(solution)/shard_map/ppermute | solution.py:24
  48.2 0.9 %collective-permute-done.8.refs_1_ = f32[64,128]{1,0:T(8,128)S(1)} collective-permute-done((f32[64,128]{1,0:T(8,128)S(1)}, f32[64,128]{1,0:T(8,128)S(1)}, u32[]{:S(2)}, u32[]{:S(2)}) %collective-permute-start.8) | collective-permute-done | bytes 32800 | tf_op jit(solution)/shard_map/ppermute | solution.py:24
  49.1 3.3 %collective-permute-done.9.refs_2_ = f32[64,128]{1,0:T(8,128)S(1)} collective-permute-done((f32[64,128]{1,0:T(8,128)S(1)}, f32[64,128]{1,0:T(8,128)S(1)}, u32[]{:S(2)}, u32[]{:S(2)}) %collective-permute-start.9) | collective-permute-done | bytes 32800 | tf_op jit(solution)/shard_map/ppermute | solution.py:24
  52.4 1.2 %collective-permute-done.12.refs_5_ = f32[64,128]{1,0:T(8,128)S(1)} collective-permute-done((f32[64,128]{1,0:T(8,128)S(1)}, f32[64,128]{1,0:T(8,128)S(1)}, u32[]{:S(2)}, u32[]{:S(2)}) %collective-permute-start.12) | collective-permute-done | bytes 32800 | tf_op jit(solution)/shard_map/ppermute | solution.py:406
  53.6 3.1 %solve.1 = f32[1,64]{1,0:T(1,128)} custom-call(f32[64,128]{1,0:T(8,128)S(1)} %get-tuple-element.51.refs_0_, f32[64,128]{1,0:T(8,128)S(1)} %collective-permute-done.8.refs_1_, f32[64,128]{1,0:T(8,128)S(1)} %collective-permute-done.9.refs_2_, f32[64,128]{1,0:T(8,128)S(1)} %collective-permute-done.10.refs_3_, f32[64,128]{1,0:T(8,128)S(1)} %collective-permute-done.11.refs_4_, ...), custom_call_target="tpu_custom_call" | custom-call | flops 1 | bytes 1 | tf_op jit(solution)/shard_map/solve/pallas_call | solution.py:395
  (11 shorter events, 0.0 us)
Async XLA Ops:
  1.9 12.9 %collective-permute-start = (bf16[64,1152]{1,0:T(8,128)(2,1)S(1)}, bf16[64,1152]{1,0:T(8,128)(2,1)S(1)}, u32[]{:S(2)}, u32[]{:S(2)}) collective-permute-start(bf16[64,1152]{1,0:T(8,128)(2,1)S(1)} %get-tuple-element.33), channel_id=1, source_target_pairs={{0,2},{2,0},{4,6},{6,4},{8,10},{10,8},{12,14},{14,12},{1,3},{3,1},... | collective-permute-start | bytes 442376 | tf_op jit(solution)/shard_map/ppermute | solution.py:24
  4.9 9.9 %collective-permute-start.1 = (bf16[64,1152]{1,0:T(8,128)(2,1)S(1)}, bf16[64,1152]{1,0:T(8,128)(2,1)S(1)}, u32[]{:S(2)}, u32[]{:S(2)}) collective-permute-start(bf16[64,1152]{1,0:T(8,128)(2,1)S(1)} %get-tuple-element.34), channel_id=1, source_target_pairs={{0,14},{2,4},{4,2},{6,8},{8,6},{10,12},{12,10},{14,0},{1,15},{3,5}... | collective-permute-start | bytes 442376 | tf_op jit(solution)/shard_map/ppermute | solution.py:24
  10.4 13.7 %collective-permute-start.3 = (bf16[64,1024]{1,0:T(8,128)(2,1)S(1)}, bf16[64,1024]{1,0:T(8,128)(2,1)S(1)}, u32[]{:S(2)}, u32[]{:S(2)}) collective-permute-start(bf16[64,1024]{1,0:T(8,128)(2,1)S(1)} %get-tuple-element.35), channel_id=1, source_target_pairs={{0,14},{2,4},{4,2},{6,8},{8,6},{10,12},{12,10},{14,0},{1,15},{3,5}... | collective-permute-start | bytes 393224 | tf_op jit(solution)/shard_map/ppermute | solution.py:24
  11.6 12.5 %collective-permute-start.2 = (bf16[64,1024]{1,0:T(8,128)(2,1)S(1)}, bf16[64,1024]{1,0:T(8,128)(2,1)S(1)}, u32[]{:S(2)}, u32[]{:S(2)}) collective-permute-start(bf16[64,1024]{1,0:T(8,128)(2,1)S(1)} %get-tuple-element.35), channel_id=1, source_target_pairs={{0,2},{2,0},{4,6},{6,4},{8,10},{10,8},{12,14},{14,12},{1,3},{3,1},... | collective-permute-start | bytes 393224 | tf_op jit(solution)/shard_map/ppermute | solution.py:24
  19.2 10.4 %collective-permute-start.7 = (bf16[64,1280]{1,0:T(8,128)(2,1)S(1)}, bf16[64,1280]{1,0:T(8,128)(2,1)S(1)}, u32[]{:S(2)}, u32[]{:S(2)}) collective-permute-start(bf16[64,1280]{1,0:T(8,128)(2,1)S(1)} %get-tuple-element.41), channel_id=1, source_target_pairs={{0,14},{2,4},{4,2},{6,8},{8,6},{10,12},{12,10},{14,0},{1,15},{3,5}... | collective-permute-start | bytes 491528 | tf_op jit(solution)/shard_map/ppermute | solution.py:24
  24.1 7.2 %collective-permute-start.6 = (bf16[64,1280]{1,0:T(8,128)(2,1)S(1)}, bf16[64,1280]{1,0:T(8,128)(2,1)S(1)}, u32[]{:S(2)}, u32[]{:S(2)}) collective-permute-start(bf16[64,1280]{1,0:T(8,128)(2,1)S(1)} %get-tuple-element.41), channel_id=1, source_target_pairs={{0,2},{2,0},{4,6},{6,4},{8,10},{10,8},{12,14},{14,12},{1,3},{3,1},... | collective-permute-start | bytes 491528 | tf_op jit(solution)/shard_map/ppermute | solution.py:24
  26.5 11.3 %collective-permute-start.5 = (bf16[64,768]{1,0:T(8,128)(2,1)S(1)}, bf16[64,768]{1,0:T(8,128)(2,1)S(1)}, u32[]{:S(2)}, u32[]{:S(2)}) collective-permute-start(bf16[64,768]{1,0:T(8,128)(2,1)S(1)} %get-tuple-element.40), channel_id=1, source_target_pairs={{0,14},{2,4},{4,2},{6,8},{8,6},{10,12},{12,10},{14,0},{1,15},{3,5}... | collective-permute-start | bytes 294920 | tf_op jit(solution)/shard_map/ppermute | solution.py:24
  29.6 8.3 %collective-permute-start.4 = (bf16[64,768]{1,0:T(8,128)(2,1)S(1)}, bf16[64,768]{1,0:T(8,128)(2,1)S(1)}, u32[]{:S(2)}, u32[]{:S(2)}) collective-permute-start(bf16[64,768]{1,0:T(8,128)(2,1)S(1)} %get-tuple-element.40), channel_id=1, source_target_pairs={{0,2},{2,0},{4,6},{6,4},{8,10},{10,8},{12,14},{14,12},{1,3},{3,1},... | collective-permute-start | bytes 294920 | tf_op jit(solution)/shard_map/ppermute | solution.py:24
  37.9 15.8 %copy-start = (f32[64]{0:T(128)S(1)}, f32[64]{0:T(128)}, u32[]{:S(2)}) copy-start(f32[64]{0:T(128)} %param.15) | copy-start | bytes 772
  45.1 4.0 %collective-permute-start.8 = (f32[64,128]{1,0:T(8,128)S(1)}, f32[64,128]{1,0:T(8,128)S(1)}, u32[]{:S(2)}, u32[]{:S(2)}) collective-permute-start(f32[64,128]{1,0:T(8,128)S(1)} %get-tuple-element.52), channel_id=1, source_target_pairs={{0,2},{2,0},{4,6},{6,4},{8,10},{10,8},{12,14},{14,12},{1,3},{3,1},... | collective-permute-start | bytes 98312 | tf_op jit(solution)/shard_map/ppermute | solution.py:24
  45.8 6.6 %collective-permute-start.9 = (f32[64,128]{1,0:T(8,128)S(1)}, f32[64,128]{1,0:T(8,128)S(1)}, u32[]{:S(2)}, u32[]{:S(2)}) collective-permute-start(f32[64,128]{1,0:T(8,128)S(1)} %get-tuple-element.53), channel_id=1, source_target_pairs={{0,14},{2,4},{4,2},{6,8},{8,6},{10,12},{12,10},{14,0},{1,15},{3,5}... | collective-permute-start | bytes 98312 | tf_op jit(solution)/shard_map/ppermute | solution.py:24
  48.2 4.2 %collective-permute-start.10 = (f32[64,128]{1,0:T(8,128)S(1)}, f32[64,128]{1,0:T(8,128)S(1)}, u32[]{:S(2)}, u32[]{:S(2)}) collective-permute-start(f32[64,128]{1,0:T(8,128)S(1)} %get-tuple-element.51.refs_0_), channel_id=1, source_target_pairs={{0,1},{1,0},{2,3},{3,2},{4,5},{5,4},{6,7},{7,6},{8,9},{9,8},{10,11... | collective-permute-start | bytes 98312 | tf_op jit(solution)/shard_map/ppermute | solution.py:406
  49.1 3.3 %collective-permute-start.11 = (f32[64,128]{1,0:T(8,128)S(1)}, f32[64,128]{1,0:T(8,128)S(1)}, u32[]{:S(2)}, u32[]{:S(2)}) collective-permute-start(f32[64,128]{1,0:T(8,128)S(1)} %collective-permute-done.8.refs_1_), channel_id=1, source_target_pairs={{0,1},{1,0},{2,3},{3,2},{4,5},{5,4},{6,7},{7,6},{8,9},{9,8},{10,11... | collective-permute-start | bytes 98312 | tf_op jit(solution)/shard_map/ppermute | solution.py:406
  52.4 1.2 %collective-permute-start.12 = (f32[64,128]{1,0:T(8,128)S(1)}, f32[64,128]{1,0:T(8,128)S(1)}, u32[]{:S(2)}, u32[]{:S(2)}) collective-permute-start(f32[64,128]{1,0:T(8,128)S(1)} %collective-permute-done.9.refs_2_), channel_id=1, source_target_pairs={{0,1},{1,0},{2,3},{3,2},{4,5},{5,4},{6,7},{7,6},{8,9},{9,8},{10,11... | collective-permute-start | bytes 98312 | tf_op jit(solution)/shard_map/ppermute | solution.py:406

commit v6 on v5

--- a/solution.py
+++ b/solution.py
@@ -12,7 +12,7 @@
 HALF = 8
 PIECE = 512
 BLOCK = 512
-WIDTHS = (8, 8, 10, 6)
+WIDTHS = (8, 12, 12)
 SMALL_BYTES = 4 << 20
 CHUNK_BYTES = 16 << 20
 CHEAP = pl.CostEstimate(flops=1, transcendentals=0, bytes_accessed=1)
@@ -91,10 +91,12 @@
     )(*pinned(level, count, length, absorber, table))
 
 
-def stage_kernel(cols_ref, mask_hbm, table_hbm, measured_hbm, place_ref, base_ref, table_ref, measured_ref, send_ref, mask_ref, sems, *, first):
+def stage_kernel(cols_ref, mask_hbm, table_hbm, measured_hbm, place_ref, base_ref, table_ref, measured_ref, *rest, firsts):
     del cols_ref
-    part = table_hbm.at[:, pl.ds(first, send_ref.shape[1])]
-    moves = ((mask_hbm, mask_ref), (part, send_ref), (table_hbm, table_ref), (measured_hbm, measured_ref))
+    *sends, mask_ref, sems = rest
+    moves = [(mask_hbm, mask_ref)]
+    moves += [(table_hbm.at[:, pl.ds(first, ref.shape[1])], ref) for first, ref in zip(firsts, sends, strict=True)]
+    moves += [(table_hbm, table_ref), (measured_hbm, measured_ref)]
     copies = [pltpu.make_async_copy(a, b, sems.at[n]) for n, (a, b) in enumerate(moves)]
     for copy in copies:
         copy.start()
@@ -114,21 +116,21 @@
         copy.wait()
 
 
-def stage(cols, mask, table, measured, first, width):
+def stage(cols, mask, table, measured, firsts, widths):
     groups = mask.shape[0]
     vmem = pl.BlockSpec(memory_space=pltpu.VMEM)
     hbm = pl.BlockSpec(memory_space=pltpu.HBM)
     return pl.pallas_call(
-        functools.partial(stage_kernel, first=first),
+        functools.partial(stage_kernel, firsts=firsts),
         in_specs=[vmem, hbm, hbm, hbm],
         out_shape=(
             jax.ShapeDtypeStruct((groups, LANES), jnp.int32),
             jax.ShapeDtypeStruct((groups + 8, LANES), jnp.int32),
             jax.ShapeDtypeStruct(table.shape, table.dtype),
             jax.ShapeDtypeStruct(measured.shape, measured.dtype),
-            jax.ShapeDtypeStruct((table.shape[0], width), table.dtype),
+            *[jax.ShapeDtypeStruct((table.shape[0], width), table.dtype) for width in widths],
         ),
-        scratch_shapes=[pltpu.VMEM(mask.shape, mask.dtype), pltpu.SemaphoreType.DMA((4,))],
+        scratch_shapes=[pltpu.VMEM(mask.shape, mask.dtype), pltpu.SemaphoreType.DMA((3 + len(widths),))],
         compiler_params=pltpu.CompilerParams(vmem_limit_bytes=SMALL_BYTES),
         cost_estimate=CHEAP,
         name="stage",
@@ -169,7 +171,7 @@
         target[k, offset : offset + ROWS, lane] = both * jnp.where(upper, rows[m : m + 1, :], rows[m + 1 : m + 2, :])
 
 
-def chunk_kernel(*refs, spans_of, carrier, opens, closes, onward):
+def chunk_kernel(*refs, spans_of, carrier, opens, closes):
     base_ref, place_ref, here_ref, measured_ref, cols_ref, carried_before, carried_after = refs[:7]
     refs = refs[7:]
     sources = []
@@ -183,9 +185,6 @@
     if closes:
         terms_refs = refs[:3]
         refs = refs[3:]
-    if onward:
-        refs[0][...] = here_ref[:, onward[0] : onward[0] + onward[1]]
-        refs = refs[1:]
     table, modelled, pairs, weights, sems = refs
     levels = here_ref.shape[0]
     rays = measured_ref.shape[0]
@@ -230,7 +229,7 @@
                 packed[at] = packed[at] + moved[:, :LANES]
                 packed[at + 1] = moved[:, LANES:]
 
-    def one_block(block, parts, then=None):
+    def one_block(block, parts):
         wide = parts * LANES
         for p in range(parts):
             lane = slice(p * LANES, (p + 1) * LANES)
@@ -239,10 +238,6 @@
                 fill_pairs(pairs, k, lane, packed[block + p, k * levels : (k + 1) * levels, :])
         for k in range(3):
             moment[k] += nt_dot(pairs[k, :, :wide], weights[:, :wide])
-            if then and k:
-                then(k - 1)
-        if then:
-            then(2)
 
     parts = BLOCK // LANES
     done = base_ref[begin // LANES, 0] // BLOCK
@@ -276,17 +271,19 @@
 
         @pl.when(left > BLOCK // 2)
         def _():
-            one_block(ready * parts, parts, contract)
-
-        @pl.when(left <= BLOCK // 2)
+            one_block(ready * parts, parts)
+
+        @pl.when((left > 0) & (left <= BLOCK // 2))
         def _():
-            one_block(ready * parts, parts // 2, contract)
-
+            one_block(ready * parts, parts // 2)
+
+        for k in range(3):
+            contract(k)
     for copy in copies:
         copy.wait()
 
 
-def chunk(base, place, here, measured, cols, carried, carrier, spans_of, sources, state, closes, onward):
+def chunk(base, place, here, measured, cols, carried, carrier, spans_of, sources, state, closes):
     levels, points = here.shape
     rays = measured.shape[0]
     _, _, _, pair_count = pair_rows(levels)
@@ -315,11 +312,8 @@
     if closes:
         shapes += [jax.ShapeDtypeStruct((levels, LANES), jnp.float32)] * 3
         out_specs += [vmem] * 3
-    if onward:
-        shapes.append(jax.ShapeDtypeStruct((levels, onward[1]), here.dtype))
-        out_specs.append(vmem)
     outs = pl.pallas_call(
-        functools.partial(chunk_kernel, spans_of=spans_of, carrier=carrier, opens=opens, closes=closes, onward=onward),
+        functools.partial(chunk_kernel, spans_of=spans_of, carrier=carrier, opens=opens, closes=closes),
         in_specs=specs,
         out_specs=out_specs,
         out_shape=shapes,
@@ -419,21 +413,21 @@
     count = seg_count.reshape(3, 1, rays)
     first_send, second_send, cols = prepare(level, count, length, absorber, table, firsts[0], widths[0])
     carried = (traded(first_send, "sector", 0), traded(second_send, "sector", 1))
-    place, base, table_here, measured_here, send = stage(cols, mask, table, measured[0], firsts[1], widths[1])
+    place, base, table_here, measured_here, *sends = stage(cols, mask, table, measured[0], firsts[1:], widths[1:])
     base = base[:, :1]
+    received = [carried]
+    for c, send in enumerate(sends):
+        if c:
+            send, *arrived = lax.optimization_barrier((send, *received[c - 1]))
+            received[c - 1] = tuple(arrived)
+        received.append((traded(send, "sector", 0), traded(send, "sector", 1)))
     state = None
-    sources = carried
+    carried = received[0]
     for c, span in enumerate(zip(firsts, widths, strict=True)):
         closes = c == len(widths) - 1
-        onward = (firsts[c + 2], widths[c + 2]) if c + 2 < len(widths) else None
-        following = None if closes else (traded(send, "sector", 0), traded(send, "sector", 1))
-        state, rest = chunk(
-            base, place, table_here, measured_here, cols, carried, widths[0], (span,), [sources], state, closes, onward
+        state, terms = chunk(
+            base, place, table_here, measured_here, cols, carried, widths[0], (span,), [received[c]], state, closes
         )
-        sources = following
-        if onward:
-            send = rest[0]
-    terms = rest
     spectrum = state[0]
     mine = (terms[1], traded(terms[0], "sector", 0), traded(terms[2], "sector", 1))
     others = tuple(swapped(part, "spec") for part in mine)

time: 56.8 us -> 54.9 us (0.967)
  waiting for transfers between devices: 10.3 us -> 7.67 us
  starting transfers between devices: 18.8 us -> 20.8 us
  Pallas kernels: 26.9 us -> 25.3 us
    ppermute x10 -> x8, waiting for transfers between devices: 9.06 us -> 6.81 us  [traded(): lax.ppermute(block, axis, [(i, (i + step) % size) for i, step in enumerat...]
    pallas_call x4 -> x3, Pallas kernels: 20.7 us -> 18.9 us  [chunk(): pl.pallas_call(functools.partial(chunk_kernel, spans_of=spans_of, carrier...]
    ppermute x10 -> x8, starting transfers between devices: 18.8 us -> 20.1 us  [traded(): lax.ppermute(block, axis, [(i, (i + step) % size) for i, step in enumerat...]
    ppermute x3, starting transfers between devices: 0.01 us -> 0.73 us  [swapped(): return lax.ppermute(block, axis, [(i, size - 1 - i) for i in range(size)])]
  transfers between devices with their start and end apart: 13 -> 11, of which waited for: 5 -> 4; matrix products, arithmetic and copies ran while one was open for 0% -> 0% of each run, Pallas kernels for 27% -> 20%
where the time goes in v6:
time: 54.9 us; the launch traced here: 54.5 us
  Pallas kernels  25.3 us (46%)
  starting transfers between devices  20.8 us (38%)
  waiting for transfers between devices  7.67 us (14%)
  between operations  0.74 us (1%)
    ppermute x8, starting transfers between devices, traded(): lax.ppermute(block, axis, [(i, (i + step) % size) for i, step in enumerat...  20.1 us
    pallas_call x3, Pallas kernels, chunk(): pl.pallas_call(functools.partial(chunk_kernel, spans_of=spans_of, carrier...  18.9 us
    ppermute x8, waiting for transfers between devices, traded(): lax.ppermute(block, axis, [(i, (i + step) % size) for i, step in enumerat...  6.81 us
    pallas_call x1, Pallas kernels, solve(): pl.pallas_call(functools.partial(solve_kernel, scale=scale), out_shape=ja...  3.08 us
    pallas_call x1, Pallas kernels, stage(): pl.pallas_call(functools.partial(stage_kernel, firsts=firsts), in_specs=[...  2.02 us
    pallas_call x1, Pallas kernels, prepare(): pl.pallas_call(functools.partial(prepare_kernel, first=first, width=width...  1.25 us
  transfers between devices with their start and end apart: 11, of which 4 were waited for; matrix products, arithmetic and copies ran while one was open for 0% of the time, Pallas kernels for 20%

profile of v6, /device:TPU:0, one launch (start us, length us, event | category | flops | bytes accessed | tf_op | source)
XLA Modules:
  0.0 54.5 jit_solution(3549281175820653147)
XLA Ops:
  0.6 1.2 %prepare.1 = (bf16[64,1152]{1,0:T(8,128)(2,1)S(1)}, bf16[64,1152]{1,0:T(8,128)(2,1)S(1)}, bf16[64,128]{1,0:T(8,128)(2,1)S(1)}) custom-call(s32[3,32,128]{2,1,0:T(8,128)} %bitcast.21, s32[3,1,128]{2,1,0:T(1,128)} %bitcast.24, f32[3,32,128]{2,1,0:T(8,128)} %bitcast.22, f32[1,64]{1,0:T(1,128)} %absorber_hbm.1, bf16[64,4096]{1,0:T(8,128)(2,1)} %bitcast.19), custom_call_target="tpu_custom_call" | custom-call | flops 1 | bytes 1 | tf_op jit(solution)/shard_map/prepare/pallas_call | solution.py:77
  1.9 3.0 %collective-permute-start = (bf16[64,1152]{1,0:T(8,128)(2,1)S(1)}, bf16[64,1152]{1,0:T(8,128)(2,1)S(1)}, u32[]{:S(2)}, u32[]{:S(2)}) collective-permute-start(bf16[64,1152]{1,0:T(8,128)(2,1)S(1)} %get-tuple-element.32), channel_id=1, source_target_pairs={{0,2},{2,0},{4,6},{6,4},{8,10},{10,8},{12,14},{14,12},{1,3},{3,1},... | collective-permute-start | bytes 442376 | tf_op jit(solution)/shard_map/ppermute | solution.py:24
  4.9 3.5 %collective-permute-start.1 = (bf16[64,1152]{1,0:T(8,128)(2,1)S(1)}, bf16[64,1152]{1,0:T(8,128)(2,1)S(1)}, u32[]{:S(2)}, u32[]{:S(2)}) collective-permute-start(bf16[64,1152]{1,0:T(8,128)(2,1)S(1)} %get-tuple-element.33), channel_id=1, source_target_pairs={{0,14},{2,4},{4,2},{6,8},{8,6},{10,12},{12,10},{14,0},{1,15},{3,5}... | collective-permute-start | bytes 442376 | tf_op jit(solution)/shard_map/ppermute | solution.py:24
  8.5 2.0 %stage.1 = (s32[32,128]{1,0:T(8,128)S(1)}, s32[40,128]{1,0:T(8,128)S(1)}, bf16[64,4096]{1,0:T(8,128)(2,1)S(1)}, f32[128,4096]{1,0:T(8,128)S(1)}, bf16[64,1536]{1...) custom-call(bf16[64,128]{1,0:T(8,128)(2,1)S(1)} %get-tuple-element.26.cols_ref.refs_4_, s32[32,128]{1,0:T(8,128)} %bitcast.23, ...), custom_call_target="tpu_custom_call" | custom-call | flops 1 | bytes 1 | tf_op jit(solution)/shard_map/stage/pallas_call | solution.py:123
  10.5 0.1 collective-permute-start.4
  10.6 1.9 %collective-permute-start.5 = (bf16[64,1536]{1,0:T(8,128)(2,1)S(1)}, bf16[64,1536]{1,0:T(8,128)(2,1)S(1)}, u32[]{:S(2)}, u32[]{:S(2)}) collective-permute-start(bf16[64,1536]{1,0:T(8,128)(2,1)S(1)} %get-tuple-element.37), channel_id=1, source_target_pairs={{0,14},{2,4},{4,2},{6,8},{8,6},{10,12},{12,10},{14,0},{1,15},{3,5}... | collective-permute-start | bytes 589832 | tf_op jit(solution)/shard_map/ppermute | solution.py:24
  12.5 0.0 collective-permute-done.refs_5_.refs_7_
  12.5 0.5 collective-permute-done.1.refs_6_.refs_8_
  13.0 1.6 %collective-permute-start.2 = (bf16[64,1536]{1,0:T(8,128)(2,1)S(1)}, bf16[64,1536]{1,0:T(8,128)(2,1)S(1)}, u32[]{:S(2)}, u32[]{:S(2)}) collective-permute-start(bf16[64,1536]{1,0:T(8,128)(2,1)S(1)} %get-tuple-element.36), channel_id=1, source_target_pairs={{0,2},{2,0},{4,6},{6,4},{8,10},{10,8},{12,14},{14,12},{1,3},{3,1},... | collective-permute-start | bytes 589832 | tf_op jit(solution)/shard_map/ppermute | solution.py:24
  14.6 9.8 %collective-permute-start.3 = (bf16[64,1536]{1,0:T(8,128)(2,1)S(1)}, bf16[64,1536]{1,0:T(8,128)(2,1)S(1)}, u32[]{:S(2)}, u32[]{:S(2)}) collective-permute-start(bf16[64,1536]{1,0:T(8,128)(2,1)S(1)} %get-tuple-element.36), channel_id=1, source_target_pairs={{0,14},{2,4},{4,2},{6,8},{8,6},{10,12},{12,10},{14,0},{1,15},{3,5}... | collective-permute-start | bytes 589832 | tf_op jit(solution)/shard_map/ppermute | solution.py:24
  24.4 4.4 %chunk.3 = (f32[128,4096]{1,0:T(8,128)}, bf16[38,320,128]{2,1,0:T(8,128)(2,1)S(1)}, f32[3,2304,128]{2,1,0:T(8,128)S(1)}, f32[192,128]{1,0:T(8,128)S(1)}) custom-call(s32[40,1]{1,0:T(8,128)S(1)} %bitcast.13, s32[32,128]{1,0:T(8,128)S(1)} %get-tuple-element.28.refs_1_, bf16[64,4096]{1,0:T(8,128)(2,1)S(1)} %get-tuple-element.29.refs_2_, ...), custom_call_target="tpu_custom_call" | custom-call | flops 1 | bytes 1 | tf_op jit(solution)/shard_map/chunk/pallas_call | solution.py:315
  28.8 0.0 collective-permute-done.4.refs_7_
  28.8 4.6 %chunk.4 = (f32[128,4096]{1,0:T(8,128)}, bf16[38,320,128]{2,1,0:T(8,128)(2,1)S(1)}, f32[3,2304,128]{2,1,0:T(8,128)S(1)}, f32[192,128]{1,0:T(8,128)S(1)}) custom-call(s32[40,1]{1,0:T(8,128)S(1)} %bitcast.14, s32[32,128]{1,0:T(8,128)S(1)} %get-tuple-element.28.refs_1_, ...), custom_call_target="tpu_custom_call", output_to_operand_aliasing={{0}: (9, {}), {1}: (10, {}), {2}: (11, {}), {3}: (12, {})} | custom-call | flops 1 | bytes 1 | tf_op jit(solution)/shard_map/chunk/pallas_call | solution.py:315
  33.4 0.0 collective-permute-done.3.refs_8_
  33.5 0.0 copy-start
  33.5 9.9 %chunk.5 = (f32[128,4096]{1,0:T(8,128)}, bf16[38,320,128]{2,1,0:T(8,128)(2,1)S(1)}, f32[3,2304,128]{2,1,0:T(8,128)S(1)}, f32[192,128]{1,0:T(8,128)S(1)}, f32[64,...) custom-call(s32[40,1]{1,0:T(8,128)S(1)} %bitcast.15, ...), custom_call_target="tpu_custom_call", output_to_operand_aliasing={{0}: (9, {}), {1}: (10, {}), {2}: (11, {}), {3}: (12, {})} | custom-call | flops 1 | bytes 1 | tf_op jit(solution)/shard_map/chunk/pallas_call | solution.py:315
  43.4 0.1 collective-permute-start.7
  43.6 0.2 collective-permute-start.8
  43.8 6.3 %collective-permute-done.7.refs_2_ = f32[64,128]{1,0:T(8,128)S(1)} collective-permute-done((f32[64,128]{1,0:T(8,128)S(1)}, f32[64,128]{1,0:T(8,128)S(1)}, u32[]{:S(2)}, u32[]{:S(2)}) %collective-permute-start.7) | collective-permute-done | bytes 32800 | tf_op jit(solution)/shard_map/ppermute | solution.py:24
  50.1 0.5 collective-permute-start.9
  50.6 0.0 collective-permute-done.8.refs_3_
  50.6 0.7 %collective-permute-done.10.refs_5_ = f32[64,128]{1,0:T(8,128)S(1)} collective-permute-done((f32[64,128]{1,0:T(8,128)S(1)}, f32[64,128]{1,0:T(8,128)S(1)}, u32[]{:S(2)}, u32[]{:S(2)}) %collective-permute-start.10) | collective-permute-done | bytes 32800 | tf_op jit(solution)/shard_map/ppermute | solution.py:400
  51.3 0.2 collective-permute-done.9.refs_4_
  51.5 3.1 %solve.1 = f32[1,64]{1,0:T(1,128)} custom-call(f32[64,128]{1,0:T(8,128)S(1)} %get-tuple-element.47.refs_0_, f32[64,128]{1,0:T(8,128)S(1)} %collective-permute-done.6.refs_1_, f32[64,128]{1,0:T(8,128)S(1)} %collective-permute-done.7.refs_2_, f32[64,128]{1,0:T(8,128)S(1)} %collective-permute-done.8.refs_3_, f32[64,128]{1,0:T(8,128)S(1)} %collective-permute-done.9.refs_4_, ...), custom_call_target="tpu_custom_call" | custom-call | flops 1 | bytes 1 | tf_op jit(solution)/shard_map/solve/pallas_call | solution.py:389
  (6 shorter events, 0.0 us)
Async XLA Ops:
  1.9 10.6 %collective-permute-start = (bf16[64,1152]{1,0:T(8,128)(2,1)S(1)}, bf16[64,1152]{1,0:T(8,128)(2,1)S(1)}, u32[]{:S(2)}, u32[]{:S(2)}) collective-permute-start(bf16[64,1152]{1,0:T(8,128)(2,1)S(1)} %get-tuple-element.32), channel_id=1, source_target_pairs={{0,2},{2,0},{4,6},{6,4},{8,10},{10,8},{12,14},{14,12},{1,3},{3,1},... | collective-permute-start | bytes 442376 | tf_op jit(solution)/shard_map/ppermute | solution.py:24
  4.9 8.1 %collective-permute-start.1 = (bf16[64,1152]{1,0:T(8,128)(2,1)S(1)}, bf16[64,1152]{1,0:T(8,128)(2,1)S(1)}, u32[]{:S(2)}, u32[]{:S(2)}) collective-permute-start(bf16[64,1152]{1,0:T(8,128)(2,1)S(1)} %get-tuple-element.33), channel_id=1, source_target_pairs={{0,14},{2,4},{4,2},{6,8},{8,6},{10,12},{12,10},{14,0},{1,15},{3,5}... | collective-permute-start | bytes 442376 | tf_op jit(solution)/shard_map/ppermute | solution.py:24
  10.5 18.3 %collective-permute-start.4 = (bf16[64,1536]{1,0:T(8,128)(2,1)S(1)}, bf16[64,1536]{1,0:T(8,128)(2,1)S(1)}, u32[]{:S(2)}, u32[]{:S(2)}) collective-permute-start(bf16[64,1536]{1,0:T(8,128)(2,1)S(1)} %get-tuple-element.37), channel_id=1, source_target_pairs={{0,2},{2,0},{4,6},{6,4},{8,10},{10,8},{12,14},{14,12},{1,3},{3,1},... | collective-permute-start | bytes 589832 | tf_op jit(solution)/shard_map/ppermute | solution.py:24
  10.6 18.2 %collective-permute-start.5 = (bf16[64,1536]{1,0:T(8,128)(2,1)S(1)}, bf16[64,1536]{1,0:T(8,128)(2,1)S(1)}, u32[]{:S(2)}, u32[]{:S(2)}) collective-permute-start(bf16[64,1536]{1,0:T(8,128)(2,1)S(1)} %get-tuple-element.37), channel_id=1, source_target_pairs={{0,14},{2,4},{4,2},{6,8},{8,6},{10,12},{12,10},{14,0},{1,15},{3,5}... | collective-permute-start | bytes 589832 | tf_op jit(solution)/shard_map/ppermute | solution.py:24
  13.0 20.5 %collective-permute-start.2 = (bf16[64,1536]{1,0:T(8,128)(2,1)S(1)}, bf16[64,1536]{1,0:T(8,128)(2,1)S(1)}, u32[]{:S(2)}, u32[]{:S(2)}) collective-permute-start(bf16[64,1536]{1,0:T(8,128)(2,1)S(1)} %get-tuple-element.36), channel_id=1, source_target_pairs={{0,2},{2,0},{4,6},{6,4},{8,10},{10,8},{12,14},{14,12},{1,3},{3,1},... | collective-permute-start | bytes 589832 | tf_op jit(solution)/shard_map/ppermute | solution.py:24
  14.6 18.9 %collective-permute-start.3 = (bf16[64,1536]{1,0:T(8,128)(2,1)S(1)}, bf16[64,1536]{1,0:T(8,128)(2,1)S(1)}, u32[]{:S(2)}, u32[]{:S(2)}) collective-permute-start(bf16[64,1536]{1,0:T(8,128)(2,1)S(1)} %get-tuple-element.36), channel_id=1, source_target_pairs={{0,14},{2,4},{4,2},{6,8},{8,6},{10,12},{12,10},{14,0},{1,15},{3,5}... | collective-permute-start | bytes 589832 | tf_op jit(solution)/shard_map/ppermute | solution.py:24
  33.5 18.0 %copy-start = (f32[64]{0:T(128)S(1)}, f32[64]{0:T(128)}, u32[]{:S(2)}) copy-start(f32[64]{0:T(128)} %param.15) | copy-start | bytes 772
  43.4 6.7 %collective-permute-start.7 = (f32[64,128]{1,0:T(8,128)S(1)}, f32[64,128]{1,0:T(8,128)S(1)}, u32[]{:S(2)}, u32[]{:S(2)}) collective-permute-start(f32[64,128]{1,0:T(8,128)S(1)} %get-tuple-element.49), channel_id=1, source_target_pairs={{0,14},{2,4},{4,2},{6,8},{8,6},{10,12},{12,10},{14,0},{1,15},{3,5}... | collective-permute-start | bytes 98312 | tf_op jit(solution)/shard_map/ppermute | solution.py:24
  43.6 6.5 %collective-permute-start.6 = (f32[64,128]{1,0:T(8,128)S(1)}, f32[64,128]{1,0:T(8,128)S(1)}, u32[]{:S(2)}, u32[]{:S(2)}) collective-permute-start(f32[64,128]{1,0:T(8,128)S(1)} %get-tuple-element.48), channel_id=1, source_target_pairs={{0,2},{2,0},{4,6},{6,4},{8,10},{10,8},{12,14},{14,12},{1,3},{3,1},... | collective-permute-start | bytes 98312 | tf_op jit(solution)/shard_map/ppermute | solution.py:24
  43.6 7.0 %collective-permute-start.8 = (f32[64,128]{1,0:T(8,128)S(1)}, f32[64,128]{1,0:T(8,128)S(1)}, u32[]{:S(2)}, u32[]{:S(2)}) collective-permute-start(f32[64,128]{1,0:T(8,128)S(1)} %get-tuple-element.47.refs_0_), channel_id=1, source_target_pairs={{0,1},{1,0},{2,3},{3,2},{4,5},{5,4},{6,7},{7,6},{8,9},{9,8},{10,11... | collective-permute-start | bytes 98312 | tf_op jit(solution)/shard_map/ppermute | solution.py:400
  50.1 1.2 %collective-permute-start.10 = (f32[64,128]{1,0:T(8,128)S(1)}, f32[64,128]{1,0:T(8,128)S(1)}, u32[]{:S(2)}, u32[]{:S(2)}) collective-permute-start(f32[64,128]{1,0:T(8,128)S(1)} %collective-permute-done.7.refs_2_), channel_id=1, source_target_pairs={{0,1},{1,0},{2,3},{3,2},{4,5},{5,4},{6,7},{7,6},{8,9},{9,8},{10,11... | collective-permute-start | bytes 98312 | tf_op jit(solution)/shard_map/ppermute | solution.py:400
  50.1 1.4 %collective-permute-start.9 = (f32[64,128]{1,0:T(8,128)S(1)}, f32[64,128]{1,0:T(8,128)S(1)}, u32[]{:S(2)}, u32[]{:S(2)}) collective-permute-start(f32[64,128]{1,0:T(8,128)S(1)} %collective-permute-done.6.refs_1_), channel_id=1, source_target_pairs={{0,1},{1,0},{2,3},{3,2},{4,5},{5,4},{6,7},{7,6},{8,9},{9,8},{10,11... | collective-permute-start | bytes 98312 | tf_op jit(solution)/shard_map/ppermute | solution.py:400

commit v7 on v6

--- a/solution.py
+++ b/solution.py
@@ -12,16 +12,20 @@
 HALF = 8
 PIECE = 512
 BLOCK = 512
-WIDTHS = (8, 12, 12)
+WIDTHS = (9, 14, 9)
 SMALL_BYTES = 4 << 20
 CHUNK_BYTES = 16 << 20
 CHEAP = pl.CostEstimate(flops=1, transcendentals=0, bytes_accessed=1)
 
 
-def traded(block, axis, side):
-    size = lax.axis_size(axis)
-    steps = [1 if (i + side) % 2 == 0 else -1 for i in range(size)]
-    return lax.ppermute(block, axis, [(i, (i + step) % size) for i, step in enumerate(steps)])
+def traded(block, side):
+    size, cores = lax.axis_size("sector"), lax.axis_size("spec")
+    route = []
+    for i in range(size):
+        for core in range(cores):
+            step = 1 if (i + core + side) % 2 == 0 else -1
+            route.append((i * cores + core, (i + step) % size * cores + core))
+    return lax.ppermute(block, ("sector", "spec"), route)
 
 
 def iota(shape, dim):
@@ -52,7 +56,7 @@
     eye = iota((levels, levels), 0) == iota((levels, levels), 1)
     amount = jnp.sum(jnp.where(eye, absorber_ref[...], 0.0), axis=1, keepdims=True)
     level_of = iota((levels, rays), 0)
-    odd = lax.axis_index("sector") % 2
+    odd = (lax.axis_index("sector") + lax.axis_index("spec")) % 2
     absorbed = []
     for k in range(sets):
         length = jnp.where(iota((segs, rays), 0) < count_ref[k], length_ref[k], 0.0)
@@ -93,13 +97,15 @@
 
 def stage_kernel(cols_ref, mask_hbm, table_hbm, measured_hbm, place_ref, base_ref, table_ref, measured_ref, *rest, firsts):
     del cols_ref
-    *sends, mask_ref, sems = rest
+    *sends, moment_ref, projected_ref, mask_ref, sems = rest
     moves = [(mask_hbm, mask_ref)]
     moves += [(table_hbm.at[:, pl.ds(first, ref.shape[1])], ref) for first, ref in zip(firsts, sends, strict=True)]
     moves += [(table_hbm, table_ref), (measured_hbm, measured_ref)]
     copies = [pltpu.make_async_copy(a, b, sems.at[n]) for n, (a, b) in enumerate(moves)]
     for copy in copies:
         copy.start()
+    moment_ref[...] = jnp.zeros_like(moment_ref)
+    projected_ref[...] = jnp.zeros_like(projected_ref)
     copies[0].wait()
     groups = mask_ref.shape[0]
     mask = mask_ref[...].astype(jnp.bfloat16)
@@ -129,6 +135,8 @@
             jax.ShapeDtypeStruct(table.shape, table.dtype),
             jax.ShapeDtypeStruct(measured.shape, measured.dtype),
             *[jax.ShapeDtypeStruct((table.shape[0], width), table.dtype) for width in widths],
+            jax.ShapeDtypeStruct((3, pair_rows(table.shape[0])[-1], measured.shape[0]), jnp.float32),
+            jax.ShapeDtypeStruct((3 * table.shape[0], measured.shape[0]), jnp.float32),
         ),
         scratch_shapes=[pltpu.VMEM(mask.shape, mask.dtype), pltpu.SemaphoreType.DMA((3 + len(widths),))],
         compiler_params=pltpu.CompilerParams(vmem_limit_bytes=SMALL_BYTES),
@@ -178,8 +186,7 @@
     for _ in spans_of:
         sources.append(refs[:2])
         refs = refs[2:]
-    if not opens:
-        refs = refs[4:]
+    refs = refs[2:] if opens else refs[4:]
     spectrum_ref, packed, moment, projected = refs[:4]
     refs = refs[4:]
     if closes:
@@ -196,8 +203,6 @@
     rows = jnp.concatenate([c.T for c in cols], axis=1).astype(jnp.bfloat16)
 
     if opens:
-        moment[...] = jnp.zeros_like(moment)
-        projected[...] = jnp.zeros_like(projected)
         packed[0] = jnp.zeros(packed.shape[1:], packed.dtype)
 
     copies = []
@@ -287,7 +292,7 @@
     levels, points = here.shape
     rays = measured.shape[0]
     _, _, _, pair_count = pair_rows(levels)
-    opens = state is None
+    opens = len(state) == 2
     smem = pl.BlockSpec(memory_space=pltpu.SMEM)
     vmem = pl.BlockSpec(memory_space=pltpu.VMEM)
     hbm = pl.BlockSpec(memory_space=pltpu.HBM)
@@ -298,10 +303,9 @@
         args += pair
         specs += [vmem, vmem]
     aliases = {}
-    if not opens:
-        aliases = {len(args) + n: n for n in range(4)}
-        args += state
-        specs += [hbm, vmem, vmem, vmem]
+    aliases = {len(args) + n: 4 - len(state) + n for n in range(len(state))}
+    args += state
+    specs += [hbm, vmem, vmem, vmem][4 - len(state) :]
     shapes = [
         jax.ShapeDtypeStruct(measured.shape, jnp.float32),
         jax.ShapeDtypeStruct(((points + BLOCK) // LANES + 2, 3 * levels + rays, LANES), jnp.bfloat16),
@@ -412,24 +416,22 @@
     length = jnp.swapaxes(seg_length[0], 1, 2)
     count = seg_count.reshape(3, 1, rays)
     first_send, second_send, cols = prepare(level, count, length, absorber, table, firsts[0], widths[0])
-    carried = (traded(first_send, "sector", 0), traded(second_send, "sector", 1))
-    place, base, table_here, measured_here, *sends = stage(cols, mask, table, measured[0], firsts[1:], widths[1:])
+    carried = (traded(first_send, 0), traded(second_send, 1))
+    place, base, table_here, measured_here, *sends, moment, projected = stage(cols, mask, table, measured[0], firsts[1:], widths[1:])
     base = base[:, :1]
-    received = [carried]
-    for c, send in enumerate(sends):
-        if c:
-            send, *arrived = lax.optimization_barrier((send, *received[c - 1]))
-            received[c - 1] = tuple(arrived)
-        received.append((traded(send, "sector", 0), traded(send, "sector", 1)))
-    state = None
-    carried = received[0]
+    received = [carried, (traded(sends[0], 0), traded(sends[0], 1))]
+    state = (moment, projected)
     for c, span in enumerate(zip(firsts, widths, strict=True)):
         closes = c == len(widths) - 1
+        if c + 2 < len(widths):
+            send, *arrived = lax.optimization_barrier((sends[c + 1], *received[c]))
+            received[c] = tuple(arrived)
+            received.append((traded(send, 0), traded(send, 1)))
         state, terms = chunk(
-            base, place, table_here, measured_here, cols, carried, widths[0], (span,), [received[c]], state, closes
+            base, place, table_here, measured_here, cols, received[0], widths[0], (span,), [received[c]], state, closes
         )
     spectrum = state[0]
-    mine = (terms[1], traded(terms[0], "sector", 0), traded(terms[2], "sector", 1))
+    mine = (terms[1], traded(terms[0], 0), traded(terms[2], 1))
     others = tuple(swapped(part, "spec") for part in mine)
     scale = 1.0 / (rays * points * lax.axis_size("spec"))
     state_step = solve(mine + others, prior_weight[None, :], scale)

time: 54.9 us -> 53.6 us (0.976)
  waiting for transfers between devices: 7.67 us -> 4.64 us
  starting transfers between devices: 20.8 us -> 23 us
  Pallas kernels: 25.3 us -> 24.4 us
    ppermute x8, waiting for transfers between devices: 6.81 us -> 3.78 us  [traded(): return lax.ppermute(block, ('sector', 'spec'), route)]
    ppermute x3, starting transfers between devices: 0.73 us -> 2.09 us  [swapped(): return lax.ppermute(block, axis, [(i, size - 1 - i) for i in range(size)])]
    pallas_call x3, Pallas kernels: 18.9 us -> 17.8 us  [chunk(): pl.pallas_call(functools.partial(chunk_kernel, spans_of=spans_of, carrier...]
    ppermute x8, starting transfers between devices: 20.1 us -> 20.9 us  [traded(): return lax.ppermute(block, ('sector', 'spec'), route)]
  transfers between devices with their start and end apart: 11 -> 11, of which waited for: 4 -> 5; matrix products, arithmetic and copies ran while one was open for 0% -> 0% of each run, Pallas kernels for 20% -> 22%
where the time goes in v7:
time: 53.6 us; the launch traced here: 52.7 us
  Pallas kernels  24.4 us (46%)
  starting transfers between devices  23 us (43%)
  waiting for transfers between devices  4.64 us (9%)
  between operations  0.73 us (1%)
    ppermute x8, starting transfers between devices, traded(): return lax.ppermute(block, ('sector', 'spec'), route)  20.9 us
    pallas_call x3, Pallas kernels, chunk(): pl.pallas_call(functools.partial(chunk_kernel, spans_of=spans_of, carrier...  17.8 us
    ppermute x8, waiting for transfers between devices, traded(): return lax.ppermute(block, ('sector', 'spec'), route)  3.78 us
    pallas_call x1, Pallas kernels, solve(): pl.pallas_call(functools.partial(solve_kernel, scale=scale), out_shape=ja...  3.08 us
    pallas_call x1, Pallas kernels, stage(): pl.pallas_call(functools.partial(stage_kernel, firsts=firsts), in_specs=[...  2.24 us
    ppermute x3, starting transfers between devices, swapped(): return lax.ppermute(block, axis, [(i, size - 1 - i) for i in range(size)])  2.09 us
    pallas_call x1, Pallas kernels, prepare(): pl.pallas_call(functools.partial(prepare_kernel, first=first, width=width...  1.25 us
  transfers between devices with their start and end apart: 11, of which 5 were waited for; matrix products, arithmetic and copies ran while one was open for 0% of the time, Pallas kernels for 22%

profile of v7, /device:TPU:0, one launch (start us, length us, event | category | flops | bytes accessed | tf_op | source)
XLA Modules:
  0.0 52.7 jit_solution(7726417490281680148)
XLA Ops:
  0.6 1.2 %prepare.1 = (bf16[64,1280]{1,0:T(8,128)(2,1)S(1)}, bf16[64,1280]{1,0:T(8,128)(2,1)S(1)}, bf16[64,128]{1,0:T(8,128)(2,1)S(1)}) custom-call(s32[3,32,128]{2,1,0:T(8,128)} %bitcast.21, s32[3,1,128]{2,1,0:T(1,128)} %bitcast.24, f32[3,32,128]{2,1,0:T(8,128)} %bitcast.22, f32[1,64]{1,0:T(1,128)} %absorber_hbm.1, bf16[64,4096]{1,0:T(8,128)(2,1)} %bitcast.19), custom_call_target="tpu_custom_call" | custom-call | flops 1 | bytes 1 | tf_op jit(solution)/shard_map/prepare/pallas_call | solution.py:81
  1.9 3.0 %collective-permute-start = (bf16[64,1280]{1,0:T(8,128)(2,1)S(1)}, bf16[64,1280]{1,0:T(8,128)(2,1)S(1)}, u32[]{:S(2)}, u32[]{:S(2)}) collective-permute-start(bf16[64,1280]{1,0:T(8,128)(2,1)S(1)} %get-tuple-element.34), channel_id=1, source_target_pairs={{0,2},{1,15},{2,0},{3,5},{4,6},{5,3},{6,4},{7,9},{8,10},{9,7},{10,... | collective-permute-start | bytes 491528 | tf_op jit(solution)/shard_map/ppermute | solution.py:28
  4.9 3.5 %collective-permute-start.1 = (bf16[64,1280]{1,0:T(8,128)(2,1)S(1)}, bf16[64,1280]{1,0:T(8,128)(2,1)S(1)}, u32[]{:S(2)}, u32[]{:S(2)}) collective-permute-start(bf16[64,1280]{1,0:T(8,128)(2,1)S(1)} %get-tuple-element.35), channel_id=1, source_target_pairs={{0,14},{1,3},{2,4},{3,1},{4,2},{5,7},{6,8},{7,5},{8,6},{9,11},{10,... | collective-permute-start | bytes 491528 | tf_op jit(solution)/shard_map/ppermute | solution.py:28
  8.5 2.2 %stage.1 = (s32[32,128]{1,0:T(8,128)S(1)}, s32[40,128]{1,0:T(8,128)S(1)}, bf16[64,4096]{1,0:T(8,128)(2,1)S(1)}, f32[128,4096]{1,0:T(8,128)S(1)}, bf16[64,1792]{1...) custom-call(bf16[64,128]{1,0:T(8,128)(2,1)S(1)} %get-tuple-element.28.cols_r, ...), custom_call_target="tpu_custom_call" | custom-call | flops 1 | bytes 1 | tf_op jit(solution)/shard_map/stage/pallas_call | solution.py:129
  10.7 0.1 collective-permute-start.4
  10.8 1.9 %collective-permute-start.5 = (bf16[64,1792]{1,0:T(8,128)(2,1)S(1)}, bf16[64,1792]{1,0:T(8,128)(2,1)S(1)}, u32[]{:S(2)}, u32[]{:S(2)}) collective-permute-start(bf16[64,1792]{1,0:T(8,128)(2,1)S(1)} %get-tuple-element.39), channel_id=1, source_target_pairs={{0,14},{1,3},{2,4},{3,1},{4,2},{5,7},{6,8},{7,5},{8,6},{9,11},{10,... | collective-permute-start | bytes 688136 | tf_op jit(solution)/shard_map/ppermute | solution.py:28
  12.7 0.1 collective-permute-done.refs_5_.refs_7_
  12.8 0.3 collective-permute-done.1.refs_6_.refs_8_
  13.0 7.0 %collective-permute-start.2 = (bf16[64,1152]{1,0:T(8,128)(2,1)S(1)}, bf16[64,1152]{1,0:T(8,128)(2,1)S(1)}, u32[]{:S(2)}, u32[]{:S(2)}) collective-permute-start(bf16[64,1152]{1,0:T(8,128)(2,1)S(1)} %get-tuple-element.38), channel_id=1, source_target_pairs={{0,2},{1,15},{2,0},{3,5},{4,6},{5,3},{6,4},{7,9},{8,10},{9,7},{10,... | collective-permute-start | bytes 442376 | tf_op jit(solution)/shard_map/ppermute | solution.py:28
  20.1 3.6 %collective-permute-start.3 = (bf16[64,1152]{1,0:T(8,128)(2,1)S(1)}, bf16[64,1152]{1,0:T(8,128)(2,1)S(1)}, u32[]{:S(2)}, u32[]{:S(2)}) collective-permute-start(bf16[64,1152]{1,0:T(8,128)(2,1)S(1)} %get-tuple-element.38), channel_id=1, source_target_pairs={{0,14},{1,3},{2,4},{3,1},{4,2},{5,7},{6,8},{7,5},{8,6},{9,11},{10,... | collective-permute-start | bytes 442376 | tf_op jit(solution)/shard_map/ppermute | solution.py:28
  23.7 4.4 %chunk.3 = (f32[128,4096]{1,0:T(8,128)}, bf16[38,320,128]{2,1,0:T(8,128)(2,1)S(1)}, f32[3,2304,128]{2,1,0:T(8,128)S(1)}, f32[192,128]{1,0:T(8,128)S(1)}) custom-call(s32[40,1]{1,0:T(8,128)S(1)} %bitcast.13, s32[32,128]{1,0:T(8,128)S(1)} %get-tuple-element.30.refs_1_, ...), custom_call_target="tpu_custom_call", output_to_operand_aliasing={{2}: (9, {}), {3}: (10, {})} | custom-call | flops 1 | bytes 1 | tf_op jit(solution)/shard_map/chunk/pallas_call | solution.py:319
  28.1 0.0 collective-permute-done.4.refs_7_
  28.1 0.0 collective-permute-done.5.refs_8_
  28.1 4.9 %chunk.4 = (f32[128,4096]{1,0:T(8,128)}, bf16[38,320,128]{2,1,0:T(8,128)(2,1)S(1)}, f32[3,2304,128]{2,1,0:T(8,128)S(1)}, f32[192,128]{1,0:T(8,128)S(1)}) custom-call(s32[40,1]{1,0:T(8,128)S(1)} %bitcast.14, s32[32,128]{1,0:T(8,128)S(1)} %get-tuple-element.30.refs_1_, ...), custom_call_target="tpu_custom_call", output_to_operand_aliasing={{0}: (9, {}), {1}: (10, {}), {2}: (11, {}), {3}: (12, {})} | custom-call | flops 1 | bytes 1 | tf_op jit(solution)/shard_map/chunk/pallas_call | solution.py:319
  33.1 0.0 copy-start
  33.1 8.5 %chunk.5 = (f32[128,4096]{1,0:T(8,128)}, bf16[38,320,128]{2,1,0:T(8,128)(2,1)S(1)}, f32[3,2304,128]{2,1,0:T(8,128)S(1)}, f32[192,128]{1,0:T(8,128)S(1)}, f32[64,...) custom-call(s32[40,1]{1,0:T(8,128)S(1)} %bitcast.15, ...), custom_call_target="tpu_custom_call", output_to_operand_aliasing={{0}: (9, {}), {1}: (10, {}), {2}: (11, {}), {3}: (12, {})} | custom-call | flops 1 | bytes 1 | tf_op jit(solution)/shard_map/chunk/pallas_call | solution.py:319
  41.6 1.5 %collective-permute-start.7 = (f32[64,128]{1,0:T(8,128)S(1)}, f32[64,128]{1,0:T(8,128)S(1)}, u32[]{:S(2)}, u32[]{:S(2)}) collective-permute-start(f32[64,128]{1,0:T(8,128)S(1)} %get-tuple-element.53), channel_id=1, source_target_pairs={{0,14},{1,3},{2,4},{3,1},{4,2},{5,7},{6,8},{7,5},{8,6},{9,11},{10,... | collective-permute-start | bytes 98312 | tf_op jit(solution)/shard_map/ppermute | solution.py:28
  43.1 0.2 collective-permute-start.6
  43.3 1.6 %collective-permute-start.8 = (f32[64,128]{1,0:T(8,128)S(1)}, f32[64,128]{1,0:T(8,128)S(1)}, u32[]{:S(2)}, u32[]{:S(2)}) collective-permute-start(f32[64,128]{1,0:T(8,128)S(1)} %get-tuple-element.51.refs_0_), channel_id=1, source_target_pairs={{0,1},{1,0},{2,3},{3,2},{4,5},{5,4},{6,7},{7,6},{8,9},{9,8},{10,11... | collective-permute-start | bytes 98312 | tf_op jit(solution)/shard_map/ppermute | solution.py:404
  44.9 3.4 %collective-permute-done.7.refs_2_ = f32[64,128]{1,0:T(8,128)S(1)} collective-permute-done((f32[64,128]{1,0:T(8,128)S(1)}, f32[64,128]{1,0:T(8,128)S(1)}, u32[]{:S(2)}, u32[]{:S(2)}) %collective-permute-start.7) | collective-permute-done | bytes 32800 | tf_op jit(solution)/shard_map/ppermute | solution.py:28
  48.3 0.5 collective-permute-start.9
  48.8 0.7 %collective-permute-done.10.refs_5_ = f32[64,128]{1,0:T(8,128)S(1)} collective-permute-done((f32[64,128]{1,0:T(8,128)S(1)}, f32[64,128]{1,0:T(8,128)S(1)}, u32[]{:S(2)}, u32[]{:S(2)}) %collective-permute-start.10) | collective-permute-done | bytes 32800 | tf_op jit(solution)/shard_map/ppermute | solution.py:404
  49.5 0.2 collective-permute-done.9.refs_4_
  49.6 3.1 %solve.1 = f32[1,64]{1,0:T(1,128)} custom-call(f32[64,128]{1,0:T(8,128)S(1)} %get-tuple-element.51.refs_0_, f32[64,128]{1,0:T(8,128)S(1)} %collective-permute-done.6.refs_1_, f32[64,128]{1,0:T(8,128)S(1)} %collective-permute-done.7.refs_2_, f32[64,128]{1,0:T(8,128)S(1)} %collective-permute-done.8.refs_3_, f32[64,128]{1,0:T(8,128)S(1)} %collective-permute-done.9.refs_4_, ...), custom_call_target="tpu_custom_call" | custom-call | flops 1 | bytes 1 | tf_op jit(solution)/shard_map/solve/pallas_call | solution.py:393
  (6 shorter events, 0.0 us)
Async XLA Ops:
  1.9 10.9 %collective-permute-start = (bf16[64,1280]{1,0:T(8,128)(2,1)S(1)}, bf16[64,1280]{1,0:T(8,128)(2,1)S(1)}, u32[]{:S(2)}, u32[]{:S(2)}) collective-permute-start(bf16[64,1280]{1,0:T(8,128)(2,1)S(1)} %get-tuple-element.34), channel_id=1, source_target_pairs={{0,2},{1,15},{2,0},{3,5},{4,6},{5,3},{6,4},{7,9},{8,10},{9,7},{10,... | collective-permute-start | bytes 491528 | tf_op jit(solution)/shard_map/ppermute | solution.py:28
  4.9 8.1 %collective-permute-start.1 = (bf16[64,1280]{1,0:T(8,128)(2,1)S(1)}, bf16[64,1280]{1,0:T(8,128)(2,1)S(1)}, u32[]{:S(2)}, u32[]{:S(2)}) collective-permute-start(bf16[64,1280]{1,0:T(8,128)(2,1)S(1)} %get-tuple-element.35), channel_id=1, source_target_pairs={{0,14},{1,3},{2,4},{3,1},{4,2},{5,7},{6,8},{7,5},{8,6},{9,11},{10,... | collective-permute-start | bytes 491528 | tf_op jit(solution)/shard_map/ppermute | solution.py:28
  10.7 17.4 %collective-permute-start.4 = (bf16[64,1792]{1,0:T(8,128)(2,1)S(1)}, bf16[64,1792]{1,0:T(8,128)(2,1)S(1)}, u32[]{:S(2)}, u32[]{:S(2)}) collective-permute-start(bf16[64,1792]{1,0:T(8,128)(2,1)S(1)} %get-tuple-element.39), channel_id=1, source_target_pairs={{0,2},{1,15},{2,0},{3,5},{4,6},{5,3},{6,4},{7,9},{8,10},{9,7},{10,... | collective-permute-start | bytes 688136 | tf_op jit(solution)/shard_map/ppermute | solution.py:28
  10.8 17.3 %collective-permute-start.5 = (bf16[64,1792]{1,0:T(8,128)(2,1)S(1)}, bf16[64,1792]{1,0:T(8,128)(2,1)S(1)}, u32[]{:S(2)}, u32[]{:S(2)}) collective-permute-start(bf16[64,1792]{1,0:T(8,128)(2,1)S(1)} %get-tuple-element.39), channel_id=1, source_target_pairs={{0,14},{1,3},{2,4},{3,1},{4,2},{5,7},{6,8},{7,5},{8,6},{9,11},{10,... | collective-permute-start | bytes 688136 | tf_op jit(solution)/shard_map/ppermute | solution.py:28
  13.0 20.0 %collective-permute-start.2 = (bf16[64,1152]{1,0:T(8,128)(2,1)S(1)}, bf16[64,1152]{1,0:T(8,128)(2,1)S(1)}, u32[]{:S(2)}, u32[]{:S(2)}) collective-permute-start(bf16[64,1152]{1,0:T(8,128)(2,1)S(1)} %get-tuple-element.38), channel_id=1, source_target_pairs={{0,2},{1,15},{2,0},{3,5},{4,6},{5,3},{6,4},{7,9},{8,10},{9,7},{10,... | collective-permute-start | bytes 442376 | tf_op jit(solution)/shard_map/ppermute | solution.py:28
  20.1 13.0 %collective-permute-start.3 = (bf16[64,1152]{1,0:T(8,128)(2,1)S(1)}, bf16[64,1152]{1,0:T(8,128)(2,1)S(1)}, u32[]{:S(2)}, u32[]{:S(2)}) collective-permute-start(bf16[64,1152]{1,0:T(8,128)(2,1)S(1)} %get-tuple-element.38), channel_id=1, source_target_pairs={{0,14},{1,3},{2,4},{3,1},{4,2},{5,7},{6,8},{7,5},{8,6},{9,11},{10,... | collective-permute-start | bytes 442376 | tf_op jit(solution)/shard_map/ppermute | solution.py:28
  33.1 16.6 %copy-start = (f32[64]{0:T(128)S(1)}, f32[64]{0:T(128)}, u32[]{:S(2)}) copy-start(f32[64]{0:T(128)} %param.15) | copy-start | bytes 772
  41.6 6.7 %collective-permute-start.7 = (f32[64,128]{1,0:T(8,128)S(1)}, f32[64,128]{1,0:T(8,128)S(1)}, u32[]{:S(2)}, u32[]{:S(2)}) collective-permute-start(f32[64,128]{1,0:T(8,128)S(1)} %get-tuple-element.53), channel_id=1, source_target_pairs={{0,14},{1,3},{2,4},{3,1},{4,2},{5,7},{6,8},{7,5},{8,6},{9,11},{10,... | collective-permute-start | bytes 98312 | tf_op jit(solution)/shard_map/ppermute | solution.py:28
  43.1 5.2 %collective-permute-start.6 = (f32[64,128]{1,0:T(8,128)S(1)}, f32[64,128]{1,0:T(8,128)S(1)}, u32[]{:S(2)}, u32[]{:S(2)}) collective-permute-start(f32[64,128]{1,0:T(8,128)S(1)} %get-tuple-element.52), channel_id=1, source_target_pairs={{0,2},{1,15},{2,0},{3,5},{4,6},{5,3},{6,4},{7,9},{8,10},{9,7},{10,... | collective-permute-start | bytes 98312 | tf_op jit(solution)/shard_map/ppermute | solution.py:28
  43.3 5.5 %collective-permute-start.8 = (f32[64,128]{1,0:T(8,128)S(1)}, f32[64,128]{1,0:T(8,128)S(1)}, u32[]{:S(2)}, u32[]{:S(2)}) collective-permute-start(f32[64,128]{1,0:T(8,128)S(1)} %get-tuple-element.51.refs_0_), channel_id=1, source_target_pairs={{0,1},{1,0},{2,3},{3,2},{4,5},{5,4},{6,7},{7,6},{8,9},{9,8},{10,11... | collective-permute-start | bytes 98312 | tf_op jit(solution)/shard_map/ppermute | solution.py:404
  48.3 1.2 %collective-permute-start.10 = (f32[64,128]{1,0:T(8,128)S(1)}, f32[64,128]{1,0:T(8,128)S(1)}, u32[]{:S(2)}, u32[]{:S(2)}) collective-permute-start(f32[64,128]{1,0:T(8,128)S(1)} %collective-permute-done.7.refs_2_), channel_id=1, source_target_pairs={{0,1},{1,0},{2,3},{3,2},{4,5},{5,4},{6,7},{7,6},{8,9},{9,8},{10,11... | collective-permute-start | bytes 98312 | tf_op jit(solution)/shard_map/ppermute | solution.py:404
  48.3 1.4 %collective-permute-start.9 = (f32[64,128]{1,0:T(8,128)S(1)}, f32[64,128]{1,0:T(8,128)S(1)}, u32[]{:S(2)}, u32[]{:S(2)}) collective-permute-start(f32[64,128]{1,0:T(8,128)S(1)} %collective-permute-done.6.refs_1_), channel_id=1, source_target_pairs={{0,1},{1,0},{2,3},{3,2},{4,5},{5,4},{6,7},{7,6},{8,9},{9,8},{10,11... | collective-permute-start | bytes 98312 | tf_op jit(solution)/shard_map/ppermute | solution.py:404

commit v8 on v7

--- a/solution.py
+++ b/solution.py
@@ -10,6 +10,8 @@
 LANES = 128
 ROWS = 16
 HALF = 8
+HERE = 1
+AWAY = (0, 2)
 PIECE = 512
 BLOCK = 512
 WIDTHS = (9, 14, 9)
@@ -179,6 +181,77 @@
         target[k, offset : offset + ROWS, lane] = both * jnp.where(upper, rows[m : m + 1, :], rows[m + 1 : m + 2, :])
 
 
+def contracted(cols, projected, moment, k):
+    levels = cols.shape[0]
+    _, _, spans, _ = pair_rows(levels)
+    lane = iota((levels, LANES), 1)
+    gradient = jnp.sum(cols * projected, axis=1, keepdims=True)
+    result = jnp.where(lane == levels, gradient, 0.0)
+    columns = {}
+    for m, low, offset, size in spans:
+        scaled = cols[low : low + size, :] * cols[m : m + 1, :]
+        column = jnp.sum(moment[k, offset : offset + size, :] * scaled, axis=1, keepdims=True)
+        columns.setdefault(m, []).append((low, column))
+    for m, found in columns.items():
+        found = sorted(found, key=lambda part: part[0])
+        low = found[0][0]
+        stack = [column for _, column in found]
+        if low:
+            stack = [jnp.zeros((low, 1), jnp.float32), *stack]
+        result = jnp.where(lane == m, jnp.concatenate(stack, axis=0) if len(stack) > 1 else stack[0], result)
+    return result
+
+
+def finish_kernel(base_ref, cols_ref, packed, projected, out_ref, pairs, weights, moment, *, groups):
+    levels = cols_ref.shape[0]
+    high = 3 * levels
+    parts = BLOCK // LANES
+    moment[...] = jnp.zeros_like(moment)
+
+    def one_block(block, parts):
+        wide = parts * LANES
+        for p in range(parts):
+            lane = slice(p * LANES, (p + 1) * LANES)
+            weights[:, lane] = packed[block + p, high:, :]
+            fill_pairs(pairs, 0, lane, packed[block + p, HERE * levels : (HERE + 1) * levels, :])
+        moment[0] += nt_dot(pairs[0, :, :wide], weights[:, :wide])
+
+    count = base_ref[groups, 0]
+    ready = count // BLOCK
+    lax.fori_loop(0, ready, lambda block, carry: (one_block(block * parts, parts), carry)[1], 0)
+    left = count - ready * BLOCK
+
+    @pl.when(left > BLOCK // 2)
+    def _():
+        one_block(ready * parts, parts)
+
+    @pl.when((left > 0) & (left <= BLOCK // 2))
+    def _():
+        one_block(ready * parts, parts // 2)
+
+    cols = cols_ref[...].astype(jnp.float32)
+    out_ref[...] = contracted(cols, projected[HERE * levels : (HERE + 1) * levels, :], moment, 0)
+
+
+def finish(base, cols, packed, projected, groups):
+    levels, rays = cols.shape
+    _, _, _, pair_count = pair_rows(levels)
+    vmem = pl.BlockSpec(memory_space=pltpu.VMEM)
+    return pl.pallas_call(
+        functools.partial(finish_kernel, groups=groups),
+        in_specs=[pl.BlockSpec(memory_space=pltpu.SMEM), vmem, vmem, vmem],
+        out_shape=jax.ShapeDtypeStruct((levels, LANES), jnp.float32),
+        scratch_shapes=[
+            pltpu.VMEM((1, pair_count, BLOCK), jnp.bfloat16),
+            pltpu.VMEM((rays, BLOCK), jnp.bfloat16),
+            pltpu.VMEM((1, pair_count, rays), jnp.float32),
+        ],
+        compiler_params=pltpu.CompilerParams(vmem_limit_bytes=CHUNK_BYTES),
+        cost_estimate=CHEAP,
+        name="finish",
+    )(base, cols, packed, projected)
+
+
 def chunk_kernel(*refs, spans_of, carrier, opens, closes):
     base_ref, place_ref, here_ref, measured_ref, cols_ref, carried_before, carried_after = refs[:7]
     refs = refs[7:]
@@ -190,8 +263,8 @@
     spectrum_ref, packed, moment, projected = refs[:4]
     refs = refs[4:]
     if closes:
-        terms_refs = refs[:3]
-        refs = refs[3:]
+        terms_refs = refs[:2]
+        refs = refs[2:]
     table, modelled, pairs, weights, sems = refs
     levels = here_ref.shape[0]
     rays = measured_ref.shape[0]
@@ -239,9 +312,9 @@
         for p in range(parts):
             lane = slice(p * LANES, (p + 1) * LANES)
             weights[:, lane] = packed[block + p, high:, :]
-            for k in range(3):
+            for k in AWAY:
                 fill_pairs(pairs, k, lane, packed[block + p, k * levels : (k + 1) * levels, :])
-        for k in range(3):
+        for k in AWAY:
             moment[k] += nt_dot(pairs[k, :, :wide], weights[:, :wide])
 
     parts = BLOCK // LANES
@@ -255,25 +328,6 @@
         for d in range(2, parts + 1):
             packed[last + d] = jnp.zeros(packed.shape[1:], packed.dtype)
         left = count - ready * BLOCK
-        lane = iota((levels, LANES), 1)
-
-        def contract(k):
-            gradient = jnp.sum(cols[k] * projected[k * levels : (k + 1) * levels, :], axis=1, keepdims=True)
-            result = jnp.where(lane == levels, gradient, 0.0)
-            columns = {}
-            for m, low, offset, size in spans:
-                scaled = cols[k][low : low + size, :] * cols[k][m : m + 1, :]
-                column = jnp.sum(moment[k, offset : offset + size, :] * scaled, axis=1, keepdims=True)
-                columns.setdefault(m, []).append((low, column))
-            for m, parts_of in columns.items():
-                parts_of = sorted(parts_of, key=lambda part: part[0])
-                low = parts_of[0][0]
-                stack = [column for _, column in parts_of]
-                if low:
-                    stack = [jnp.zeros((low, 1), jnp.float32), *stack]
-                result = jnp.where(lane == m, jnp.concatenate(stack, axis=0) if len(stack) > 1 else stack[0], result)
-            terms_refs[k][...] = result
-
         @pl.when(left > BLOCK // 2)
         def _():
             one_block(ready * parts, parts)
@@ -282,8 +336,8 @@
         def _():
             one_block(ready * parts, parts // 2)
 
-        for k in range(3):
-            contract(k)
+        for terms_ref, k in zip(terms_refs, AWAY, strict=True):
+            terms_ref[...] = contracted(cols[k], projected[k * levels : (k + 1) * levels, :], moment, k)
     for copy in copies:
         copy.wait()
 
@@ -314,8 +368,8 @@
     ]
     out_specs = [hbm, vmem, vmem, vmem]
     if closes:
-        shapes += [jax.ShapeDtypeStruct((levels, LANES), jnp.float32)] * 3
-        out_specs += [vmem] * 3
+        shapes += [jax.ShapeDtypeStruct((levels, LANES), jnp.float32)] * 2
+        out_specs += [vmem] * 2
     outs = pl.pallas_call(
         functools.partial(chunk_kernel, spans_of=spans_of, carrier=carrier, opens=opens, closes=closes),
         in_specs=specs,
@@ -431,7 +485,8 @@
             base, place, table_here, measured_here, cols, received[0], widths[0], (span,), [received[c]], state, closes
         )
     spectrum = state[0]
-    mine = (terms[1], traded(terms[0], 0), traded(terms[2], 1))
+    arriving = (traded(terms[0], 0), traded(terms[1], 1))
+    mine = (finish(base, cols, state[1], state[3], points // LANES), *arriving)
     others = tuple(swapped(part, "spec") for part in mine)
     scale = 1.0 / (rays * points * lax.axis_size("spec"))
     state_step = solve(mine + others, prior_weight[None, :], scale)

time: 53.6 us -> 52.8 us (0.985)
  waiting for transfers between devices: 4.64 us -> 1.37 us
  Pallas kernels: 24.4 us -> 27.5 us
  starting transfers between devices: 23 us -> 22.3 us
    pallas_call x0 -> x1, Pallas kernels: none -> 5.39 us  [finish(): pl.pallas_call(functools.partial(finish_kernel, groups=groups), in_specs=...]
    ppermute x8, waiting for transfers between devices: 3.78 us -> 0.37 us  [traded(): return lax.ppermute(block, ('sector', 'spec'), route)]
    pallas_call x3, Pallas kernels: 17.8 us -> 15.5 us  [chunk(): pl.pallas_call(functools.partial(chunk_kernel, spans_of=spans_of, carrier...]
    ppermute x3, starting transfers between devices: 2.09 us -> 0.78 us  [swapped(): return lax.ppermute(block, axis, [(i, size - 1 - i) for i in range(size)])]
    ppermute x8, starting transfers between devices: 20.9 us -> 21.6 us  [traded(): return lax.ppermute(block, ('sector', 'spec'), route)]
  transfers between devices with their start and end apart: 11 -> 11, of which waited for: 5 -> 5; matrix products, arithmetic and copies ran while one was open for 0% -> 0% of each run, Pallas kernels for 22% -> 30%
where the time goes in v8:
time: 52.8 us; the launch traced here: 51.9 us
  Pallas kernels  27.5 us (52%)
  starting transfers between devices  22.3 us (42%)
  waiting for transfers between devices  1.37 us (3%)
  between operations  0.74 us (1%)
    ppermute x8, starting transfers between devices, traded(): return lax.ppermute(block, ('sector', 'spec'), route)  21.6 us
    pallas_call x3, Pallas kernels, chunk(): pl.pallas_call(functools.partial(chunk_kernel, spans_of=spans_of, carrier...  15.5 us
    pallas_call x1, Pallas kernels, finish(): pl.pallas_call(functools.partial(finish_kernel, groups=groups), in_specs=...  5.39 us
    pallas_call x1, Pallas kernels, solve(): pl.pallas_call(functools.partial(solve_kernel, scale=scale), out_shape=ja...  3.08 us
    pallas_call x1, Pallas kernels, stage(): pl.pallas_call(functools.partial(stage_kernel, firsts=firsts), in_specs=[...  2.24 us
    pallas_call x1, Pallas kernels, prepare(): pl.pallas_call(functools.partial(prepare_kernel, first=first, width=width...  1.25 us
  transfers between devices with their start and end apart: 11, of which 5 were waited for; matrix products, arithmetic and copies ran while one was open for 0% of the time, Pallas kernels for 30%

profile of v8, /device:TPU:0, one launch (start us, length us, event | category | flops | bytes accessed | tf_op | source)
XLA Modules:
  0.0 51.9 jit_solution(8870848182194682948)
XLA Ops:
  0.6 1.2 %prepare.1 = (bf16[64,1280]{1,0:T(8,128)(2,1)S(1)}, bf16[64,1280]{1,0:T(8,128)(2,1)S(1)}, bf16[64,128]{1,0:T(8,128)(2,1)S(1)}) custom-call(s32[3,32,128]{2,1,0:T(8,128)} %bitcast.22, s32[3,1,128]{2,1,0:T(1,128)} %bitcast.25, f32[3,32,128]{2,1,0:T(8,128)} %bitcast.23, f32[1,64]{1,0:T(1,128)} %absorber_hbm.1, bf16[64,4096]{1,0:T(8,128)(2,1)} %bitcast.20), custom_call_target="tpu_custom_call" | custom-call | flops 1 | bytes 1 | tf_op jit(solution)/shard_map/prepare/pallas_call | solution.py:83
  1.9 3.0 %collective-permute-start = (bf16[64,1280]{1,0:T(8,128)(2,1)S(1)}, bf16[64,1280]{1,0:T(8,128)(2,1)S(1)}, u32[]{:S(2)}, u32[]{:S(2)}) collective-permute-start(bf16[64,1280]{1,0:T(8,128)(2,1)S(1)} %get-tuple-element.35), channel_id=1, source_target_pairs={{0,2},{1,15},{2,0},{3,5},{4,6},{5,3},{6,4},{7,9},{8,10},{9,7},{10,... | collective-permute-start | bytes 491528 | tf_op jit(solution)/shard_map/ppermute | solution.py:30
  4.9 3.5 %collective-permute-start.1 = (bf16[64,1280]{1,0:T(8,128)(2,1)S(1)}, bf16[64,1280]{1,0:T(8,128)(2,1)S(1)}, u32[]{:S(2)}, u32[]{:S(2)}) collective-permute-start(bf16[64,1280]{1,0:T(8,128)(2,1)S(1)} %get-tuple-element.36), channel_id=1, source_target_pairs={{0,14},{1,3},{2,4},{3,1},{4,2},{5,7},{6,8},{7,5},{8,6},{9,11},{10,... | collective-permute-start | bytes 491528 | tf_op jit(solution)/shard_map/ppermute | solution.py:30
  8.5 2.2 %stage.1 = (s32[32,128]{1,0:T(8,128)S(1)}, s32[40,128]{1,0:T(8,128)S(1)}, bf16[64,4096]{1,0:T(8,128)(2,1)S(1)}, f32[128,4096]{1,0:T(8,128)S(1)}, bf16[64,1792]{1...) custom-call(bf16[64,128]{1,0:T(8,128)(2,1)S(1)} %get-tuple-element.29.cols_r, ...), custom_call_target="tpu_custom_call" | custom-call | flops 1 | bytes 1 | tf_op jit(solution)/shard_map/stage/pallas_call | solution.py:131
  10.7 0.1 collective-permute-start.4
  10.8 1.9 %collective-permute-start.5 = (bf16[64,1792]{1,0:T(8,128)(2,1)S(1)}, bf16[64,1792]{1,0:T(8,128)(2,1)S(1)}, u32[]{:S(2)}, u32[]{:S(2)}) collective-permute-start(bf16[64,1792]{1,0:T(8,128)(2,1)S(1)} %get-tuple-element.40), channel_id=1, source_target_pairs={{0,14},{1,3},{2,4},{3,1},{4,2},{5,7},{6,8},{7,5},{8,6},{9,11},{10,... | collective-permute-start | bytes 688136 | tf_op jit(solution)/shard_map/ppermute | solution.py:30
  12.7 0.1 collective-permute-done.refs_5_.refs_7_
  12.8 0.3 collective-permute-done.1.refs_6_.refs_8_
  13.0 7.0 %collective-permute-start.2 = (bf16[64,1152]{1,0:T(8,128)(2,1)S(1)}, bf16[64,1152]{1,0:T(8,128)(2,1)S(1)}, u32[]{:S(2)}, u32[]{:S(2)}) collective-permute-start(bf16[64,1152]{1,0:T(8,128)(2,1)S(1)} %get-tuple-element.39), channel_id=1, source_target_pairs={{0,2},{1,15},{2,0},{3,5},{4,6},{5,3},{6,4},{7,9},{8,10},{9,7},{10,... | collective-permute-start | bytes 442376 | tf_op jit(solution)/shard_map/ppermute | solution.py:30
  20.1 3.6 %collective-permute-start.3 = (bf16[64,1152]{1,0:T(8,128)(2,1)S(1)}, bf16[64,1152]{1,0:T(8,128)(2,1)S(1)}, u32[]{:S(2)}, u32[]{:S(2)}) collective-permute-start(bf16[64,1152]{1,0:T(8,128)(2,1)S(1)} %get-tuple-element.39), channel_id=1, source_target_pairs={{0,14},{1,3},{2,4},{3,1},{4,2},{5,7},{6,8},{7,5},{8,6},{9,11},{10,... | collective-permute-start | bytes 442376 | tf_op jit(solution)/shard_map/ppermute | solution.py:30
  23.7 3.7 %chunk.3 = (f32[128,4096]{1,0:T(8,128)}, bf16[38,320,128]{2,1,0:T(8,128)(2,1)S(1)}, f32[3,2304,128]{2,1,0:T(8,128)S(1)}, f32[192,128]{1,0:T(8,128)S(1)}) custom-call(s32[40,1]{1,0:T(8,128)S(1)} %bitcast.13, s32[32,128]{1,0:T(8,128)S(1)} %get-tuple-element.31.refs_1_, ...), custom_call_target="tpu_custom_call", output_to_operand_aliasing={{2}: (9, {}), {3}: (10, {})} | custom-call | flops 1 | bytes 1 | tf_op jit(solution)/shard_map/chunk/pallas_call | solution.py:373
  27.5 4.2 %chunk.4 = (f32[128,4096]{1,0:T(8,128)}, bf16[38,320,128]{2,1,0:T(8,128)(2,1)S(1)}, f32[3,2304,128]{2,1,0:T(8,128)S(1)}, f32[192,128]{1,0:T(8,128)S(1)}) custom-call(s32[40,1]{1,0:T(8,128)S(1)} %bitcast.14, s32[32,128]{1,0:T(8,128)S(1)} %get-tuple-element.31.refs_1_, ...), custom_call_target="tpu_custom_call", output_to_operand_aliasing={{0}: (9, {}), {1}: (10, {}), {2}: (11, {}), {3}: (12, {})} | custom-call | flops 1 | bytes 1 | tf_op jit(solution)/shard_map/chunk/pallas_call | solution.py:373
  31.8 7.5 %chunk.5 = (f32[128,4096]{1,0:T(8,128)}, bf16[38,320,128]{2,1,0:T(8,128)(2,1)S(1)}, f32[3,2304,128]{2,1,0:T(8,128)S(1)}, f32[192,128]{1,0:T(8,128)S(1)}, f32[64,128]{1,0:T(8,128)S(1)}, /*index=5*/f32[64,128]{1,0:T(8,128)S(1)}) custom-call(s32[40,1]{1,0:T(8,128)S(1)} %bitcast.15, ...), custom_call_target="tpu_custom_call", output_to_operand_aliasing={{0}: (9, {}), {1}: (10, {}), {2}: (11, {}), {3}: (12, {})} | custom-call | flops 1 | bytes 1 | tf_op jit(solution)/shard_map/chunk/pallas_call | solution.py:373
  39.3 0.0 copy-start
  39.3 2.1 %collective-permute-start.7 = (f32[64,128]{1,0:T(8,128)S(1)}, f32[64,128]{1,0:T(8,128)S(1)}, u32[]{:S(2)}, u32[]{:S(2)}) collective-permute-start(f32[64,128]{1,0:T(8,128)S(1)} %get-tuple-element.55), channel_id=1, source_target_pairs={{0,14},{1,3},{2,4},{3,1},{4,2},{5,7},{6,8},{7,5},{8,6},{9,11},{10,... | collective-permute-start | bytes 98312 | tf_op jit(solution)/shard_map/ppermute | solution.py:30
  41.4 0.2 collective-permute-start.6
  41.6 5.4 %finish.1.refs_0_ = f32[64,128]{1,0:T(8,128)S(1)} custom-call(s32[40,1]{1,0:T(8,128)S(1)} %bitcast.16, bf16[64,128]{1,0:T(8,128)(2,1)S(1)} %get-tuple-element.29.cols_ref.refs_4_, bf16[38,320,128]{2,1,0:T(8,128)(2,1)S(1)} %get-tuple-element.52.packed, f32[192,128]{1,0:T(8,128)S(1)} %get-tuple-element.53.projected), custom_call_target="tpu_custom_call" | custom-call | flops 1 | bytes 1 | tf_op jit(solution)/shard_map/finish/pallas_call | solution.py:240
  47.0 0.3 collective-permute-start.8
  47.3 0.3 collective-permute-start.10
  47.6 0.2 collective-permute-start.9
  47.8 0.5 collective-permute-done.8.refs_3_
  48.3 0.2 collective-permute-done.10.refs_5_
  48.5 0.3 collective-permute-done.9.refs_4_
  48.8 3.1 %solve.1 = f32[1,64]{1,0:T(1,128)} custom-call(f32[64,128]{1,0:T(8,128)S(1)} %finish.1.refs_0_, f32[64,128]{1,0:T(8,128)S(1)} %collective-permute-done.6.refs_1_, f32[64,128]{1,0:T(8,128)S(1)} %collective-permute-done.7.refs_2_, f32[64,128]{1,0:T(8,128)S(1)} %collective-permute-done.8.refs_3_, f32[64,128]{1,0:T(8,128)S(1)} %collective-permute-done.9.refs_4_, ...), custom_call_target="tpu_custom_call" | custom-call | flops 1 | bytes 1 | tf_op jit(solution)/shard_map/solve/pallas_call | solution.py:447
  (7 shorter events, 0.0 us)
Async XLA Ops:
  1.9 10.9 %collective-permute-start = (bf16[64,1280]{1,0:T(8,128)(2,1)S(1)}, bf16[64,1280]{1,0:T(8,128)(2,1)S(1)}, u32[]{:S(2)}, u32[]{:S(2)}) collective-permute-start(bf16[64,1280]{1,0:T(8,128)(2,1)S(1)} %get-tuple-element.35), channel_id=1, source_target_pairs={{0,2},{1,15},{2,0},{3,5},{4,6},{5,3},{6,4},{7,9},{8,10},{9,7},{10,... | collective-permute-start | bytes 491528 | tf_op jit(solution)/shard_map/ppermute | solution.py:30
  4.9 8.1 %collective-permute-start.1 = (bf16[64,1280]{1,0:T(8,128)(2,1)S(1)}, bf16[64,1280]{1,0:T(8,128)(2,1)S(1)}, u32[]{:S(2)}, u32[]{:S(2)}) collective-permute-start(bf16[64,1280]{1,0:T(8,128)(2,1)S(1)} %get-tuple-element.36), channel_id=1, source_target_pairs={{0,14},{1,3},{2,4},{3,1},{4,2},{5,7},{6,8},{7,5},{8,6},{9,11},{10,... | collective-permute-start | bytes 491528 | tf_op jit(solution)/shard_map/ppermute | solution.py:30
  10.7 16.8 %collective-permute-start.4 = (bf16[64,1792]{1,0:T(8,128)(2,1)S(1)}, bf16[64,1792]{1,0:T(8,128)(2,1)S(1)}, u32[]{:S(2)}, u32[]{:S(2)}) collective-permute-start(bf16[64,1792]{1,0:T(8,128)(2,1)S(1)} %get-tuple-element.40), channel_id=1, source_target_pairs={{0,2},{1,15},{2,0},{3,5},{4,6},{5,3},{6,4},{7,9},{8,10},{9,7},{10,... | collective-permute-start | bytes 688136 | tf_op jit(solution)/shard_map/ppermute | solution.py:30
  10.8 16.7 %collective-permute-start.5 = (bf16[64,1792]{1,0:T(8,128)(2,1)S(1)}, bf16[64,1792]{1,0:T(8,128)(2,1)S(1)}, u32[]{:S(2)}, u32[]{:S(2)}) collective-permute-start(bf16[64,1792]{1,0:T(8,128)(2,1)S(1)} %get-tuple-element.40), channel_id=1, source_target_pairs={{0,14},{1,3},{2,4},{3,1},{4,2},{5,7},{6,8},{7,5},{8,6},{9,11},{10,... | collective-permute-start | bytes 688136 | tf_op jit(solution)/shard_map/ppermute | solution.py:30
  13.0 18.7 %collective-permute-start.2 = (bf16[64,1152]{1,0:T(8,128)(2,1)S(1)}, bf16[64,1152]{1,0:T(8,128)(2,1)S(1)}, u32[]{:S(2)}, u32[]{:S(2)}) collective-permute-start(bf16[64,1152]{1,0:T(8,128)(2,1)S(1)} %get-tuple-element.39), channel_id=1, source_target_pairs={{0,2},{1,15},{2,0},{3,5},{4,6},{5,3},{6,4},{7,9},{8,10},{9,7},{10,... | collective-permute-start | bytes 442376 | tf_op jit(solution)/shard_map/ppermute | solution.py:30
  20.1 11.7 %collective-permute-start.3 = (bf16[64,1152]{1,0:T(8,128)(2,1)S(1)}, bf16[64,1152]{1,0:T(8,128)(2,1)S(1)}, u32[]{:S(2)}, u32[]{:S(2)}) collective-permute-start(bf16[64,1152]{1,0:T(8,128)(2,1)S(1)} %get-tuple-element.39), channel_id=1, source_target_pairs={{0,14},{1,3},{2,4},{3,1},{4,2},{5,7},{6,8},{7,5},{8,6},{9,11},{10,... | collective-permute-start | bytes 442376 | tf_op jit(solution)/shard_map/ppermute | solution.py:30
  39.3 9.5 %copy-start = (f32[64]{0:T(128)S(1)}, f32[64]{0:T(128)}, u32[]{:S(2)}) copy-start(f32[64]{0:T(128)} %param.15) | copy-start | bytes 772
  39.3 8.0 %collective-permute-start.7 = (f32[64,128]{1,0:T(8,128)S(1)}, f32[64,128]{1,0:T(8,128)S(1)}, u32[]{:S(2)}, u32[]{:S(2)}) collective-permute-start(f32[64,128]{1,0:T(8,128)S(1)} %get-tuple-element.55), channel_id=1, source_target_pairs={{0,14},{1,3},{2,4},{3,1},{4,2},{5,7},{6,8},{7,5},{8,6},{9,11},{10,... | collective-permute-start | bytes 98312 | tf_op jit(solution)/shard_map/ppermute | solution.py:30
  41.4 6.2 %collective-permute-start.6 = (f32[64,128]{1,0:T(8,128)S(1)}, f32[64,128]{1,0:T(8,128)S(1)}, u32[]{:S(2)}, u32[]{:S(2)}) collective-permute-start(f32[64,128]{1,0:T(8,128)S(1)} %get-tuple-element.54), channel_id=1, source_target_pairs={{0,2},{1,15},{2,0},{3,5},{4,6},{5,3},{6,4},{7,9},{8,10},{9,7},{10,... | collective-permute-start | bytes 98312 | tf_op jit(solution)/shard_map/ppermute | solution.py:30
  47.0 1.3 %collective-permute-start.8 = (f32[64,128]{1,0:T(8,128)S(1)}, f32[64,128]{1,0:T(8,128)S(1)}, u32[]{:S(2)}, u32[]{:S(2)}) collective-permute-start(f32[64,128]{1,0:T(8,128)S(1)} %finish.1.refs_0_), channel_id=1, source_target_pairs={{0,1},{1,0},{2,3},{3,2},{4,5},{5,4},{6,7},{7,6},{8,9},{9,8},{10,11... | collective-permute-start | bytes 98312 | tf_op jit(solution)/shard_map/ppermute | solution.py:458
  47.3 1.2 %collective-permute-start.10 = (f32[64,128]{1,0:T(8,128)S(1)}, f32[64,128]{1,0:T(8,128)S(1)}, u32[]{:S(2)}, u32[]{:S(2)}) collective-permute-start(f32[64,128]{1,0:T(8,128)S(1)} %collective-permute-done.7.refs_2_), channel_id=1, source_target_pairs={{0,1},{1,0},{2,3},{3,2},{4,5},{5,4},{6,7},{7,6},{8,9},{9,8},{10,11... | collective-permute-start | bytes 98312 | tf_op jit(solution)/shard_map/ppermute | solution.py:458
  47.6 1.2 %collective-permute-start.9 = (f32[64,128]{1,0:T(8,128)S(1)}, f32[64,128]{1,0:T(8,128)S(1)}, u32[]{:S(2)}, u32[]{:S(2)}) collective-permute-start(f32[64,128]{1,0:T(8,128)S(1)} %collective-permute-done.6.refs_1_), channel_id=1, source_target_pairs={{0,1},{1,0},{2,3},{3,2},{4,5},{5,4},{6,7},{7,6},{8,9},{9,8},{10,11... | collective-permute-start | bytes 98312 | tf_op jit(solution)/shard_map/ppermute | solution.py:458

commit v9 on v8

--- a/solution.py
+++ b/solution.py
@@ -202,11 +202,11 @@
     return result
 
 
-def finish_kernel(base_ref, cols_ref, packed, projected, out_ref, pairs, weights, moment, *, groups):
+def finish_kernel(base_ref, cols_ref, packed, projected, earlier, out_ref, pairs, weights, moment, *, opened, groups):
     levels = cols_ref.shape[0]
     high = 3 * levels
     parts = BLOCK // LANES
-    moment[...] = jnp.zeros_like(moment)
+    moment[0] = earlier[HERE]
 
     def one_block(block, parts):
         wide = parts * LANES
@@ -218,7 +218,7 @@
 
     count = base_ref[groups, 0]
     ready = count // BLOCK
-    lax.fori_loop(0, ready, lambda block, carry: (one_block(block * parts, parts), carry)[1], 0)
+    lax.fori_loop(base_ref[opened, 0] // BLOCK, ready, lambda block, carry: (one_block(block * parts, parts), carry)[1], 0)
     left = count - ready * BLOCK
 
     @pl.when(left > BLOCK // 2)
@@ -233,13 +233,13 @@
     out_ref[...] = contracted(cols, projected[HERE * levels : (HERE + 1) * levels, :], moment, 0)
 
 
-def finish(base, cols, packed, projected, groups):
+def finish(base, cols, packed, projected, moment, opened, groups):
     levels, rays = cols.shape
     _, _, _, pair_count = pair_rows(levels)
     vmem = pl.BlockSpec(memory_space=pltpu.VMEM)
     return pl.pallas_call(
-        functools.partial(finish_kernel, groups=groups),
-        in_specs=[pl.BlockSpec(memory_space=pltpu.SMEM), vmem, vmem, vmem],
+        functools.partial(finish_kernel, opened=opened, groups=groups),
+        in_specs=[pl.BlockSpec(memory_space=pltpu.SMEM), vmem, vmem, vmem, vmem],
         out_shape=jax.ShapeDtypeStruct((levels, LANES), jnp.float32),
         scratch_shapes=[
             pltpu.VMEM((1, pair_count, BLOCK), jnp.bfloat16),
@@ -249,7 +249,7 @@
         compiler_params=pltpu.CompilerParams(vmem_limit_bytes=CHUNK_BYTES),
         cost_estimate=CHEAP,
         name="finish",
-    )(base, cols, packed, projected)
+    )(base, cols, packed, projected, moment)
 
 
 def chunk_kernel(*refs, spans_of, carrier, opens, closes):
@@ -278,6 +278,7 @@
     if opens:
         packed[0] = jnp.zeros(packed.shape[1:], packed.dtype)
 
+    kinds = range(3) if opens else AWAY
     copies = []
     for (first, width), (before_ref, after_ref) in zip(spans_of, sources, strict=True):
         for low_lane in range(0, width, PIECE):
@@ -312,9 +313,9 @@
         for p in range(parts):
             lane = slice(p * LANES, (p + 1) * LANES)
             weights[:, lane] = packed[block + p, high:, :]
-            for k in AWAY:
+            for k in kinds:
                 fill_pairs(pairs, k, lane, packed[block + p, k * levels : (k + 1) * levels, :])
-        for k in AWAY:
+        for k in kinds:
             moment[k] += nt_dot(pairs[k, :, :wide], weights[:, :wide])
 
     parts = BLOCK // LANES
@@ -486,7 +487,7 @@
         )
     spectrum = state[0]
     arriving = (traded(terms[0], 0), traded(terms[1], 1))
-    mine = (finish(base, cols, state[1], state[3], points // LANES), *arriving)
+    mine = (finish(base, cols, state[1], state[3], state[2], widths[0] // LANES, points // LANES), *arriving)
     others = tuple(swapped(part, "spec") for part in mine)
     scale = 1.0 / (rays * points * lax.axis_size("spec"))
     state_step = solve(mine + others, prior_weight[None, :], scale)

time: 52.8 us -> 52 us (0.985); the launches traced: 51.9 us -> 52.3 us
  starting transfers between devices: 22.3 us -> 24.4 us
  Pallas kernels: 27.5 us -> 25.9 us
    ppermute x3, starting transfers between devices: 0.78 us -> 3.54 us  [swapped(): return lax.ppermute(block, axis, [(i, size - 1 - i) for i in range(size)])]
    pallas_call x1, Pallas kernels: 5.39 us -> 4.07 us  [finish(): pl.pallas_call(functools.partial(finish_kernel, opened=opened, groups=gro...]
    ppermute x8, starting transfers between devices: 21.6 us -> 20.9 us  [traded(): return lax.ppermute(block, ('sector', 'spec'), route)]
  transfers between devices with their start and end apart: 11 -> 11, of which waited for: 5 -> 5; matrix products, arithmetic and copies ran while one was open for 0% -> 0% of each run, Pallas kernels for 30% -> 29%
where the time goes in v9:
time: 52 us; the launch traced here: 52.3 us
  Pallas kernels  25.9 us (50%)
  starting transfers between devices  24.4 us (47%)
  waiting for transfers between devices  1.23 us (2%)
  between operations  0.73 us (1%)
    ppermute x8, starting transfers between devices, traded(): return lax.ppermute(block, ('sector', 'spec'), route)  20.9 us
    pallas_call x3, Pallas kernels, chunk(): pl.pallas_call(functools.partial(chunk_kernel, spans_of=spans_of, carrier...  15.3 us
    pallas_call x1, Pallas kernels, finish(): pl.pallas_call(functools.partial(finish_kernel, opened=opened, groups=gro...  4.07 us
    ppermute x3, starting transfers between devices, swapped(): return lax.ppermute(block, axis, [(i, size - 1 - i) for i in range(size)])  3.54 us
    pallas_call x1, Pallas kernels, solve(): pl.pallas_call(functools.partial(solve_kernel, scale=scale), out_shape=ja...  3.09 us
    pallas_call x1, Pallas kernels, stage(): pl.pallas_call(functools.partial(stage_kernel, firsts=firsts), in_specs=[...  2.24 us
    pallas_call x1, Pallas kernels, prepare(): pl.pallas_call(functools.partial(prepare_kernel, first=first, width=width...  1.25 us
  transfers between devices with their start and end apart: 11, of which 5 were waited for; matrix products, arithmetic and copies ran while one was open for 0% of the time, Pallas kernels for 29%

profile of v9, /device:TPU:0, one launch (start us, length us, event | category | flops | bytes accessed | tf_op | source)
XLA Modules:
  0.0 52.3 jit_solution(4134299567410188757)
XLA Ops:
  0.6 1.2 %prepare.1 = (bf16[64,1280]{1,0:T(8,128)(2,1)S(1)}, bf16[64,1280]{1,0:T(8,128)(2,1)S(1)}, bf16[64,128]{1,0:T(8,128)(2,1)S(1)}) custom-call(s32[3,32,128]{2,1,0:T(8,128)} %bitcast.22, s32[3,1,128]{2,1,0:T(1,128)} %bitcast.25, f32[3,32,128]{2,1,0:T(8,128)} %bitcast.23, f32[1,64]{1,0:T(1,128)} %absorber_hbm.1, bf16[64,4096]{1,0:T(8,128)(2,1)} %bitcast.20), custom_call_target="tpu_custom_call" | custom-call | flops 1 | bytes 1 | tf_op jit(solution)/shard_map/prepare/pallas_call | solution.py:83
  1.9 3.0 %collective-permute-start = (bf16[64,1280]{1,0:T(8,128)(2,1)S(1)}, bf16[64,1280]{1,0:T(8,128)(2,1)S(1)}, u32[]{:S(2)}, u32[]{:S(2)}) collective-permute-start(bf16[64,1280]{1,0:T(8,128)(2,1)S(1)} %get-tuple-element.36), channel_id=1, source_target_pairs={{0,2},{1,15},{2,0},{3,5},{4,6},{5,3},{6,4},{7,9},{8,10},{9,7},{10,... | collective-permute-start | bytes 491528 | tf_op jit(solution)/shard_map/ppermute | solution.py:30
  4.9 3.5 %collective-permute-start.1 = (bf16[64,1280]{1,0:T(8,128)(2,1)S(1)}, bf16[64,1280]{1,0:T(8,128)(2,1)S(1)}, u32[]{:S(2)}, u32[]{:S(2)}) collective-permute-start(bf16[64,1280]{1,0:T(8,128)(2,1)S(1)} %get-tuple-element.37), channel_id=1, source_target_pairs={{0,14},{1,3},{2,4},{3,1},{4,2},{5,7},{6,8},{7,5},{8,6},{9,11},{10,... | collective-permute-start | bytes 491528 | tf_op jit(solution)/shard_map/ppermute | solution.py:30
  8.5 2.2 %stage.1 = (s32[32,128]{1,0:T(8,128)S(1)}, s32[40,128]{1,0:T(8,128)S(1)}, bf16[64,4096]{1,0:T(8,128)(2,1)S(1)}, f32[128,4096]{1,0:T(8,128)S(1)}, bf16[64,1792]{1...) custom-call(bf16[64,128]{1,0:T(8,128)(2,1)S(1)} %get-tuple-element.30.cols_r, ...), custom_call_target="tpu_custom_call" | custom-call | flops 1 | bytes 1 | tf_op jit(solution)/shard_map/stage/pallas_call | solution.py:131
  10.7 0.1 collective-permute-start.4
  10.8 1.9 %collective-permute-start.5 = (bf16[64,1792]{1,0:T(8,128)(2,1)S(1)}, bf16[64,1792]{1,0:T(8,128)(2,1)S(1)}, u32[]{:S(2)}, u32[]{:S(2)}) collective-permute-start(bf16[64,1792]{1,0:T(8,128)(2,1)S(1)} %get-tuple-element.41), channel_id=1, source_target_pairs={{0,14},{1,3},{2,4},{3,1},{4,2},{5,7},{6,8},{7,5},{8,6},{9,11},{10,... | collective-permute-start | bytes 688136 | tf_op jit(solution)/shard_map/ppermute | solution.py:30
  12.7 0.1 collective-permute-done.refs_5_.refs_7_
  12.8 0.3 collective-permute-done.1.refs_6_.refs_8_
  13.0 7.0 %collective-permute-start.2 = (bf16[64,1152]{1,0:T(8,128)(2,1)S(1)}, bf16[64,1152]{1,0:T(8,128)(2,1)S(1)}, u32[]{:S(2)}, u32[]{:S(2)}) collective-permute-start(bf16[64,1152]{1,0:T(8,128)(2,1)S(1)} %get-tuple-element.40), channel_id=1, source_target_pairs={{0,2},{1,15},{2,0},{3,5},{4,6},{5,3},{6,4},{7,9},{8,10},{9,7},{10,... | collective-permute-start | bytes 442376 | tf_op jit(solution)/shard_map/ppermute | solution.py:30
  20.1 3.6 %collective-permute-start.3 = (bf16[64,1152]{1,0:T(8,128)(2,1)S(1)}, bf16[64,1152]{1,0:T(8,128)(2,1)S(1)}, u32[]{:S(2)}, u32[]{:S(2)}) collective-permute-start(bf16[64,1152]{1,0:T(8,128)(2,1)S(1)} %get-tuple-element.40), channel_id=1, source_target_pairs={{0,14},{1,3},{2,4},{3,1},{4,2},{5,7},{6,8},{7,5},{8,6},{9,11},{10,... | collective-permute-start | bytes 442376 | tf_op jit(solution)/shard_map/ppermute | solution.py:30
  23.7 4.4 %chunk.3 = (f32[128,4096]{1,0:T(8,128)}, bf16[38,320,128]{2,1,0:T(8,128)(2,1)S(1)}, f32[3,2304,128]{2,1,0:T(8,128)S(1)}, f32[192,128]{1,0:T(8,128)S(1)}) custom-call(s32[40,1]{1,0:T(8,128)S(1)} %bitcast.13, s32[32,128]{1,0:T(8,128)S(1)} %get-tuple-element.32.refs_1_, ...), custom_call_target="tpu_custom_call", output_to_operand_aliasing={{2}: (9, {}), {3}: (10, {})} | custom-call | flops 1 | bytes 1 | tf_op jit(solution)/shard_map/chunk/pallas_call | solution.py:374
  28.1 0.0 collective-permute-done.4.refs_7_
  28.1 4.2 %chunk.4 = (f32[128,4096]{1,0:T(8,128)}, bf16[38,320,128]{2,1,0:T(8,128)(2,1)S(1)}, f32[3,2304,128]{2,1,0:T(8,128)S(1)}, f32[192,128]{1,0:T(8,128)S(1)}) custom-call(s32[40,1]{1,0:T(8,128)S(1)} %bitcast.14, s32[32,128]{1,0:T(8,128)S(1)} %get-tuple-element.32.refs_1_, ...), custom_call_target="tpu_custom_call", output_to_operand_aliasing={{0}: (9, {}), {1}: (10, {}), {2}: (11, {}), {3}: (12, {})} | custom-call | flops 1 | bytes 1 | tf_op jit(solution)/shard_map/chunk/pallas_call | solution.py:374
  32.4 6.7 %chunk.5 = (f32[128,4096]{1,0:T(8,128)}, bf16[38,320,128]{2,1,0:T(8,128)(2,1)S(1)}, f32[3,2304,128]{2,1,0:T(8,128)S(1)}, f32[192,128]{1,0:T(8,128)S(1)}, f32[64,128]{1,0:T(8,128)S(1)}, /*index=5*/f32[64,128]{1,0:T(8,128)S(1)}) custom-call(s32[40,1]{1,0:T(8,128)S(1)} %bitcast.15, ...), custom_call_target="tpu_custom_call", output_to_operand_aliasing={{0}: (9, {}), {1}: (10, {}), {2}: (11, {}), {3}: (12, {})} | custom-call | flops 1 | bytes 1 | tf_op jit(solution)/shard_map/chunk/pallas_call | solution.py:374
  39.1 1.5 %collective-permute-start.7 = (f32[64,128]{1,0:T(8,128)S(1)}, f32[64,128]{1,0:T(8,128)S(1)}, u32[]{:S(2)}, u32[]{:S(2)}) collective-permute-start(f32[64,128]{1,0:T(8,128)S(1)} %get-tuple-element.57), channel_id=1, source_target_pairs={{0,14},{1,3},{2,4},{3,1},{4,2},{5,7},{6,8},{7,5},{8,6},{9,11},{10,... | collective-permute-start | bytes 98312 | tf_op jit(solution)/shard_map/ppermute | solution.py:30
  40.5 0.2 collective-permute-start.6
  40.8 4.1 %finish.1.refs_0_ = f32[64,128]{1,0:T(8,128)S(1)} custom-call(s32[40,1]{1,0:T(8,128)S(1)} %bitcast.16, bf16[64,128]{1,0:T(8,128)(2,1)S(1)} %get-tuple-element.30.cols_ref.refs_4_, bf16[38,320,128]{2,1,0:T(8,128)(2,1)S(1)} %get-tuple-element.53.packed, f32[192,128]{1,0:T(8,128)S(1)} %get-tuple-element.54.projected, f32[3,2304,128]{2,1,0:T(8,128)S(1)} %get-tuple-element.55.earlier), custom_call_target="tpu_custom_call" | custom-call | flops 1 | bytes 1 | tf_op jit(solution)/shard_map/finish/pallas_call | solution.py:240
  44.8 3.0 %collective-permute-start.8 = (f32[64,128]{1,0:T(8,128)S(1)}, f32[64,128]{1,0:T(8,128)S(1)}, u32[]{:S(2)}, u32[]{:S(2)}) collective-permute-start(f32[64,128]{1,0:T(8,128)S(1)} %finish.1.refs_0_), channel_id=1, source_target_pairs={{0,1},{1,0},{2,3},{3,2},{4,5},{5,4},{6,7},{7,6},{8,9},{9,8},{10,11... | collective-permute-start | bytes 98312 | tf_op jit(solution)/shard_map/ppermute | solution.py:459
  47.9 0.1 collective-permute-start.10
  48.0 0.4 collective-permute-start.9
  48.4 0.3 collective-permute-done.8.refs_3_
  48.7 0.4 collective-permute-done.10.refs_5_
  49.1 0.2 collective-permute-done.9.refs_4_
  49.3 3.1 %solve.1 = f32[1,64]{1,0:T(1,128)} custom-call(f32[64,128]{1,0:T(8,128)S(1)} %finish.1.refs_0_, f32[64,128]{1,0:T(8,128)S(1)} %collective-permute-done.6.refs_1_, f32[64,128]{1,0:T(8,128)S(1)} %collective-permute-done.7.refs_2_, f32[64,128]{1,0:T(8,128)S(1)} %collective-permute-done.8.refs_3_, f32[64,128]{1,0:T(8,128)S(1)} %collective-permute-done.9.refs_4_, ...), custom_call_target="tpu_custom_call" | custom-call | flops 1 | bytes 1 | tf_op jit(solution)/shard_map/solve/pallas_call | solution.py:448
  (7 shorter events, 0.0 us)
Async XLA Ops:
  1.9 10.9 %collective-permute-start = (bf16[64,1280]{1,0:T(8,128)(2,1)S(1)}, bf16[64,1280]{1,0:T(8,128)(2,1)S(1)}, u32[]{:S(2)}, u32[]{:S(2)}) collective-permute-start(bf16[64,1280]{1,0:T(8,128)(2,1)S(1)} %get-tuple-element.36), channel_id=1, source_target_pairs={{0,2},{1,15},{2,0},{3,5},{4,6},{5,3},{6,4},{7,9},{8,10},{9,7},{10,... | collective-permute-start | bytes 491528 | tf_op jit(solution)/shard_map/ppermute | solution.py:30
  4.9 8.1 %collective-permute-start.1 = (bf16[64,1280]{1,0:T(8,128)(2,1)S(1)}, bf16[64,1280]{1,0:T(8,128)(2,1)S(1)}, u32[]{:S(2)}, u32[]{:S(2)}) collective-permute-start(bf16[64,1280]{1,0:T(8,128)(2,1)S(1)} %get-tuple-element.37), channel_id=1, source_target_pairs={{0,14},{1,3},{2,4},{3,1},{4,2},{5,7},{6,8},{7,5},{8,6},{9,11},{10,... | collective-permute-start | bytes 491528 | tf_op jit(solution)/shard_map/ppermute | solution.py:30
  10.7 17.4 %collective-permute-start.4 = (bf16[64,1792]{1,0:T(8,128)(2,1)S(1)}, bf16[64,1792]{1,0:T(8,128)(2,1)S(1)}, u32[]{:S(2)}, u32[]{:S(2)}) collective-permute-start(bf16[64,1792]{1,0:T(8,128)(2,1)S(1)} %get-tuple-element.41), channel_id=1, source_target_pairs={{0,2},{1,15},{2,0},{3,5},{4,6},{5,3},{6,4},{7,9},{8,10},{9,7},{10,... | collective-permute-start | bytes 688136 | tf_op jit(solution)/shard_map/ppermute | solution.py:30
  10.8 17.3 %collective-permute-start.5 = (bf16[64,1792]{1,0:T(8,128)(2,1)S(1)}, bf16[64,1792]{1,0:T(8,128)(2,1)S(1)}, u32[]{:S(2)}, u32[]{:S(2)}) collective-permute-start(bf16[64,1792]{1,0:T(8,128)(2,1)S(1)} %get-tuple-element.41), channel_id=1, source_target_pairs={{0,14},{1,3},{2,4},{3,1},{4,2},{5,7},{6,8},{7,5},{8,6},{9,11},{10,... | collective-permute-start | bytes 688136 | tf_op jit(solution)/shard_map/ppermute | solution.py:30
  13.0 19.3 %collective-permute-start.2 = (bf16[64,1152]{1,0:T(8,128)(2,1)S(1)}, bf16[64,1152]{1,0:T(8,128)(2,1)S(1)}, u32[]{:S(2)}, u32[]{:S(2)}) collective-permute-start(bf16[64,1152]{1,0:T(8,128)(2,1)S(1)} %get-tuple-element.40), channel_id=1, source_target_pairs={{0,2},{1,15},{2,0},{3,5},{4,6},{5,3},{6,4},{7,9},{8,10},{9,7},{10,... | collective-permute-start | bytes 442376 | tf_op jit(solution)/shard_map/ppermute | solution.py:30
  20.1 12.3 %collective-permute-start.3 = (bf16[64,1152]{1,0:T(8,128)(2,1)S(1)}, bf16[64,1152]{1,0:T(8,128)(2,1)S(1)}, u32[]{:S(2)}, u32[]{:S(2)}) collective-permute-start(bf16[64,1152]{1,0:T(8,128)(2,1)S(1)} %get-tuple-element.40), channel_id=1, source_target_pairs={{0,14},{1,3},{2,4},{3,1},{4,2},{5,7},{6,8},{7,5},{8,6},{9,11},{10,... | collective-permute-start | bytes 442376 | tf_op jit(solution)/shard_map/ppermute | solution.py:30
  39.1 8.8 %collective-permute-start.7 = (f32[64,128]{1,0:T(8,128)S(1)}, f32[64,128]{1,0:T(8,128)S(1)}, u32[]{:S(2)}, u32[]{:S(2)}) collective-permute-start(f32[64,128]{1,0:T(8,128)S(1)} %get-tuple-element.57), channel_id=1, source_target_pairs={{0,14},{1,3},{2,4},{3,1},{4,2},{5,7},{6,8},{7,5},{8,6},{9,11},{10,... | collective-permute-start | bytes 98312 | tf_op jit(solution)/shard_map/ppermute | solution.py:30
  40.5 7.4 %collective-permute-start.6 = (f32[64,128]{1,0:T(8,128)S(1)}, f32[64,128]{1,0:T(8,128)S(1)}, u32[]{:S(2)}, u32[]{:S(2)}) collective-permute-start(f32[64,128]{1,0:T(8,128)S(1)} %get-tuple-element.56), channel_id=1, source_target_pairs={{0,2},{1,15},{2,0},{3,5},{4,6},{5,3},{6,4},{7,9},{8,10},{9,7},{10,... | collective-permute-start | bytes 98312 | tf_op jit(solution)/shard_map/ppermute | solution.py:30
  40.8 8.5 %copy-start = (f32[64]{0:T(128)S(1)}, f32[64]{0:T(128)}, u32[]{:S(2)}) copy-start(f32[64]{0:T(128)} %param.15) | copy-start | bytes 772
  44.8 3.9 %collective-permute-start.8 = (f32[64,128]{1,0:T(8,128)S(1)}, f32[64,128]{1,0:T(8,128)S(1)}, u32[]{:S(2)}, u32[]{:S(2)}) collective-permute-start(f32[64,128]{1,0:T(8,128)S(1)} %finish.1.refs_0_), channel_id=1, source_target_pairs={{0,1},{1,0},{2,3},{3,2},{4,5},{5,4},{6,7},{7,6},{8,9},{9,8},{10,11... | collective-permute-start | bytes 98312 | tf_op jit(solution)/shard_map/ppermute | solution.py:459
  47.9 1.2 %collective-permute-start.10 = (f32[64,128]{1,0:T(8,128)S(1)}, f32[64,128]{1,0:T(8,128)S(1)}, u32[]{:S(2)}, u32[]{:S(2)}) collective-permute-start(f32[64,128]{1,0:T(8,128)S(1)} %collective-permute-done.7.refs_2_), channel_id=1, source_target_pairs={{0,1},{1,0},{2,3},{3,2},{4,5},{5,4},{6,7},{7,6},{8,9},{9,8},{10,11... | collective-permute-start | bytes 98312 | tf_op jit(solution)/shard_map/ppermute | solution.py:459
  48.0 1.3 %collective-permute-start.9 = (f32[64,128]{1,0:T(8,128)S(1)}, f32[64,128]{1,0:T(8,128)S(1)}, u32[]{:S(2)}, u32[]{:S(2)}) collective-permute-start(f32[64,128]{1,0:T(8,128)S(1)} %collective-permute-done.6.refs_1_), channel_id=1, source_target_pairs={{0,1},{1,0},{2,3},{3,2},{4,5},{5,4},{6,7},{7,6},{8,9},{9,8},{10,11... | collective-permute-start | bytes 98312 | tf_op jit(solution)/shard_map/ppermute | solution.py:459
